TPU v7x, 128 devices: a whole 4x4x4 slice. The times are simulated.
128 devices in a mesh: req: 32 (over x, z, core), mlp: 4 (over y).
Axes of the slice: x: 4, y: 4, z: 4, core: 2. Of those that a mesh axis runs over, the one named last changes fastest.
Arguments:
- tokens: bfloat16 [4096, 3584], P('req'), may hold values from -40 to 40
- segment_ids: int32 [32, 128], P('req'), may hold values from 0 to 3, never falling along the last dimension, each value on 1 to 64 neighbouring positions
- past_len: int32 [32, 4], P('req'), may hold values from 0 to 2047
- page_table: int32 [32, 64], P('req'), may hold values from 0 to 63, each once within a row
- migrate_pages: int32 [32, 32, 1], P('req'), may hold values from 0 to 31
- pooled_key_cache: bfloat16 [1024, 64, 1024], P('req', None, 'mlp'), may hold values from -6 to 6
- pooled_value_cache: bfloat16 [1024, 64, 1024], P('req', None, 'mlp'), may hold values from -6 to 6
- attn_gain: float32 [3584], replicated, may hold values from 0.25 to 1.75
- w_query: bfloat16 [3584, 2048], P(None, 'mlp'), may hold values from -0.09375 to 0.09375
- key_matrix: bfloat16 [3584, 1024], P(None, 'mlp'), may hold values from -0.09375 to 0.09375
- value_matrix: bfloat16 [3584, 1024], P(None, 'mlp'), may hold values from -0.09375 to 0.09375
- w_out: bfloat16 [2048, 3584], P('mlp'), may hold values from -1 to 1
- post_attn_gain: float32 [3584], replicated, may hold values from 0.25 to 1.75
- ffw_gain: float32 [3584], replicated, may hold values from 0.25 to 1.75
- w_gate: bfloat16 [3584, 14336], P(None, 'req'), may hold values from -0.09375 to 0.09375
- w_up: bfloat16 [3584, 14336], P(None, 'req'), may hold values from -0.09375 to 0.09375
- w_down: bfloat16 [14336, 3584], P('req'), may hold values from -1 to 1
- post_ffw_gain: float32 [3584], replicated, may hold values from 0.25 to 1.75
Outputs:
- mixed: bfloat16 [4096, 3584], P(('req', 'mlp'))
- written_key_rows: bfloat16 [4096, 1024], P('req', 'mlp')
- written_value_rows: bfloat16 [4096, 1024], P('req', 'mlp')
Inputs may be any that keep to these rules, and one draw needn't show every extreme that they name: `segment_ids`: in each row the requests 0 to 3 appear in order; each request has 1 to 64 new tokens, and some request exactly 64. `page_table`: each row is a permutation; every page of the owner's list (own pool and received pages) lies in exactly one request's window. `migrate_pages`: entry [s, d, m] names a page of owner s's pool.
All inputs are finite; a program needn't handle non-finite values.
Results may differ from a plain program's by a relative error of at most 0.015.
Values may be sent and summed in bfloat16 or wider, within the bound.
No kernel may reach another device: no remote copies, remote signals or barrier semaphores. Data moves between devices by JAX's collectives and lax.ppermute only.
A program may use at most 128 MiB of HBM per device.

v0:
```python
import jax
import jax.numpy as jnp
from jax import lax
from jax.sharding import PartitionSpec as P

HEAD_SIZE = 256
WINDOW_LENGTH = 1024


SOFT_CAP = 50.0
NORM_EPS = 1e-06
ROPE_BASE = 10000.0


def rms_scale(values, gain):
    return values * lax.rsqrt(jnp.mean(values * values, axis=-1, keepdims=True) + NORM_EPS) * gain


def apply_rotary(vectors, token_positions):
    width = vectors.shape[-1]
    half = width // 2
    frequency = ROPE_BASE ** (-jnp.arange(half, dtype=jnp.float32) * (2.0 / width))
    angles = token_positions.astype(jnp.float32)[:, None] * frequency[None, :]
    cosine = jnp.cos(angles)[:, None, :]
    sine = jnp.sin(angles)[:, None, :]
    first = vectors[..., :half]
    second = vectors[..., half:]
    return jnp.concatenate(
        [first * cosine - second * sine, second * cosine + first * sine], axis=-1
    )


def token_layout(segment, past):
    requests = jnp.arange(past.shape[0], dtype=jnp.int32)
    member = segment[:, None] == requests[None, :]
    firsts = jnp.sum((segment[:, None] < requests[None, :]).astype(jnp.int32), axis=0)
    offsets = jnp.arange(segment.shape[0], dtype=jnp.int32) - jnp.sum(
        jnp.where(member, firsts[None, :], 0), axis=1
    )
    token_positions = jnp.sum(jnp.where(member, past[None, :], 0), axis=1) + offsets
    return (offsets, token_positions)


def visibility(segment, offsets, past, window):
    count_req = past.shape[0]
    requests = jnp.arange(count_req, dtype=jnp.int32)
    slots = jnp.arange(count_req * window, dtype=jnp.int32)
    slot_req = slots // window
    slot_pos = slots % window
    slot_past = jnp.sum(jnp.where(slot_req[:, None] == requests[None, :], past[None, :], 0), axis=1)
    cached = (
        (segment[:, None] == slot_req[None, :])
        & (slot_pos[None, :] > offsets[:, None])
        & (slot_pos[None, :] >= window - slot_past[None, :])
    )
    order = jnp.arange(segment.shape[0], dtype=jnp.int32)
    fresh = (segment[:, None] == segment[None, :]) & (order[None, :] <= order[:, None])
    return (cached, fresh)


def local(
    tokens,
    segment_ids,
    past_len,
    page_table,
    migrate_pages,
    pooled_key_cache,
    pooled_value_cache,
    attn_gain,
    w_query,
    key_matrix,
    value_matrix,
    w_out,
    post_attn_gain,
    ffw_gain,
    w_gate,
    w_up,
    w_down,
    post_ffw_gain,
):
    tok_count = tokens.shape[0]
    key_heads = key_matrix.shape[1] // HEAD_SIZE
    query_heads = w_query.shape[1] // HEAD_SIZE
    query_group = query_heads // key_heads
    scale = float(HEAD_SIZE) ** (-0.5)
    page_len = pooled_key_cache.shape[1]
    columns = pooled_key_cache.shape[2]
    send_list = migrate_pages[0]
    owners = send_list.shape[0]
    flat_list = send_list.reshape(-1)
    send_keys = jnp.take(pooled_key_cache, flat_list, axis=0).reshape(
        owners, send_list.shape[1], page_len, columns
    )
    send_values = jnp.take(pooled_value_cache, flat_list, axis=0).reshape(
        owners, send_list.shape[1], page_len, columns
    )
    recv_keys, recv_values = (
        lax.all_to_all(send_keys, "req", split_axis=0, concat_axis=0, tiled=True),
        lax.all_to_all(send_values, "req", split_axis=0, concat_axis=0, tiled=True),
    )
    page_lookup = page_table[0]
    listed_keys = jnp.concatenate(
        [pooled_key_cache, recv_keys.reshape(-1, page_len, columns)], axis=0
    )
    listed_values = jnp.concatenate(
        [pooled_value_cache, recv_values.reshape(-1, page_len, columns)], axis=0
    )
    window_keys = jnp.take(listed_keys, page_lookup, axis=0).reshape(-1, key_heads, HEAD_SIZE)
    window_values = jnp.take(listed_values, page_lookup, axis=0).reshape(-1, key_heads, HEAD_SIZE)
    segment = segment_ids[0]
    past = past_len[0]
    offsets, token_positions = token_layout(segment, past)
    normalized_input = rms_scale(tokens.astype(jnp.float32), attn_gain).astype(jnp.bfloat16)
    query_rows = apply_rotary(
        jnp.dot(normalized_input, w_query, preferred_element_type=jnp.float32).reshape(
            tok_count, query_heads, HEAD_SIZE
        ),
        token_positions,
    ).astype(jnp.bfloat16)
    incoming_keys = apply_rotary(
        jnp.dot(normalized_input, key_matrix, preferred_element_type=jnp.float32).reshape(
            tok_count, key_heads, HEAD_SIZE
        ),
        token_positions,
    ).astype(jnp.bfloat16)
    incoming_values = jnp.dot(
        normalized_input, value_matrix, preferred_element_type=jnp.float32
    ).astype(jnp.bfloat16)
    grouped_queries = query_rows.reshape(tok_count, key_heads, query_group, HEAD_SIZE)
    value_heads = incoming_values.reshape(tok_count, key_heads, HEAD_SIZE)
    score_cached = jnp.einsum(
        "tkgd,skd->tkgs", grouped_queries, window_keys, preferred_element_type=jnp.float32
    )
    score_fresh = jnp.einsum(
        "tkgd,skd->tkgs", grouped_queries, incoming_keys, preferred_element_type=jnp.float32
    )
    cached, fresh = visibility(segment, offsets, past, WINDOW_LENGTH)
    weight_cached = jnp.where(
        cached[:, None, None, :],
        jnp.exp(SOFT_CAP * jnp.tanh(score_cached * (scale / SOFT_CAP))),
        0.0,
    )
    weight_fresh = jnp.where(
        fresh[:, None, None, :], jnp.exp(SOFT_CAP * jnp.tanh(score_fresh * (scale / SOFT_CAP))), 0.0
    )
    totals = jnp.sum(weight_cached, axis=-1, keepdims=True) + jnp.sum(
        weight_fresh, axis=-1, keepdims=True
    )
    prob_cached = (weight_cached / totals).astype(jnp.bfloat16)
    prob_fresh = (weight_fresh / totals).astype(jnp.bfloat16)
    attended = jnp.einsum(
        "tkgs,skd->tkgd", prob_cached, window_values, preferred_element_type=jnp.float32
    )
    attended = attended + jnp.einsum(
        "tkgs,skd->tkgd", prob_fresh, value_heads, preferred_element_type=jnp.float32
    )
    attention = attended.astype(jnp.bfloat16).reshape(tok_count, query_heads * HEAD_SIZE)
    rows_mine = tok_count // lax.axis_size("mlp")
    attn_out = lax.psum_scatter(
        jnp.dot(attention, w_out, preferred_element_type=jnp.float32).astype(jnp.bfloat16),
        "mlp",
        scatter_dimension=0,
        tiled=True,
    ).astype(jnp.float32)
    own_rows = lax.dynamic_slice_in_dim(
        tokens, lax.axis_index("mlp") * rows_mine, rows_mine, 0
    ).astype(jnp.float32)
    residual_stream = own_rows + rms_scale(attn_out, post_attn_gain)
    feedforward_input = rms_scale(residual_stream, ffw_gain).astype(jnp.bfloat16)
    piece = lax.all_gather(feedforward_input, "req", axis=0, tiled=True)
    gate_part = jnp.dot(piece, w_gate, preferred_element_type=jnp.float32)
    up_part = jnp.dot(piece, w_up, preferred_element_type=jnp.float32)
    hidden = (jax.nn.gelu(gate_part, approximate=True) * up_part).astype(jnp.bfloat16)
    ffw_out = lax.psum_scatter(
        jnp.dot(hidden, w_down, preferred_element_type=jnp.float32).astype(jnp.bfloat16),
        "req",
        scatter_dimension=0,
        tiled=True,
    ).astype(jnp.float32)
    mixed = (residual_stream + rms_scale(ffw_out, post_ffw_gain)).astype(jnp.bfloat16)
    return (mixed, incoming_keys.reshape(tok_count, key_heads * HEAD_SIZE), incoming_values)


def solution(mesh):
    return jax.shard_map(
        local,
        mesh=mesh,
        in_specs=(
            P("req", None),
            P("req", None),
            P("req", None),
            P("req", None),
            P("req", None, None),
            P("req", None, "mlp"),
            P("req", None, "mlp"),
            P(),
            P(None, "mlp"),
            P(None, "mlp"),
            P(None, "mlp"),
            P("mlp", None),
            P(),
            P(),
            P(None, "req"),
            P(None, "req"),
            P("req", None),
            P(),
        ),
        out_specs=(P(("req", "mlp"), None), P("req", "mlp"), P("req", "mlp")),
        check_vma=False,
    )
```

profile of v0, /device:TPU:16, one launch (start us, length us, event | category | flops | bytes accessed | tf_op | source)
XLA Modules:
  0.0 281.9 jit_solution(7771821692837029242)
XLA Ops:
  8.8 2.8 gather_fusion.2
  11.6 2.9 %gather_fusion = bf16[32,64,256]{2,1,0:T(8,128)(2,1)} fusion(bf16[32,64,256]{2,1,0:T(8,128)(2,1)} %param.28, s32[1024]{0:T(1024)S(1)} %pad_clamp_fusion.1), kind=kCustom, calls=%fused_computation.clone | custom fusion | bytes 2097280 | tf_op jit(solution)/shard_map/jit(_take)/gather | solution.py:94
  14.5 3.1 %select_bitcast_fusion = (bf16[32,1,64,256]{3,2,1,0:T(8,128)(2,1)}, bf16[32,1,64,256]{3,2,1,0:T(8,128)(2,1)}) fusion(bf16[32,64,256]{2,1,0:T(8,128)(2,1)} %gather_fusion.2, pred[32]{0:T(512)(128)(4,1)S(1)} %compare_and_fusion.1, bf16[32,64,256]{2,1,0:T(8,128)(2,1)} %gather_fusion), kind=kLoop, calls=%fused_computation.45 | loop fusion | flops 1048576 | bytes 4194336 | tf_op jit(solution)/shard_map/reshape | solution.py:91
  17.6 8.4 %all-to-all-start = ((bf16[32,1,64,256]{3,2,1,0:T(8,128)(2,1)}), bf16[32,1,64,256]{3,2,1,0:T(8,128)(2,1)}, u32[]{:S(2)}, u32[]{:S(2)}) async-start(bf16[32,1,64,256]{3,2,1,0:T(8,128)(2,1)} %get-tuple-element.20), calls=%async_computation | async-start | bytes 2097152 | tf_op jit(solution)/shard_map/all_to_all | solution.py:99
  27.3 1.7 fusion.7
  31.3 0.9 multiply_cosine_fusion.1
  32.2 2.2 convolution_bitcast_fusion
  34.8 1.4 fusion.57
  37.4 1.1 reshape.421
  39.5 1.7 fusion.61
  41.3 2.3 convolution_convert_fusion.2
  43.6 7.4 %all-to-all-start.1 = ((bf16[32,1,64,256]{3,2,1,0:T(8,128)(2,1)}), bf16[32,1,64,256]{3,2,1,0:T(8,128)(2,1)}, u32[]{:S(2)}, u32[]{:S(2)}) async-start(bf16[32,1,64,256]{3,2,1,0:T(8,128)(2,1)} %get-tuple-element.19), calls=%async_computation.1 | async-start | bytes 2097152 | tf_op jit(solution)/shard_map/all_to_all | solution.py:98
  51.1 4.6 %and_and_fusion = pred[128,4096]{0,1:T(8,128)(4,1)} fusion(s32[128]{0:T(128)S(1)} %copy-done.13, s32[128]{0:T(128)S(1)} %bitcast.86, s32[4096]{0:T(1024)S(1)} %copy-done.6, s32[4096]{0:T(1024)S(1)} %get-tuple-element.26, pred[4096]{0:T(1024)(128)(4,1)S(1)} %copy-done.8), kind=kLoop, calls=%fused_computation.22 | loop fusion | flops 2097152 | bytes 562176 | tf_op jit(solution)/shard_map/and | solution.py:52
  55.8 3.0 %pad_maximum_fusion = bf16[64,64,256]{2,1,0:T(8,128)(2,1)} fusion(bf16[32,64,256]{2,1,0:T(8,128)(2,1)} %bitcast.3, bf16[32,64,256]{2,1,0:T(8,128)(2,1)} %param.28), kind=kLoop, calls=%fused_computation.16 | loop fusion | flops 1048576 | bytes 4194304 | tf_op jit(solution)/shard_map/concatenate | solution.py:105
  58.8 9.0 %all-to-all-done.1 = bf16[32,1,64,256]{3,2,1,0:T(8,128)(2,1)} async-done(((bf16[32,1,64,256]{3,2,1,0:T(8,128)(2,1)}), bf16[32,1,64,256]{3,2,1,0:T(8,128)(2,1)}, u32[]{:S(2)}, u32[]{:S(2)}) %all-to-all-start.1) | async-done | bytes 1048608 | tf_op jit(solution)/shard_map/all_to_all | solution.py:98
  67.8 3.1 %pad_maximum_fusion.1 = bf16[64,64,256]{2,1,0:T(8,128)(2,1)} fusion(bf16[32,64,256]{2,1,0:T(8,128)(2,1)} %bitcast.9, bf16[32,64,256]{2,1,0:T(8,128)(2,1)} %param.27), kind=kLoop, calls=%fused_computation.17 | loop fusion | flops 1048576 | bytes 4194304 | tf_op jit(solution)/shard_map/concatenate | solution.py:102
  70.9 3.7 %gather_fusion.1 = bf16[64,64,256]{2,1,0:T(8,128)(2,1)} fusion(bf16[64,64,256]{2,1,0:T(8,128)(2,1)} %pad_maximum_fusion, s32[1024]{0:T(1024)} %pad_clamp_fusion), kind=kCustom, calls=%fused_computation.1.clone | custom fusion | bytes 4194560 | tf_op jit(solution)/shard_map/jit(_take)/gather | solution.py:109
  74.6 3.7 %gather_fusion.3 = bf16[64,64,256]{2,1,0:T(8,128)(2,1)} fusion(bf16[64,64,256]{2,1,0:T(8,128)(2,1)} %pad_maximum_fusion.1, s32[1024]{0:T(1024)} %pad_clamp_fusion), kind=kCustom, calls=%fused_computation.3.clone | custom fusion | bytes 4194560 | tf_op jit(solution)/shard_map/jit(_take)/gather | solution.py:108
  78.3 2.7 broadcast_select_fusion
  81.1 1.4 fusion.60
  83.5 1.0 copy-done.1
  84.5 1.6 convolution_convert_fusion.1
  86.2 19.7 %reduce-scatter.3.cloned.1.call-done = bf16[32,3584]{1,0:T(8,128)(2,1)} async-done(((bf16[128,3584]{1,0:T(8,128)(2,1)}), bf16[32,3584]{1,0:T(8,128)(2,1)}) %reduce-scatter.3.cloned.1.call-update) | async-done | bytes 229392 | tf_op jit(solution)/shard_map/reduce_scatter | solution.py:159
  105.9 1.1 fusion.25
  107.0 1.3 multiply_reduce_fusion
  108.4 1.9 multiply_convert_fusion
  110.5 52.1 %all-gather.2.cloned.1.call-done = bf16[1024,3584]{1,0:T(8,128)(2,1)} async-done(((bf16[32,3584]{1,0:T(8,128)(2,1)}), bf16[1024,3584]{1,0:T(8,128)(2,1)}) %all-gather.2.cloned.1.call-update) | async-done | bytes 7340048 | tf_op jit(solution)/shard_map/all_gather | solution.py:170
  162.7 8.7 %fusion.62 = f32[1024,448]{0,1:T(8,128)} fusion(bf16[1024,3584]{1,0:T(8,128)(2,1)} %all-gather.2.cloned.1.call-done, bf16[3584,448]{0,1:T(8,128)(2,1)} %param.36), kind=kOutput, calls=%fused_computation.122 | convolution fusion | flops 3288334336 | bytes 12386304 | tf_op jit(solution)/shard_map/dot_general | solution.py:171
  171.4 13.0 %convolution_convert_fusion = bf16[1024,3584]{1,0:T(8,128)(2,1)} fusion(bf16[448,3584]{1,0:T(8,128)(2,1)S(1)} %copy-done, f32[1024,448]{0,1:T(8,128)} %fusion.62, bf16[1024,3584]{1,0:T(8,128)(2,1)} %all-gather.2.cloned.1.call-done, bf16[3584,448]{0,1:T(8,128)(2,1)} %param.37), kind=kOutput, calls=%fused_computation.4 | convolution fusion | flops 6584926208 | bytes 22937600 | tf_op jit(solution)/shard_map/dot_general | solution.py:175
  184.5 87.8 %reduce-scatter.5.cloned.1.call-done = bf16[32,3584]{1,0:T(8,128)(2,1)} async-done(((bf16[1024,3584]{1,0:T(8,128)(2,1)}), bf16[32,3584]{1,0:T(8,128)(2,1)}) %reduce-scatter.5.cloned.1.call-update) | async-done | bytes 229392 | tf_op jit(solution)/shard_map/reduce_scatter | solution.py:174
  272.3 1.1 fusion.28
  273.4 2.0 fusion.31
  (73 shorter events, 9.1 us)
Async XLA Ops:
  7.2 164.3 %copy-start = (bf16[448,3584]{1,0:T(8,128)(2,1)S(1)}, bf16[448,3584]{1,0:T(8,128)(2,1)}, u32[]{:S(2)}) copy-start(bf16[448,3584]{1,0:T(8,128)(2,1)} %param.38) | copy-start | bytes 9633796
  17.6 8.5 %copy-start.17 = (s32[1,64]{1,0:T(1,128)S(1)}, s32[1,64]{1,0:T(1,128)}, u32[]{:S(2)}) copy-start(s32[1,64]{1,0:T(1,128)} %param.25) | copy-start | bytes 772
  17.6 11.4 %copy-start.10 = (s32[1,128]{1,0:T(1,128)S(1)}, s32[1,128]{1,0:T(1,128)}, u32[]{:S(2)}) copy-start(s32[1,128]{1,0:T(1,128)} %param.23) | copy-start | bytes 1540
  17.6 12.1 %copy-start.12 = (s32[1,4]{1,0:T(1,128)S(1)}, s32[1,4]{1,0:T(1,128)}, u32[]{:S(2)}) copy-start(s32[1,4]{1,0:T(1,128)} %param.24) | copy-start | bytes 52
  17.6 14.6 %copy-start.16 = (f32[3584]{0:T(1024)S(1)}, f32[3584]{0:T(1024)}, u32[]{:S(2)}) copy-start(f32[3584]{0:T(1024)} %param.29) | copy-start | bytes 43012
  17.6 26.0 %all-to-all-start = ((bf16[32,1,64,256]{3,2,1,0:T(8,128)(2,1)}), bf16[32,1,64,256]{3,2,1,0:T(8,128)(2,1)}, u32[]{:S(2)}, u32[]{:S(2)}) async-start(bf16[32,1,64,256]{3,2,1,0:T(8,128)(2,1)} %get-tuple-element.20), calls=%async_computation | async-start | bytes 2097152 | tf_op jit(solution)/shard_map/all_to_all | solution.py:99
  26.7 8.1 %copy-start.15 = (bf16[3584,512]{1,0:T(8,128)(2,1)S(1)}, bf16[3584,512]{1,0:T(8,128)(2,1)}, u32[]{:S(2)}) copy-start(bf16[3584,512]{1,0:T(8,128)(2,1)} %param.30) | copy-start | bytes 11010052
  27.3 7.5 %copy-start.3 = (bf16[128,3584]{1,0:T(8,128)(2,1)S(1)}, bf16[128,3584]{1,0:T(8,128)(2,1)}, u32[]{:S(2)}) copy-start(bf16[128,3584]{1,0:T(8,128)(2,1)} %param.22) | copy-start | bytes 2752516
  29.0 7.2 %copy-start.20 = (f32[128]{0:T(128)}, f32[128]{0:T(128)S(1)}, u32[]{:S(2)}) copy-start(f32[128]{0:T(128)S(1)} %add_rsqrt_fusion.3) | copy-start | bytes 1540
  41.3 9.8 %copy-start.6 = (s32[4096]{0:T(1024)S(1)}, s32[4096]{0:T(1024)}, u32[]{:S(2)}) copy-start(s32[4096]{0:T(1024)} %get-tuple-element.25) | copy-start | bytes 49156
  41.3 9.8 %copy-start.8 = (pred[4096]{0:T(1024)(128)(4,1)S(1)}, pred[4096]{0:T(1024)(128)(4,1)}, u32[]{:S(2)}) copy-start(pred[4096]{0:T(1024)(128)(4,1)} %subtract_compare_fusion) | copy-start | bytes 12292
  41.3 9.8 %copy-start.11 = (s32[1,128]{1,0:T(1,128)S(1)}, s32[1,128]{1,0:T(1,128)}, u32[]{:S(2)}) copy-start(s32[1,128]{1,0:T(1,128)} %param.23) | copy-start | bytes 1540
  41.3 9.8 %copy-start.13 = (s32[128]{0:T(128)S(1)}, s32[128]{0:T(128)}, u32[]{:S(2)}) copy-start(s32[128]{0:T(128)} %get-tuple-element.16) | copy-start | bytes 1540
  43.6 39.7 %copy-start.18 = (bf16[128,256]{1,0:T(8,128)(2,1)}, bf16[128,256]{1,0:T(8,128)(2,1)S(1)}, u32[]{:S(2)}) copy-start(bf16[128,256]{1,0:T(8,128)(2,1)S(1)} %convolution_convert_fusion.2) | copy-start | bytes 196612
  43.6 24.2 %all-to-all-start.1 = ((bf16[32,1,64,256]{3,2,1,0:T(8,128)(2,1)}), bf16[32,1,64,256]{3,2,1,0:T(8,128)(2,1)}, u32[]{:S(2)}, u32[]{:S(2)}) async-start(bf16[32,1,64,256]{3,2,1,0:T(8,128)(2,1)} %get-tuple-element.19), calls=%async_computation.1 | async-start | bytes 2097152 | tf_op jit(solution)/shard_map/all_to_all | solution.py:98
  51.0 54.9 %reduce-scatter.3.cloned.1.call-start = ((), (), s32[]{:S(2)}) async-start(), calls=%async_computation.4 | async-start | bytes 1146880 | tf_op jit(solution)/shard_map/reduce_scatter | solution.py:159
  74.6 3.7 %copy-start.14 = (pred[64]{0:T(512)(128)(4,1)S(1)}, pred[64]{0:T(512)(128)(4,1)}, u32[]{:S(2)}) copy-start(pred[64]{0:T(512)(128)(4,1)} %compare_and_fusion) | copy-start | bytes 196
  78.3 2.7 copy-start.4
  82.4 0.9 copy-start.19
  82.4 2.1 copy-start.1
  84.5 22.5 %copy-start.5 = (f32[3584]{0:T(1024)S(1)}, f32[3584]{0:T(1024)}, u32[]{:S(2)}) copy-start(f32[3584]{0:T(1024)} %param.34) | copy-start | bytes 43012
  84.5 23.8 %copy-start.9 = (f32[3584]{0:T(1024)S(1)}, f32[3584]{0:T(1024)}, u32[]{:S(2)}) copy-start(f32[3584]{0:T(1024)} %param.35) | copy-start | bytes 43012
  86.2 76.5 %all-gather.2.cloned.1.call-start = ((), (), s32[]{:S(2)}) async-start(), calls=%async_computation.5 | async-start | bytes 7569408 | tf_op jit(solution)/shard_map/all_gather | solution.py:170
  110.3 162.0 %reduce-scatter.5.cloned.1.call-start = ((), (), s32[]{:S(2)}) async-start(), calls=%async_computation.6 | async-start | bytes 7569408 | tf_op jit(solution)/shard_map/reduce_scatter | solution.py:174
  184.5 88.9 %copy-start.2 = (bf16[32,3584]{1,0:T(8,128)(2,1)S(1)}, bf16[32,3584]{1,0:T(8,128)(2,1)}, u32[]{:S(2)}) copy-start(bf16[32,3584]{1,0:T(8,128)(2,1)} %reduce-scatter.3.cloned.1.call-done) | copy-start | bytes 688132
  184.5 88.9 %copy-start.7 = (f32[3584]{0:T(1024)S(1)}, f32[3584]{0:T(1024)}, u32[]{:S(2)}) copy-start(f32[3584]{0:T(1024)} %param.39) | copy-start | bytes 43012
Sparse Core Ops, SparseCore 0:
  86.3 19.5 reduce-scatter.2
  110.4 52.2 all-gather.1
  184.6 87.6 reduce-scatter.4
where the time goes:
time: 283 us; the launch traced here: 282 us
  waiting for transfers between devices  169 us (60%)
  other arithmetic  34.1 us (12%)
  matrix products  33.4 us (12%)
  starting transfers between devices  16.2 us (6%)
  local copies, waits for them, and re-layouts  15.5 us (5%)
  between operations  14 us (5%)
    reduce_scatter x1, waiting for transfers between devices, local(): lax.psum_scatter(jnp.dot(hidden, w_down, preferred_element_type=jnp.float...  87.8 us
    all_gather x1, waiting for transfers between devices, local(): piece = lax.all_gather(feedforward_input, 'req', axis=0, tiled=True)  52.1 us
    reduce_scatter x1, waiting for transfers between devices, local(): lax.psum_scatter(jnp.dot(attention, w_out, preferred_element_type=jnp.flo...  19.7 us
    dot_general x1, matrix products, local(): jnp.dot(hidden, w_down, preferred_element_type=jnp.float32)  13 us
    all_to_all x1, waiting for transfers between devices, local(): lax.all_to_all(send_keys, 'req', split_axis=0, concat_axis=0, tiled=True)  9.04 us
    dot_general x1, matrix products, local(): gate_part = jnp.dot(piece, w_gate, preferred_element_type=jnp.float32)  8.75 us
    all_to_all x1, starting transfers between devices, local(): lax.all_to_all(send_values, 'req', split_axis=0, concat_axis=0, tiled=True)  8.44 us
    all_to_all x1, starting transfers between devices, local(): lax.all_to_all(send_keys, 'req', split_axis=0, concat_axis=0, tiled=True)  7.45 us
  transfers between devices with their start and end apart: 5, of which 4 were waited for; matrix products, arithmetic and copies ran while one was open for 9% of the time, Pallas kernels for 0%

commit v1 on v0

v1 whole, which is shorter than its diff:
```python
import jax
import jax.numpy as jnp
from jax import lax
from jax.experimental import pallas as pl
from jax.experimental.pallas import tpu as pltpu
from jax.sharding import Mesh, PartitionSpec as P

HEAD_SIZE = 256
WINDOW_LENGTH = 1024
PAGE = 64
WIN_PAGES = 16
OWNERS = 32
POOL = 32
HEADS = 2
ROWS = 32

SOFT_CAP = 50.0
NORM_EPS = 1e-06
ROPE_BASE = 10000.0

BF16 = jnp.bfloat16
F32 = jnp.float32

REQ = ("x", "z", "core")


def rms_scale(values, gain):
    return values * lax.rsqrt(jnp.mean(values * values, axis=-1, keepdims=True) + NORM_EPS) * gain


def apply_rotary(vectors, token_positions):
    half = HEAD_SIZE // 2
    frequency = ROPE_BASE ** (-jnp.arange(half, dtype=F32) * (2.0 / HEAD_SIZE))
    angles = token_positions.astype(F32)[:, None] * frequency[None, :]
    cosine = jnp.cos(angles)[:, None, :]
    sine = jnp.sin(angles)[:, None, :]
    first = vectors[..., :half]
    second = vectors[..., half:]
    return jnp.concatenate(
        [first * cosine - second * sine, second * cosine + first * sine], axis=-1
    )


def token_layout(segment, past):
    requests = jnp.arange(past.shape[0], dtype=jnp.int32)
    member = segment[:, None] == requests[None, :]
    firsts = jnp.sum((segment[:, None] < requests[None, :]).astype(jnp.int32), axis=0)
    offsets = jnp.arange(segment.shape[0], dtype=jnp.int32) - jnp.sum(
        jnp.where(member, firsts[None, :], 0), axis=1
    )
    token_positions = jnp.sum(jnp.where(member, past[None, :], 0), axis=1) + offsets
    return (offsets, token_positions)


def chip_shift(first, k):
    pairs = []
    for x in range(4):
        for z in range(4):
            for c in range(2):
                if (c == 0) == first:
                    to = ((x + k) % 4, z)
                else:
                    to = (x, (z + k) % 4)
                pairs.append(((x * 4 + z) * 2 + c, (to[0] * 4 + to[1]) * 2 + c))
    return pairs


def shift(value, first, k):
    return lax.ppermute(value, REQ, chip_shift(first, k % 4))


def pick_pages_kernel(pages_ref, keys_ref, values_ref, out_ref, sems):
    copies = []
    for d in range(OWNERS):
        page = pages_ref[d]
        copies.append(pltpu.make_async_copy(keys_ref.at[page], out_ref.at[d, 0], sems.at[d, 0]))
        copies.append(pltpu.make_async_copy(values_ref.at[page], out_ref.at[d, 1], sems.at[d, 1]))
    for copy in copies:
        copy.start()
    for copy in copies:
        copy.wait()


def pick_pages(pages, keys, values):
    return pl.pallas_call(
        pick_pages_kernel,
        out_shape=jax.ShapeDtypeStruct((OWNERS, 2, PAGE, HEAD_SIZE), BF16),
        grid_spec=pltpu.PrefetchScalarGridSpec(
            num_scalar_prefetch=1,
            grid=(),
            in_specs=[pl.BlockSpec(memory_space=pl.ANY)] * 2,
            out_specs=pl.BlockSpec(memory_space=pl.ANY),
            scratch_shapes=[pltpu.SemaphoreType.DMA((OWNERS, 2))],
        ),
        name="pick_pages",
    )(pages, keys, values)


def weights_of(query, keys, visible):
    scores = lax.dot_general(
        query, keys, (((1,), (1,)), ((), ())), preferred_element_type=F32
    )
    raw = jnp.exp(SOFT_CAP * jnp.tanh(scores * (1.0 / (16.0 * SOFT_CAP))))
    return jnp.where(visible, raw, 0.0)


def attend(query_ref, keys, values, visible, acc_ref, total_ref):
    for h in range(HEADS):
        weight = weights_of(query_ref[h], keys, visible)
        total_ref[h] += jnp.broadcast_to(
            jnp.sum(weight, axis=-1, keepdims=True), total_ref.shape[1:]
        )
        acc_ref[h] += jnp.dot(weight.astype(BF16), values, preferred_element_type=F32)


STEP_PAGES = 8
STEP = STEP_PAGES * PAGE


def own_kernel(low_ref, high_ref, order_ref, seg_row_ref, query_ref, new_keys_ref, new_values_ref,
               code_ref, keys_ref, values_ref, acc_ref, total_ref):
    acc_ref[...] = jnp.zeros_like(acc_ref)
    total_ref[...] = jnp.zeros_like(total_ref)
    low, high, order = low_ref[...], high_ref[...], order_ref[...]
    count = order.shape[0]
    column = lax.broadcasted_iota(jnp.int32, (count, count), 1)
    same = lax.div(high, 4096) == seg_row_ref[...]
    attend(query_ref, new_keys_ref[...], new_values_ref[...], same & (column <= order), acc_ref, total_ref)
    for b in range(POOL // STEP_PAGES):
        keys = keys_ref[b * STEP_PAGES:(b + 1) * STEP_PAGES].reshape(STEP, HEAD_SIZE)
        values = values_ref[b * STEP_PAGES:(b + 1) * STEP_PAGES].reshape(STEP, HEAD_SIZE)
        code = code_ref[:, b * STEP:(b + 1) * STEP]
        attend(query_ref, keys, values, (code > low) & (code < high), acc_ref, total_ref)


def own_attention(low, high, order, seg_row, query, new_keys, new_values, code, keys, values):
    vmem = pl.BlockSpec(memory_space=pltpu.VMEM)
    return pl.pallas_call(
        own_kernel,
        out_shape=(
            jax.ShapeDtypeStruct((HEADS, 128, HEAD_SIZE), F32),
            jax.ShapeDtypeStruct((HEADS, 128, 128), F32),
        ),
        in_specs=[vmem] * 10,
        out_specs=(vmem, vmem),
        cost_estimate=pl.CostEstimate(
            flops=4 * 256 * 2176 * 256, transcendentals=2 * 256 * 2176, bytes_accessed=3_000_000
        ),
        name="own_attention",
    )(low, high, order, seg_row, query, new_keys, new_values, code, keys, values)


def far_kernel(low_ref, high_ref, query_ref, code_ref, pages_ref, acc_in_ref, total_in_ref, w_ref,
               out_ref, acc_ref, total_ref):
    acc_ref[...] = acc_in_ref[...]
    total_ref[...] = total_in_ref[...]
    low, high = low_ref[...], high_ref[...]
    for b in range(OWNERS // STEP_PAGES):
        keys = pages_ref[b * STEP_PAGES:(b + 1) * STEP_PAGES, 0].reshape(STEP, HEAD_SIZE)
        values = pages_ref[b * STEP_PAGES:(b + 1) * STEP_PAGES, 1].reshape(STEP, HEAD_SIZE)
        code = code_ref[:, b * STEP:(b + 1) * STEP]
        attend(query_ref, keys, values, (code > low) & (code < high), acc_ref, total_ref)
    heads = [(acc_ref[h] / total_ref[h][:, :1]).astype(BF16) for h in range(HEADS)]
    attention = jnp.concatenate(heads, axis=1)
    width = out_ref.shape[1]
    for n in range(0, width, 512):
        out_ref[:, n:n + 512] = jnp.dot(
            attention, w_ref[:, n:n + 512], preferred_element_type=F32
        ).astype(BF16)


def far_attention(low, high, query, code, pages, acc, total, w_out):
    vmem = pl.BlockSpec(memory_space=pltpu.VMEM)
    width = w_out.shape[1]
    return pl.pallas_call(
        far_kernel,
        out_shape=jax.ShapeDtypeStruct((128, width), BF16),
        in_specs=[vmem] * 8,
        out_specs=vmem,
        scratch_shapes=[
            pltpu.VMEM((HEADS, 128, HEAD_SIZE), F32),
            pltpu.VMEM((HEADS, 128, 128), F32),
        ],
        cost_estimate=pl.CostEstimate(
            flops=4 * 256 * 2048 * 256, transcendentals=2 * 256 * 2048, bytes_accessed=7_000_000
        ),
        compiler_params=pltpu.CompilerParams(vmem_limit_bytes=24 * 1024 * 1024),
        name="far_attention",
    )(low, high, query, code, pages, acc, total, w_out)


def enter_kernel(own_ref, a_ref, b_ref, c_ref, d_ref, post_ref, ffw_ref, residual_ref, out_ref):
    total = (a_ref[...].astype(F32) + b_ref[...].astype(F32)) + (
        c_ref[...].astype(F32) + d_ref[...].astype(F32)
    )
    residual = own_ref[...].astype(F32) + rms_scale(total, post_ref[...])
    residual_ref[...] = residual
    out_ref[...] = rms_scale(residual, ffw_ref[...]).astype(BF16)


def leave_kernel(residual_ref, a_ref, b_ref, c_ref, d_ref, post_ref, out_ref):
    total = (a_ref[...].astype(F32) + b_ref[...].astype(F32)) + (
        c_ref[...].astype(F32) + d_ref[...].astype(F32)
    )
    out_ref[...] = (residual_ref[...] + rms_scale(total, post_ref[...])).astype(BF16)


def local(
    tokens,
    segment_ids,
    past_len,
    page_table,
    migrate_pages,
    pooled_key_cache,
    pooled_value_cache,
    attn_gain,
    w_query,
    key_matrix,
    value_matrix,
    w_out,
    post_attn_gain,
    ffw_gain,
    w_gate,
    w_up,
    w_down,
    post_ffw_gain,
):
    tok_count, width = tokens.shape
    here = lax.axis_index("mlp")
    other = [(0, 1), (1, 0)]

    packed = pick_pages(migrate_pages.reshape(-1), pooled_key_cache, pooled_value_cache)
    received = lax.all_to_all(packed, REQ, split_axis=0, concat_axis=0, tiled=True)

    gate_sib = lax.ppermute(w_gate, "core", other)
    up_sib = lax.ppermute(w_up, "core", other)
    down_sib = lax.ppermute(w_down, "core", other)

    segment = segment_ids[0]
    past = past_len[0]
    offsets, token_positions = token_layout(segment, past)
    normalized_input = rms_scale(tokens.astype(F32), attn_gain).astype(BF16)
    query_rows = apply_rotary(
        jnp.dot(normalized_input, w_query, preferred_element_type=F32).reshape(
            tok_count, HEADS, HEAD_SIZE
        ),
        token_positions,
    ).astype(BF16)
    incoming_keys = apply_rotary(
        jnp.dot(normalized_input, key_matrix, preferred_element_type=F32).reshape(
            tok_count, 1, HEAD_SIZE
        ),
        token_positions,
    ).astype(BF16).reshape(tok_count, HEAD_SIZE)
    incoming_values = jnp.dot(
        normalized_input, value_matrix, preferred_element_type=F32
    ).astype(BF16)

    page_ids = jnp.arange(2 * POOL, dtype=jnp.int32)
    place = jnp.sum(
        jnp.where(page_table[0][None, :] == page_ids[:, None], page_ids[None, :], 0), axis=1
    )
    page_req = place // WIN_PAGES
    page_past = jnp.sum(
        jnp.where(page_req[:, None] == jnp.arange(4, dtype=jnp.int32)[None, :], past[None, :], 0),
        axis=1,
    )
    slot = (place % WIN_PAGES * PAGE)[:, None] + jnp.arange(PAGE, dtype=jnp.int32)[None, :]
    code = jnp.where(
        slot >= WINDOW_LENGTH - page_past[:, None], page_req[:, None] * 4096 + slot, -1
    ).reshape(1, -1)

    order = (jnp.arange(tok_count, dtype=jnp.int32) + here * ROWS) % tok_count
    turn = lambda v: lax.dynamic_slice_in_dim(jnp.concatenate([v, v], 0), here * ROWS, tok_count, 0)
    low = turn(segment * 4096 + offsets)[:, None]
    high = turn(segment * 4096 + WINDOW_LENGTH)[:, None]
    query = turn(query_rows).transpose(1, 0, 2)
    own_rows = lax.dynamic_slice_in_dim(tokens, here * ROWS, ROWS, 0)

    acc, total = own_attention(
        low, high, order[:, None], segment[None, :], query, incoming_keys, incoming_values,
        code[:, : POOL * PAGE], pooled_key_cache, pooled_value_cache,
    )
    partial = far_attention(
        low, high, query, code[:, POOL * PAGE:], received, acc, total, w_out
    )

    parts = [partial[k * ROWS:(k + 1) * ROWS] for k in range(4)]
    for k in range(1, 4):
        parts[k] = lax.ppermute(parts[k], "mlp", [(i, (i + k) % 4) for i in range(4)])
    vmem = pl.BlockSpec(memory_space=pltpu.VMEM)
    residual, entering = pl.pallas_call(
        enter_kernel,
        out_shape=(
            jax.ShapeDtypeStruct((ROWS, width), F32),
            jax.ShapeDtypeStruct((ROWS, width), BF16),
        ),
        in_specs=[vmem] * 7,
        out_specs=(vmem, vmem),
        name="enter",
    )(own_rows, *parts, post_attn_gain[None, :], ffw_gain[None, :])

    line = jnp.concatenate([entering] + [shift(entering, True, k) for k in (1, 2, 3)], axis=0)
    far = jnp.concatenate([shift(line, False, k) for k in (1, 2, 3)], axis=0)

    def hidden_of(rows, gate, up):
        gate_part = jnp.dot(rows, gate, preferred_element_type=F32)
        up_part = jnp.dot(rows, up, preferred_element_type=F32)
        return (jax.nn.gelu(gate_part, approximate=True) * up_part).astype(BF16)

    def mlp(rows):
        return jnp.dot(hidden_of(rows, w_gate, w_up), w_down, preferred_element_type=F32) + jnp.dot(
            hidden_of(rows, gate_sib, up_sib), down_sib, preferred_element_type=F32
        )

    near_out = mlp(line)
    far_out = mlp(far).astype(BF16)
    step = 4 * ROWS
    back = [shift(far_out[(k - 1) * step:k * step], False, -k) for k in (1, 2, 3)]
    line_out = near_out + sum(b.astype(F32) for b in back)
    line_out = line_out.astype(BF16)
    ends = [line_out[:ROWS]] + [
        shift(line_out[k * ROWS:(k + 1) * ROWS], True, -k) for k in (1, 2, 3)
    ]
    mixed = pl.pallas_call(
        leave_kernel,
        out_shape=jax.ShapeDtypeStruct((ROWS, width), BF16),
        in_specs=[vmem] * 6,
        out_specs=vmem,
        name="leave",
    )(residual, *ends, post_ffw_gain[None, :])
    return (mixed, incoming_keys, incoming_values)


def solution(mesh):
    chips = Mesh(mesh.devices.reshape(4, 4, 2, 4), ("x", "z", "core", "mlp"))
    return jax.shard_map(
        local,
        mesh=chips,
        in_specs=(
            P(REQ, None),
            P(REQ, None),
            P(REQ, None),
            P(REQ, None),
            P(REQ, None, None),
            P(REQ, None, "mlp"),
            P(REQ, None, "mlp"),
            P(),
            P(None, "mlp"),
            P(None, "mlp"),
            P(None, "mlp"),
            P("mlp", None),
            P(),
            P(),
            P(None, REQ),
            P(None, REQ),
            P(REQ, None),
            P(),
        ),
        out_specs=(P((*REQ, "mlp"), None), P(REQ, "mlp"), P(REQ, "mlp")),
        check_vma=False,
    )
```

time: 283 us -> 260 us (0.919)
  waiting for transfers between devices: 169 us -> 82.2 us
  Pallas kernels: 0 us -> 79.8 us
  other arithmetic: 34.1 us -> 3.56 us
  matrix products: 33.4 us -> 48.7 us
  between operations: 14 us -> 1.04 us
  starting transfers between devices: 16.2 us -> 23.8 us
    reduce_scatter x2 -> x0, waiting for transfers between devices: 107 us -> none  [the longest x1 87.8 us: local(): lax.psum_scatter(jnp.dot(hidden, w_down, preferred_element_type=jnp.float...]
    pallas_call x0 -> x5, Pallas kernels: none -> 79.8 us  [the longest x1 66 us: pick_pages(): pl.pallas_call(pick_pages_kernel, out_shape=jax.ShapeDtypeStruct((OWNERS,...]
    ppermute x0 -> x18, waiting for transfers between devices: none -> 71 us  [the longest x12 61.3 us: shift(): return lax.ppermute(value, REQ, chip_shift(first, k % 4))]
    all_gather x1 -> x0, waiting for transfers between devices: 52.1 us -> none  [local(): piece = lax.all_gather(feedforward_input, 'req', axis=0, tiled=True)]
    dot_general x10 -> x11, matrix products: 33.4 us -> 48.7 us  [the longest x2 17.9 us: mlp(): jnp.dot(hidden_of(rows, gate_sib, up_sib), down_sib, preferred_element_ty...]
    ppermute x0 -> x18, starting transfers between devices: none -> 15.3 us  [the longest x12 11.2 us: shift(): return lax.ppermute(value, REQ, chip_shift(first, k % 4))]
    gather x4 -> x0, local copies, waits for them, and re-layouts: 13.1 us -> none  [the longest x1 3.71 us: local(): jnp.take(listed_keys, page_lookup, axis=0).reshape(-1, key_heads, HEAD_SIZE)]
    all_to_all x2 -> x1, starting transfers between devices: 15.9 us -> 8.44 us  [local(): lax.all_to_all(packed, REQ, split_axis=0, concat_axis=0, tiled=True)]
  transfers between devices with their start and end apart: 5 -> 19, of which waited for: 4 -> 11; matrix products, arithmetic and copies ran while one was open for 9% -> 16% of each run, Pallas kernels for 0% -> 4%
where the time goes in v1:
time: 260 us; the launch traced here: 257 us
  waiting for transfers between devices  82.2 us (32%)
  Pallas kernels  79.8 us (31%)
  matrix products  48.7 us (19%)
  starting transfers between devices  23.8 us (9%)
  local copies, waits for them, and re-layouts  17.4 us (7%)
  other arithmetic  3.56 us (1%)
    pallas_call x1, Pallas kernels, pick_pages(): pl.pallas_call(pick_pages_kernel, out_shape=jax.ShapeDtypeStruct((OWNERS,...  66 us
    ppermute x12, waiting for transfers between devices, shift(): return lax.ppermute(value, REQ, chip_shift(first, k % 4))  61.3 us
    dot_general x2, matrix products, mlp(): jnp.dot(hidden_of(rows, gate_sib, up_sib), down_sib, preferred_element_ty...  17.9 us
    dot_general x2, matrix products, mlp(): jnp.dot(hidden_of(rows, w_gate, w_up), w_down, preferred_element_type=F32)  16.2 us
    all_to_all x1, waiting for transfers between devices, local(): lax.all_to_all(packed, REQ, split_axis=0, concat_axis=0, tiled=True)  11.2 us
    ppermute x12, starting transfers between devices, shift(): return lax.ppermute(value, REQ, chip_shift(first, k % 4))  11.2 us
    ppermute x3, waiting for transfers between devices, local(): lax.ppermute(parts[k], 'mlp', [(i, (i + k) % 4) for i in range(4)])  9.69 us
    dot_general x4, matrix products, hidden_of(): gate_part = jnp.dot(rows, gate, preferred_element_type=F32)  9.44 us
  transfers between devices with their start and end apart: 19, of which 11 were waited for; matrix products, arithmetic and copies ran while one was open for 16% of the time, Pallas kernels for 4%

profile of v1, /device:TPU:16, one launch (start us, length us, event | category | flops | bytes accessed | tf_op | source)
XLA Modules:
  0.0 256.5 jit_solution(7278384515536186784)
XLA Ops:
  0.6 66.0 %pick_pages.1 = bf16[32,2,64,256]{3,2,1,0:T(8,128)(2,1)} custom-call(s32[32]{0:T(128)} %bitcast.45, bf16[32,64,256]{2,1,0:T(8,128)(2,1)} %keys_ref.3, bf16[32,64,256]{2,1,0:T(8,128)(2,1)} %values_ref.3), custom_call_target="tpu_custom_call" | custom-call | tf_op jit(solution)/shard_map/pick_pages/pallas_call | solution.py:85
  66.7 8.4 %all-to-all-start = ((bf16[32,2,64,256]{3,2,1,0:T(8,128)(2,1)}), bf16[32,2,64,256]{3,2,1,0:T(8,128)(2,1)}, u32[]{:S(2)}, u32[]{:S(2)}) async-start(bf16[32,2,64,256]{3,2,1,0:T(8,128)(2,1)} %pick_pages.1), calls=%async_computation | async-start | bytes 4194304 | tf_op jit(solution)/shard_map/all_to_all | solution.py:233
  76.9 3.6 %fusion.103 = f32[128,512]{0,1:T(8,128)S(1)} fusion(bf16[3584,512]{1,0:T(8,128)(2,1)} %param.26, bf16[128,3584]{1,0:T(8,128)(2,1)S(1)} %copy-done.8, f32[3584]{0:T(1024)S(1)} %copy-done.18, f32[128]{0:T(128)S(1)} %add_rsqrt_fusion), kind=kOutput, calls=%fused_computation.156 | convolution fusion | flops 471597056 | bytes 4864512 | tf_op jit(solution)/shard_map/dot_general | solution.py:244
  86.4 1.1 convolution_convert_fusion.new_values_ref
  88.1 4.8 %own_attention.1 = (f32[2,128,256]{2,1,0:T(8,128)}, f32[2,128,128]{2,1,0:T(8,128)}) custom-call(s32[128,1]{1,0:T(8,128)} %copy.37.low_ref, s32[128,1]{1,0:T(8,128)} %copy.38.high_ref, s32[128,1]{1,0:T(8,128)} %add_select_fusion.order_ref, s32[1,128]{1,0:T(1,128)} %seg_row_ref.1, bf16[2,128,256]{2,1,0:T(8,128)(2,1)} %fusion.55.query_ref, ...), custom_call_target="tpu_custom_call" | custom-call | flops 570425344 | bytes 3000000 | tf_op jit(solution)/shard_map/own_attention/pallas_call | solution.py:138
  92.9 11.2 %all-to-all-done.pages_ref = bf16[32,2,64,256]{3,2,1,0:T(8,128)(2,1)} async-done(((bf16[32,2,64,256]{3,2,1,0:T(8,128)(2,1)}), bf16[32,2,64,256]{3,2,1,0:T(8,128)(2,1)}, u32[]{:S(2)}, u32[]{:S(2)}) %all-to-all-start) | async-done | bytes 2097184 | tf_op jit(solution)/shard_map/all_to_all | solution.py:233
  104.1 2.0 copy-done.2
  108.0 4.2 %far_attention.1 = bf16[128,3584]{1,0:T(8,128)(2,1)S(1)} custom-call(s32[128,1]{1,0:T(8,128)S(1)} %copy-done.5, s32[128,1]{1,0:T(8,128)S(1)} %copy-done.4, bf16[2,128,256]{2,1,0:T(8,128)(2,1)S(1)} %copy-done.3, s32[1,2048]{1,0:T(1,128)S(1)} %get-tuple-element.33.code_ref, bf16[32,2,64,256]{3,2,1,0:T(8,128)(2,1)} %all-to-all-done.pages_ref, ...), custom_call_target="tpu_custom_call" | custom-call | flops 536870912 | bytes 7000000 | tf_op jit(solution)/shard_map/far_attention/pallas_call | solution.py:175
  113.4 2.9 %collective-permute-start.1 = (bf16[32,3584]{1,0:T(8,128)(2,1)S(1)}, bf16[32,3584]{1,0:T(8,128)(2,1)S(1)}, u32[]{:S(2)}, u32[]{:S(2)}) collective-permute-start(bf16[32,3584]{1,0:T(8,128)(2,1)S(1)} %get-tuple-element.23), channel_id=1, source_target_pairs={{0,2},{1,3},{2,0},{3,1},{4,6},{5,7},{6,4},{7,5},{8,10},{9,11},{10,... | collective-permute-start | bytes 688136 | tf_op jit(solution)/shard_map/ppermute | solution.py:290
  117.0 4.5 %collective-permute-done.2.d_ref = bf16[32,3584]{1,0:T(8,128)(2,1)S(1)} collective-permute-done((bf16[32,3584]{1,0:T(8,128)(2,1)S(1)}, bf16[32,3584]{1,0:T(8,128)(2,1)S(1)}, u32[]{:S(2)}, u32[]{:S(2)}) %collective-permute-start.2) | collective-permute-done | bytes 229408 | tf_op jit(solution)/shard_map/ppermute | solution.py:290
  121.5 2.0 collective-permute-done.1.c_ref
  123.5 3.2 %collective-permute-done.b_ref = bf16[32,3584]{1,0:T(8,128)(2,1)S(1)} collective-permute-done((bf16[32,3584]{1,0:T(8,128)(2,1)S(1)}, bf16[32,3584]{1,0:T(8,128)(2,1)S(1)}, u32[]{:S(2)}, u32[]{:S(2)}) %collective-permute-start) | collective-permute-done | bytes 229408 | tf_op jit(solution)/shard_map/ppermute | solution.py:290
  127.4 2.5 enter.1
  133.4 7.5 %collective-permute-done.3 = bf16[32,3584]{1,0:T(8,128)(2,1)S(1)} collective-permute-done((bf16[32,3584]{1,0:T(8,128)(2,1)}, bf16[32,3584]{1,0:T(8,128)(2,1)S(1)}, u32[]{:S(2)}, u32[]{:S(2)}) %collective-permute-start.3) | collective-permute-done | bytes 229408 | tf_op jit(solution)/shard_map/ppermute | solution.py:69
  141.3 2.5 collective-permute-start.10
  144.3 21.3 %collective-permute-done.9 = bf16[128,3584]{1,0:T(8,128)(2,1)S(1)} collective-permute-done((bf16[128,3584]{1,0:T(8,128)(2,1)S(1)}, bf16[128,3584]{1,0:T(8,128)(2,1)S(1)}, u32[]{:S(2)}, u32[]{:S(2)}) %collective-permute-start.9) | collective-permute-done | bytes 917536 | tf_op jit(solution)/shard_map/ppermute | solution.py:69
  165.7 13.2 %collective-permute-done.11 = bf16[128,3584]{1,0:T(8,128)(2,1)S(1)} collective-permute-done((bf16[128,3584]{1,0:T(8,128)(2,1)S(1)}, bf16[128,3584]{1,0:T(8,128)(2,1)S(1)}, u32[]{:S(2)}, u32[]{:S(2)}) %collective-permute-start.11) | collective-permute-done | bytes 917536 | tf_op jit(solution)/shard_map/ppermute | solution.py:69
  179.0 1.8 fusion.120
  180.9 3.7 %fusion.121 = f32[384,448]{0,1:T(8,128)S(1)} fusion(bf16[384,3584]{1,0:T(8,128)(2,1)S(1)} %constant_dynamic-update-slice_fusion.4, bf16[3584,448]{0,1:T(8,128)(2,1)} %collective-permute-done.6), kind=kOutput, calls=%fused_computation.169 | convolution fusion | flops 1233125376 | bytes 6651904 | tf_op jit(solution)/shard_map/dot_general | solution.py:307
  184.7 9.5 %fusion.25 = f32[384,3584]{1,0:T(8,128)} fusion(bf16[448,3584]{1,0:T(8,128)(2,1)} %param.34, f32[384,448]{0,1:T(8,128)S(1)} %fusion.120, bf16[384,3584]{1,0:T(8,128)(2,1)} %copy-done.11, bf16[3584,448]{0,1:T(8,128)(2,1)} %param.33), kind=kOutput, calls=%fused_computation.32 | convolution fusion | flops 2467971072 | bytes 15368192 | tf_op jit(solution)/shard_map/dot_general | solution.py:312
  194.2 10.2 %fusion = bf16[384,3584]{1,0:T(8,128)(2,1)} fusion(f32[384,3584]{1,0:T(8,128)} %fusion.25, bf16[448,3584]{1,0:T(8,128)(2,1)} %collective-permute-done.8, f32[384,448]{0,1:T(8,128)S(1)} %fusion.121, bf16[384,3584]{1,0:T(8,128)(2,1)} %copy-done.11, bf16[3584,448]{0,1:T(8,128)(2,1)} %collective-permute-done.7), kind=kOutput, calls=%fused_computation.1 | convolution fusion | flops 2470723584 | bytes 18120704 | tf_op jit(solution)/shard_map/dot_general | solution.py:312
  204.4 3.0 %fusion.105 = (bf16[128,3584]{1,0:T(8,128)(2,1)}, bf16[128,3584]{1,0:T(8,128)(2,1)S(1)}, bf16[128,3584]{1,0:T(8,128)(2,1)S(1)}) fusion(bf16[384,3584]{1,0:T(8,128)(2,1)} %fusion), kind=kLoop, calls=%fused_computation.157 | loop fusion | bytes 5505024 | tf_op jit(solution)/shard_map/slice | solution.py:319
  207.4 1.2 collective-permute-start.12
  211.1 6.6 %fusion.58 = f32[128,3584]{1,0:T(8,128)} fusion(bf16[448,3584]{1,0:T(8,128)(2,1)} %param.34, f32[128,448]{0,1:T(8,128)S(1)} %fusion.118, bf16[128,3584]{1,0:T(8,128)(2,1)S(1)} %constant_dynamic-update-slice_fusion, bf16[3584,448]{0,1:T(8,128)(2,1)} %param.33), kind=kOutput, calls=%fused_computation.71 | convolution fusion | flops 822657024 | bytes 9404416 | tf_op jit(solution)/shard_map/dot_general | solution.py:312
  217.7 2.9 %fusion.119 = f32[128,448]{0,1:T(8,128)S(1)} fusion(bf16[128,3584]{1,0:T(8,128)(2,1)S(1)} %constant_dynamic-update-slice_fusion, bf16[3584,448]{0,1:T(8,128)(2,1)} %collective-permute-done.6), kind=kOutput, calls=%fused_computation.167 | convolution fusion | flops 411041792 | bytes 4358144 | tf_op jit(solution)/shard_map/dot_general | solution.py:307
  221.1 12.0 %collective-permute-done.14 = bf16[128,3584]{1,0:T(8,128)(2,1)} collective-permute-done((bf16[128,3584]{1,0:T(8,128)(2,1)S(1)}, bf16[128,3584]{1,0:T(8,128)(2,1)}, u32[]{:S(2)}, u32[]{:S(2)}) %collective-permute-start.14) | collective-permute-done | bytes 917536 | tf_op jit(solution)/shard_map/ppermute | solution.py:69
  233.2 7.7 %fusion.2 = bf16[128,3584]{1,0:T(8,128)(2,1)} fusion(f32[128,3584]{1,0:T(8,128)} %fusion.58, bf16[448,3584]{1,0:T(8,128)(2,1)} %collective-permute-done.8, bf16[128,3584]{1,0:T(8,128)(2,1)} %collective-permute-done.14, bf16[128,3584]{1,0:T(8,128)(2,1)} %collective-permute-done.13, bf16[128,3584]{1,0:T(8,128)(2,1)} %collective-permute-done.12, ...), kind=kOutput, calls=%fused_computation.4 | convolution fusion | flops 826327040 | bytes 13074432 | tf_op jit(solution)/shard_map/dot_general | solution.py:312
  240.9 2.0 fusion.106
  242.9 2.0 collective-permute-start.16
  245.0 1.2 collective-permute-start.15
  246.8 5.8 %collective-permute-done.17.d_ref = bf16[32,3584]{1,0:T(8,128)(2,1)S(1)} collective-permute-done((bf16[32,3584]{1,0:T(8,128)(2,1)S(1)}, bf16[32,3584]{1,0:T(8,128)(2,1)S(1)}, u32[]{:S(2)}, u32[]{:S(2)}) %collective-permute-start.17) | collective-permute-done | bytes 229408 | tf_op jit(solution)/shard_map/ppermute | solution.py:69
  254.2 2.3 leave.1
  (115 shorter events, 22.2 us)
Async XLA Ops:
  0.6 83.2 %copy-start = (bf16[3584,256]{1,0:T(8,128)(2,1)S(1)}, bf16[3584,256]{1,0:T(8,128)(2,1)}, u32[]{:S(2)}) copy-start(bf16[3584,256]{1,0:T(8,128)(2,1)} %param.27) | copy-start | bytes 5505028
  66.7 9.5 %copy-start.25 = (s32[1,64]{1,0:T(1,128)S(1)}, s32[1,64]{1,0:T(1,128)}, u32[]{:S(2)}) copy-start(s32[1,64]{1,0:T(1,128)} %param.21) | copy-start | bytes 772
  66.7 9.6 %copy-start.22 = (s32[1,128]{1,0:T(1,128)S(1)}, s32[1,128]{1,0:T(1,128)}, u32[]{:S(2)}) copy-start(s32[1,128]{1,0:T(1,128)} %seg_row_ref.1) | copy-start | bytes 1540
  66.7 9.7 %copy-start.8 = (bf16[128,3584]{1,0:T(8,128)(2,1)S(1)}, bf16[128,3584]{1,0:T(8,128)(2,1)}, u32[]{:S(2)}) copy-start(bf16[128,3584]{1,0:T(8,128)(2,1)} %param.18) | copy-start | bytes 2752516
  66.7 10.0 %copy-start.23 = (s32[1,4]{1,0:T(1,128)S(1)}, s32[1,4]{1,0:T(1,128)}, u32[]{:S(2)}) copy-start(s32[1,4]{1,0:T(1,128)} %param.20) | copy-start | bytes 52
  66.7 10.2 %copy-start.18 = (f32[3584]{0:T(1024)S(1)}, f32[3584]{0:T(1024)}, u32[]{:S(2)}) copy-start(f32[3584]{0:T(1024)} %param.25) | copy-start | bytes 43012
  66.7 37.3 %all-to-all-start = ((bf16[32,2,64,256]{3,2,1,0:T(8,128)(2,1)}), bf16[32,2,64,256]{3,2,1,0:T(8,128)(2,1)}, u32[]{:S(2)}, u32[]{:S(2)}) async-start(bf16[32,2,64,256]{3,2,1,0:T(8,128)(2,1)} %pick_pages.1), calls=%async_computation | async-start | bytes 4194304 | tf_op jit(solution)/shard_map/all_to_all | solution.py:233
  75.2 105.7 %collective-permute-start.6 = (bf16[3584,448]{0,1:T(8,128)(2,1)}, bf16[3584,448]{0,1:T(8,128)(2,1)}, u32[]{:S(2)}, u32[]{:S(2)}) collective-permute-start(bf16[3584,448]{0,1:T(8,128)(2,1)} %param.32), channel_id=1, source_target_pairs={{0,4},{4,0},{1,5},{5,1},{2,6},{6,2},{3,7},{7,3},{8,12},{12,8},{9,1... | collective-permute-start | bytes 9633800 | tf_op jit(solution)/shard_map/ppermute | solution.py:235
  86.4 17.7 %copy-start.3 = (bf16[2,128,256]{2,1,0:T(8,128)(2,1)S(1)}, bf16[2,128,256]{2,1,0:T(8,128)(2,1)}, u32[]{:S(2)}) copy-start(bf16[2,128,256]{2,1,0:T(8,128)(2,1)} %fusion.55.query_ref) | copy-start | bytes 393220
  86.4 17.7 %copy-start.4 = (s32[128,1]{1,0:T(8,128)S(1)}, s32[128,1]{1,0:T(8,128)}, u32[]{:S(2)}) copy-start(s32[128,1]{1,0:T(8,128)} %copy.38.high_ref) | copy-start | bytes 1540
  86.4 17.7 %copy-start.5 = (s32[128,1]{1,0:T(8,128)S(1)}, s32[128,1]{1,0:T(8,128)}, u32[]{:S(2)}) copy-start(s32[128,1]{1,0:T(8,128)} %copy.37.low_ref) | copy-start | bytes 1540
  112.9 8.5 %collective-permute-start.2 = (bf16[32,3584]{1,0:T(8,128)(2,1)S(1)}, bf16[32,3584]{1,0:T(8,128)(2,1)S(1)}, u32[]{:S(2)}, u32[]{:S(2)}) collective-permute-start(bf16[32,3584]{1,0:T(8,128)(2,1)S(1)} %get-tuple-element.22), channel_id=1, source_target_pairs={{0,3},{1,0},{2,1},{3,2},{4,7},{5,4},{6,5},{7,6},{8,11},{9,8},{10,9... | collective-permute-start | bytes 688136 | tf_op jit(solution)/shard_map/ppermute | solution.py:290
  113.4 10.1 %collective-permute-start.1 = (bf16[32,3584]{1,0:T(8,128)(2,1)S(1)}, bf16[32,3584]{1,0:T(8,128)(2,1)S(1)}, u32[]{:S(2)}, u32[]{:S(2)}) collective-permute-start(bf16[32,3584]{1,0:T(8,128)(2,1)S(1)} %get-tuple-element.23), channel_id=1, source_target_pairs={{0,2},{1,3},{2,0},{3,1},{4,6},{5,7},{6,4},{7,5},{8,10},{9,11},{10,... | collective-permute-start | bytes 688136 | tf_op jit(solution)/shard_map/ppermute | solution.py:290
  116.3 10.4 %collective-permute-start = (bf16[32,3584]{1,0:T(8,128)(2,1)S(1)}, bf16[32,3584]{1,0:T(8,128)(2,1)S(1)}, u32[]{:S(2)}, u32[]{:S(2)}) collective-permute-start(bf16[32,3584]{1,0:T(8,128)(2,1)S(1)} %get-tuple-element.24), channel_id=1, source_target_pairs={{0,1},{1,2},{2,3},{3,0},{4,5},{5,6},{6,7},{7,4},{8,9},{9,10},{10,1... | collective-permute-start | bytes 688136 | tf_op jit(solution)/shard_map/ppermute | solution.py:290
  129.9 11.1 %collective-permute-start.5 = (bf16[32,3584]{1,0:T(8,128)(2,1)}, bf16[32,3584]{1,0:T(8,128)(2,1)S(1)}, u32[]{:S(2)}, u32[]{:S(2)}) collective-permute-start(bf16[32,3584]{1,0:T(8,128)(2,1)} %get-tuple-element.10), channel_id=1, source_target_pairs={{0,96},{4,28},{8,104},{12,4},{16,112},{20,12},{24,120},{28,20},{32... | collective-permute-start | bytes 688136 | tf_op jit(solution)/shard_map/ppermute | solution.py:69
  130.8 10.2 %collective-permute-start.4 = (bf16[32,3584]{1,0:T(8,128)(2,1)}, bf16[32,3584]{1,0:T(8,128)(2,1)S(1)}, u32[]{:S(2)}, u32[]{:S(2)}) collective-permute-start(bf16[32,3584]{1,0:T(8,128)(2,1)} %get-tuple-element.10), channel_id=1, source_target_pairs={{0,64},{4,20},{8,72},{12,28},{16,80},{20,4},{24,88},{28,12},{32,96... | collective-permute-start | bytes 688136 | tf_op jit(solution)/shard_map/ppermute | solution.py:69
  131.5 9.5 %collective-permute-start.3 = (bf16[32,3584]{1,0:T(8,128)(2,1)}, bf16[32,3584]{1,0:T(8,128)(2,1)S(1)}, u32[]{:S(2)}, u32[]{:S(2)}) collective-permute-start(bf16[32,3584]{1,0:T(8,128)(2,1)} %get-tuple-element.10), channel_id=1, source_target_pairs={{0,32},{4,12},{8,40},{12,20},{16,48},{20,28},{24,56},{28,4},{32,64... | collective-permute-start | bytes 688136 | tf_op jit(solution)/shard_map/ppermute | solution.py:69
  141.1 38.0 %copy-start.9 = (bf16[3584,448]{0,1:T(8,128)(2,1)S(1)}, bf16[3584,448]{0,1:T(8,128)(2,1)}, u32[]{:S(2)}) copy-start(bf16[3584,448]{0,1:T(8,128)(2,1)} %param.32) | copy-start | bytes 9633796
  141.1 24.5 %collective-permute-start.9 = (bf16[128,3584]{1,0:T(8,128)(2,1)S(1)}, bf16[128,3584]{1,0:T(8,128)(2,1)S(1)}, u32[]{:S(2)}, u32[]{:S(2)}) collective-permute-start(bf16[128,3584]{1,0:T(8,128)(2,1)S(1)} %constant_dynamic-update-slice_fusion), channel_id=1, source_target_pairs={{0,8},{4,36},{8,16},{12,44},{16,24},{20,52},{24,0},{28,60},{32,40}... | collective-permute-start | bytes 2752520 | tf_op jit(solution)/shard_map/ppermute | solution.py:69
  141.3 24.3 %collective-permute-start.10 = (bf16[128,3584]{1,0:T(8,128)(2,1)S(1)}, bf16[128,3584]{1,0:T(8,128)(2,1)S(1)}, u32[]{:S(2)}, u32[]{:S(2)}) collective-permute-start(bf16[128,3584]{1,0:T(8,128)(2,1)S(1)} %constant_dynamic-update-slice_fusion), channel_id=1, source_target_pairs={{0,16},{4,68},{8,24},{12,76},{16,0},{20,84},{24,8},{28,92},{32,48}... | collective-permute-start | bytes 2752520 | tf_op jit(solution)/shard_map/ppermute | solution.py:69
  143.8 50.4 %collective-permute-start.7 = (bf16[3584,448]{0,1:T(8,128)(2,1)}, bf16[3584,448]{0,1:T(8,128)(2,1)}, u32[]{:S(2)}, u32[]{:S(2)}) collective-permute-start(bf16[3584,448]{0,1:T(8,128)(2,1)} %param.33), channel_id=1, source_target_pairs={{0,4},{4,0},{1,5},{5,1},{2,6},{6,2},{3,7},{7,3},{8,12},{12,8},{9,1... | collective-permute-start | bytes 9633800 | tf_op jit(solution)/shard_map/ppermute | solution.py:236
  143.8 50.4 %collective-permute-start.8 = (bf16[448,3584]{1,0:T(8,128)(2,1)}, bf16[448,3584]{1,0:T(8,128)(2,1)}, u32[]{:S(2)}, u32[]{:S(2)}) collective-permute-start(bf16[448,3584]{1,0:T(8,128)(2,1)} %param.34), channel_id=1, source_target_pairs={{0,4},{4,0},{1,5},{5,1},{2,6},{6,2},{3,7},{7,3},{8,12},{12,8},{9,1... | collective-permute-start | bytes 9633800 | tf_op jit(solution)/shard_map/ppermute | solution.py:237
  165.6 13.4 %collective-permute-start.11 = (bf16[128,3584]{1,0:T(8,128)(2,1)S(1)}, bf16[128,3584]{1,0:T(8,128)(2,1)S(1)}, u32[]{:S(2)}, u32[]{:S(2)}) collective-permute-start(bf16[128,3584]{1,0:T(8,128)(2,1)S(1)} %constant_dynamic-update-slice_fusion), channel_id=1, source_target_pairs={{0,24},{4,100},{8,0},{12,108},{16,8},{20,116},{24,16},{28,124},{32... | collective-permute-start | bytes 2752520 | tf_op jit(solution)/shard_map/ppermute | solution.py:69
  204.4 5.7 %copy-start.10 = (bf16[3584,448]{0,1:T(8,128)(2,1)S(1)}, bf16[3584,448]{0,1:T(8,128)(2,1)}, u32[]{:S(2)}) copy-start(bf16[3584,448]{0,1:T(8,128)(2,1)} %param.32) | copy-start | bytes 9633796
  207.4 13.7 %collective-permute-start.12 = (bf16[128,3584]{1,0:T(8,128)(2,1)}, bf16[128,3584]{1,0:T(8,128)(2,1)}, u32[]{:S(2)}, u32[]{:S(2)}) collective-permute-start(bf16[128,3584]{1,0:T(8,128)(2,1)} %get-tuple-element.15), channel_id=1, source_target_pairs={{0,24},{4,100},{8,0},{12,108},{16,8},{20,116},{24,16},{28,124},{32... | collective-permute-start | bytes 2752520 | tf_op jit(solution)/shard_map/ppermute | solution.py:69
  208.6 24.5 %collective-permute-start.14 = (bf16[128,3584]{1,0:T(8,128)(2,1)S(1)}, bf16[128,3584]{1,0:T(8,128)(2,1)}, u32[]{:S(2)}, u32[]{:S(2)}) collective-permute-start(bf16[128,3584]{1,0:T(8,128)(2,1)S(1)} %get-tuple-element.16), channel_id=1, source_target_pairs={{0,8},{4,36},{8,16},{12,44},{16,24},{20,52},{24,0},{28,60},{32,40}... | collective-permute-start | bytes 2752520 | tf_op jit(solution)/shard_map/ppermute | solution.py:69
  209.4 23.7 %collective-permute-start.13 = (bf16[128,3584]{1,0:T(8,128)(2,1)S(1)}, bf16[128,3584]{1,0:T(8,128)(2,1)}, u32[]{:S(2)}, u32[]{:S(2)}) collective-permute-start(bf16[128,3584]{1,0:T(8,128)(2,1)S(1)} %get-tuple-element.17), channel_id=1, source_target_pairs={{0,16},{4,68},{8,24},{12,76},{16,0},{20,84},{24,8},{28,92},{32,48}... | collective-permute-start | bytes 2752520 | tf_op jit(solution)/shard_map/ppermute | solution.py:69
  220.6 25.5 %copy-start.21 = (f32[3584]{0:T(1024)S(1)}, f32[3584]{0:T(1024)}, u32[]{:S(2)}) copy-start(f32[3584]{0:T(1024)} %param.35) | copy-start | bytes 43012
  233.2 23.3 %copy-start.1 = (bf16[3584,256]{1,0:T(8,128)(2,1)S(1)}, bf16[3584,256]{1,0:T(8,128)(2,1)}, u32[]{:S(2)}) copy-start(bf16[3584,256]{1,0:T(8,128)(2,1)} %param.27) | copy-start | bytes 5505028
  242.9 9.7 %collective-permute-start.17 = (bf16[32,3584]{1,0:T(8,128)(2,1)S(1)}, bf16[32,3584]{1,0:T(8,128)(2,1)S(1)}, u32[]{:S(2)}, u32[]{:S(2)}) collective-permute-start(bf16[32,3584]{1,0:T(8,128)(2,1)S(1)} %get-tuple-element.18), channel_id=1, source_target_pairs={{0,32},{4,12},{8,40},{12,20},{16,48},{20,28},{24,56},{28,4},{32,64... | collective-permute-start | bytes 688136 | tf_op jit(solution)/shard_map/ppermute | solution.py:69
  242.9 9.7 %collective-permute-start.16 = (bf16[32,3584]{1,0:T(8,128)(2,1)S(1)}, bf16[32,3584]{1,0:T(8,128)(2,1)S(1)}, u32[]{:S(2)}, u32[]{:S(2)}) collective-permute-start(bf16[32,3584]{1,0:T(8,128)(2,1)S(1)} %get-tuple-element.19), channel_id=1, source_target_pairs={{0,64},{4,20},{8,72},{12,28},{16,80},{20,4},{24,88},{28,12},{32,96... | collective-permute-start | bytes 688136 | tf_op jit(solution)/shard_map/ppermute | solution.py:69
  245.0 8.5 %collective-permute-start.15 = (bf16[32,3584]{1,0:T(8,128)(2,1)S(1)}, bf16[32,3584]{1,0:T(8,128)(2,1)S(1)}, u32[]{:S(2)}, u32[]{:S(2)}) collective-permute-start(bf16[32,3584]{1,0:T(8,128)(2,1)S(1)} %get-tuple-element.20), channel_id=1, source_target_pairs={{0,96},{4,28},{8,104},{12,4},{16,112},{20,12},{24,120},{28,20},{32... | collective-permute-start | bytes 688136 | tf_op jit(solution)/shard_map/ppermute | solution.py:69
  (13 other events, 28.9 us)

commit v2 on v1

--- a/solution.py
+++ b/solution.py
@@ -69,6 +69,10 @@
     return lax.ppermute(value, REQ, chip_shift(first, k % 4))
 
 
+def small(megabytes):
+    return pltpu.CompilerParams(vmem_limit_bytes=megabytes * 1024 * 1024)
+
+
 def pick_pages_kernel(pages_ref, keys_ref, values_ref, out_ref, sems):
     copies = []
     for d in range(OWNERS):
@@ -89,9 +93,10 @@
             num_scalar_prefetch=1,
             grid=(),
             in_specs=[pl.BlockSpec(memory_space=pl.ANY)] * 2,
-            out_specs=pl.BlockSpec(memory_space=pl.ANY),
+            out_specs=pl.BlockSpec(memory_space=pltpu.VMEM),
             scratch_shapes=[pltpu.SemaphoreType.DMA((OWNERS, 2))],
         ),
+        compiler_params=small(4),
         name="pick_pages",
     )(pages, keys, values)
 
@@ -146,6 +151,7 @@
         cost_estimate=pl.CostEstimate(
             flops=4 * 256 * 2176 * 256, transcendentals=2 * 256 * 2176, bytes_accessed=3_000_000
         ),
+        compiler_params=small(10),
         name="own_attention",
     )(low, high, order, seg_row, query, new_keys, new_values, code, keys, values)
 
@@ -184,7 +190,7 @@
         cost_estimate=pl.CostEstimate(
             flops=4 * 256 * 2048 * 256, transcendentals=2 * 256 * 2048, bytes_accessed=7_000_000
         ),
-        compiler_params=pltpu.CompilerParams(vmem_limit_bytes=24 * 1024 * 1024),
+        compiler_params=small(12),
         name="far_attention",
     )(low, high, query, code, pages, acc, total, w_out)
 
@@ -203,6 +209,44 @@
         c_ref[...].astype(F32) + d_ref[...].astype(F32)
     )
     out_ref[...] = (residual_ref[...] + rms_scale(total, post_ref[...])).astype(BF16)
+
+
+def mlp_kernel(rows_ref, gate_ref, up_ref, down_ref, gate2_ref, up2_ref, down2_ref, out_ref, hidden_ref):
+    rows = rows_ref[...]
+    units = gate_ref.shape[0]
+    last = (((1,), (1,)), ((), ()))
+    for i, (gate, up) in enumerate(((gate_ref, up_ref), (gate2_ref, up2_ref))):
+        gate_part = lax.dot_general(rows, gate[...], last, preferred_element_type=F32)
+        up_part = lax.dot_general(rows, up[...], last, preferred_element_type=F32)
+        hidden_ref[:, i * units:(i + 1) * units] = (
+            jax.nn.gelu(gate_part, approximate=True) * up_part
+        ).astype(BF16)
+    width = out_ref.shape[1]
+    for n in range(0, width, 512):
+        out_ref[:, n:n + 512] = (
+            jnp.dot(hidden_ref[:, :units], down_ref[:, n:n + 512], preferred_element_type=F32)
+            + jnp.dot(hidden_ref[:, units:], down2_ref[:, n:n + 512], preferred_element_type=F32)
+        ).astype(out_ref.dtype)
+
+
+def mlp(rows, weights, out_type):
+    count, width = rows.shape
+    units = weights[0].shape[0]
+    vmem = pl.BlockSpec(memory_space=pltpu.VMEM)
+    return pl.pallas_call(
+        mlp_kernel,
+        out_shape=jax.ShapeDtypeStruct((count, width), out_type),
+        in_specs=[vmem] * 7,
+        out_specs=vmem,
+        scratch_shapes=[pltpu.VMEM((count, 2 * units), BF16)],
+        cost_estimate=pl.CostEstimate(
+            flops=12 * count * width * units,
+            transcendentals=2 * count * units,
+            bytes_accessed=12 * units * width + 4 * count * width,
+        ),
+        compiler_params=small(20),
+        name="mlp",
+    )(rows, *weights)
 
 
 def local(
@@ -232,9 +276,10 @@
     packed = pick_pages(migrate_pages.reshape(-1), pooled_key_cache, pooled_value_cache)
     received = lax.all_to_all(packed, REQ, split_axis=0, concat_axis=0, tiled=True)
 
-    gate_sib = lax.ppermute(w_gate, "core", other)
-    up_sib = lax.ppermute(w_up, "core", other)
-    down_sib = lax.ppermute(w_down, "core", other)
+    gate, up = w_gate.T, w_up.T
+    weights = (gate, up, w_down) + tuple(
+        lax.ppermute(w, "core", other) for w in (gate, up, w_down)
+    )
 
     segment = segment_ids[0]
     past = past_len[0]
@@ -297,26 +342,19 @@
         ),
         in_specs=[vmem] * 7,
         out_specs=(vmem, vmem),
+        compiler_params=small(6),
         name="enter",
     )(own_rows, *parts, post_attn_gain[None, :], ffw_gain[None, :])
 
     line = jnp.concatenate([entering] + [shift(entering, True, k) for k in (1, 2, 3)], axis=0)
-    far = jnp.concatenate([shift(line, False, k) for k in (1, 2, 3)], axis=0)
-
-    def hidden_of(rows, gate, up):
-        gate_part = jnp.dot(rows, gate, preferred_element_type=F32)
-        up_part = jnp.dot(rows, up, preferred_element_type=F32)
-        return (jax.nn.gelu(gate_part, approximate=True) * up_part).astype(BF16)
-
-    def mlp(rows):
-        return jnp.dot(hidden_of(rows, w_gate, w_up), w_down, preferred_element_type=F32) + jnp.dot(
-            hidden_of(rows, gate_sib, up_sib), down_sib, preferred_element_type=F32
-        )
-
-    near_out = mlp(line)
-    far_out = mlp(far).astype(BF16)
+    near_out = mlp(line, weights, F32)
+    sides = jnp.concatenate([shift(line, False, k) for k in (1, 3)], axis=0)
+    line_later, near_out = lax.optimization_barrier((line, near_out))
+    across = shift(line_later, False, 2)
+    side_out = mlp(sides, weights, BF16)
+    across_out = mlp(across, weights, BF16)
     step = 4 * ROWS
-    back = [shift(far_out[(k - 1) * step:k * step], False, -k) for k in (1, 2, 3)]
+    back = [shift(side_out[:step], False, -1), shift(side_out[step:], False, -3), shift(across_out, False, -2)]
     line_out = near_out + sum(b.astype(F32) for b in back)
     line_out = line_out.astype(BF16)
     ends = [line_out[:ROWS]] + [
@@ -327,6 +365,7 @@
         out_shape=jax.ShapeDtypeStruct((ROWS, width), BF16),
         in_specs=[vmem] * 6,
         out_specs=vmem,
+        compiler_params=small(6),
         name="leave",
     )(residual, *ends, post_ffw_gain[None, :])
     return (mixed, incoming_keys, incoming_values)

time: 260 us -> 161 us (0.62); the launches traced: 257 us -> 160 us
  matrix products: 48.7 us -> 6.14 us
  Pallas kernels: 79.8 us -> 39.5 us
  waiting for transfers between devices: 82.2 us -> 61.8 us
  starting transfers between devices: 23.8 us -> 35.1 us
  local copies, waits for them, and re-layouts: 17.4 us -> 13.4 us
    pallas_call x1, Pallas kernels: 66 us -> 4.02 us  [pick_pages(): pl.pallas_call(pick_pages_kernel, out_shape=jax.ShapeDtypeStruct((OWNERS,...]
    dot_general x8 -> x0, matrix products: 43.5 us -> none  [the longest x2 17.9 us: mlp(): jnp.dot(hidden_of(rows, gate_sib, up_sib), down_sib, preferred_element_ty...]
    pallas_call x0 -> x3, Pallas kernels: none -> 27.7 us  [mlp(): pl.pallas_call(mlp_kernel, out_shape=jax.ShapeDtypeStruct((count, width),...]
    ppermute x12, waiting for transfers between devices: 61.3 us -> 35.7 us  [shift(): return lax.ppermute(value, REQ, chip_shift(first, k % 4))]
    ppermute x12, starting transfers between devices: 11.2 us -> 23.4 us  [shift(): return lax.ppermute(value, REQ, chip_shift(first, k % 4))]
    unnamed x59 -> x49, local copies, waits for them, and re-layouts: 6.7 us -> 11.7 us
    all_to_all x1, waiting for transfers between devices: 11.2 us -> 15 us  [local(): lax.all_to_all(packed, REQ, split_axis=0, concat_axis=0, tiled=True)]
    slice x1, local copies, waits for them, and re-layouts: 3.01 us -> 0.12 us  [local(): side_out[:step]]
  transfers between devices with their start and end apart: 19 -> 19, of which waited for: 11 -> 15; matrix products, arithmetic and copies ran while one was open for 16% -> 7% of each run, Pallas kernels for 4% -> 22%
where the time goes in v2:
time: 161 us; the launch traced here: 160 us
  waiting for transfers between devices  61.8 us (38%)
  Pallas kernels  39.5 us (25%)
  starting transfers between devices  35.1 us (22%)
  local copies, waits for them, and re-layouts  13.4 us (8%)
  matrix products  6.14 us (4%)
  other arithmetic  3.36 us (2%)
    ppermute x12, waiting for transfers between devices, shift(): return lax.ppermute(value, REQ, chip_shift(first, k % 4))  35.7 us
    pallas_call x3, Pallas kernels, mlp(): pl.pallas_call(mlp_kernel, out_shape=jax.ShapeDtypeStruct((count, width),...  27.7 us
    ppermute x12, starting transfers between devices, shift(): return lax.ppermute(value, REQ, chip_shift(first, k % 4))  23.4 us
    all_to_all x1, waiting for transfers between devices, local(): lax.all_to_all(packed, REQ, split_axis=0, concat_axis=0, tiled=True)  15 us
    unnamed x49, local copies, waits for them, and re-layouts  11.7 us
    ppermute x3, waiting for transfers between devices, local(): lax.ppermute(parts[k], 'mlp', [(i, (i + k) % 4) for i in range(4)])  11.1 us
    all_to_all x1, starting transfers between devices, local(): lax.all_to_all(packed, REQ, split_axis=0, concat_axis=0, tiled=True)  8.42 us
    pallas_call x1, Pallas kernels, far_attention(): pl.pallas_call(far_kernel, out_shape=jax.ShapeDtypeStruct((128, width), B...  4.19 us
  transfers between devices with their start and end apart: 19, of which 15 were waited for; matrix products, arithmetic and copies ran while one was open for 7% of the time, Pallas kernels for 22%

profile of v2, /device:TPU:16, one launch (start us, length us, event | category | flops | bytes accessed | tf_op | source)
XLA Modules:
  0.0 160.4 jit_solution(8343771843674231147)
XLA Ops:
  3.9 4.0 %pick_pages.1 = bf16[32,2,64,256]{3,2,1,0:T(8,128)(2,1)S(1)} custom-call(s32[32]{0:T(128)S(1)} %bitcast.34, bf16[32,64,256]{2,1,0:T(8,128)(2,1)S(1)} %copy-done.5, bf16[32,64,256]{2,1,0:T(8,128)(2,1)S(1)} %copy-done.7), custom_call_target="tpu_custom_call" | custom-call | tf_op jit(solution)/shard_map/pick_pages/pallas_call | solution.py:89
  9.3 8.4 %all-to-all-start = ((bf16[32,2,64,256]{3,2,1,0:T(8,128)(2,1)}), bf16[32,2,64,256]{3,2,1,0:T(8,128)(2,1)}, u32[]{:S(2)}, u32[]{:S(2)}) async-start(bf16[32,2,64,256]{3,2,1,0:T(8,128)(2,1)} %copy-done.4), calls=%async_computation | async-start | bytes 4194304 | tf_op jit(solution)/shard_map/all_to_all | solution.py:277
  18.7 1.5 fusion
  20.2 3.9 %fusion.26 = f32[128,512]{0,1:T(8,128)S(1)} fusion(bf16[3584,512]{1,0:T(8,128)(2,1)} %param.26, bf16[128,3584]{1,0:T(8,128)(2,1)} %param.18, f32[3584]{0:T(1024)S(1)} %copy-done.15, f32[128]{0:T(128)S(1)} %add_rsqrt_fusion), kind=kOutput, calls=%fused_computation.76 | convolution fusion | flops 471597056 | bytes 4864512 | tf_op jit(solution)/shard_map/dot_general | solution.py:289
  25.3 1.8 %convolution_bitcast_fusion = f32[128,1,256]{2,0,1:T(8,128)S(1)} fusion(bf16[3584,256]{1,0:T(8,128)(2,1)S(1)} %copy-done, bf16[128,3584]{1,0:T(8,128)(2,1)} %param.18, f32[3584]{0:T(1024)S(1)} %copy-done.15, f32[128]{0:T(128)S(1)} %add_rsqrt_fusion), kind=kOutput, calls=%fused_computation.7 | convolution fusion | flops 236716032 | bytes 2898432 | tf_op jit(solution)/shard_map/dot_general | solution.py:295
  29.4 2.2 %own_attention.1 = (f32[2,128,256]{2,1,0:T(8,128)S(1)}, f32[2,128,128]{2,1,0:T(8,128)S(1)}) custom-call(s32[128,1]{1,0:T(8,128)S(1)} %copy.37.low_ref, s32[128,1]{1,0:T(8,128)S(1)} %copy.38.high_ref, s32[128,1]{1,0:T(8,128)S(1)} %add_select_fusion.order_ref, s32[1,128]{1,0:T(1,128)S(1)} %copy-done.12, bf16[2,128,256]{2,1,0:T(8,128)(2,1)S(1)} %fusion.5.query_ref, ...), custom_call_target="tpu_custom_call" | custom-call | flops 570425344 | bytes 3000000 | tf_op jit(solution)/shard_map/own_attention/pallas_call | solution.py:143
  31.6 15.0 %all-to-all-done.pages_ref = bf16[32,2,64,256]{3,2,1,0:T(8,128)(2,1)} async-done(((bf16[32,2,64,256]{3,2,1,0:T(8,128)(2,1)}), bf16[32,2,64,256]{3,2,1,0:T(8,128)(2,1)}, u32[]{:S(2)}, u32[]{:S(2)}) %all-to-all-start) | async-done | bytes 2097184 | tf_op jit(solution)/shard_map/all_to_all | solution.py:277
  46.7 2.0 %copy-done.9 = bf16[512,3584]{1,0:T(8,128)(2,1)S(1)} copy-done((bf16[512,3584]{1,0:T(8,128)(2,1)S(1)}, bf16[512,3584]{1,0:T(8,128)(2,1)}, u32[]{:S(2)}) %copy-start.9) | copy-done | bytes 3670040
  48.7 4.2 %far_attention.1 = bf16[128,3584]{1,0:T(8,128)(2,1)S(1)} custom-call(s32[128,1]{1,0:T(8,128)S(1)} %copy.37.low_ref, s32[128,1]{1,0:T(8,128)S(1)} %copy.38.high_ref, bf16[2,128,256]{2,1,0:T(8,128)(2,1)S(1)} %fusion.5.query_ref, s32[1,2048]{1,0:T(1,128)S(1)} %get-tuple-element.36.code_ref, bf16[32,2,64,256]{3,2,1,0:T(8,128)(2,1)} %all-to-all-done.pages_ref, ...), custom_call_target="tpu_custom_call" | custom-call | flops 536870912 | bytes 7000000 | tf_op jit(solution)/shard_map/far_attention/pallas_call | solution.py:181
  55.1 6.5 %collective-permute-done.b_ref = bf16[32,3584]{1,0:T(8,128)(2,1)S(1)} collective-permute-done((bf16[32,3584]{1,0:T(8,128)(2,1)S(1)}, bf16[32,3584]{1,0:T(8,128)(2,1)S(1)}, u32[]{:S(2)}, u32[]{:S(2)}) %collective-permute-start) | collective-permute-done | bytes 229408 | tf_op jit(solution)/shard_map/ppermute | solution.py:335
  63.0 2.1 %collective-permute-done.1.c_ref = bf16[32,3584]{1,0:T(8,128)(2,1)S(1)} collective-permute-done((bf16[32,3584]{1,0:T(8,128)(2,1)S(1)}, bf16[32,3584]{1,0:T(8,128)(2,1)S(1)}, u32[]{:S(2)}, u32[]{:S(2)}) %collective-permute-start.1) | collective-permute-done | bytes 229408 | tf_op jit(solution)/shard_map/ppermute | solution.py:335
  65.1 2.5 %collective-permute-done.2.d_ref = bf16[32,3584]{1,0:T(8,128)(2,1)S(1)} collective-permute-done((bf16[32,3584]{1,0:T(8,128)(2,1)S(1)}, bf16[32,3584]{1,0:T(8,128)(2,1)S(1)}, u32[]{:S(2)}, u32[]{:S(2)}) %collective-permute-start.2) | collective-permute-done | bytes 229408 | tf_op jit(solution)/shard_map/ppermute | solution.py:335
  68.0 3.1 %collective-permute-start.3 = (bf16[32,3584]{1,0:T(8,128)(2,1)S(1)}, bf16[32,3584]{1,0:T(8,128)(2,1)S(1)}, u32[]{:S(2)}, u32[]{:S(2)}) collective-permute-start(bf16[32,3584]{1,0:T(8,128)(2,1)S(1)} %get-tuple-element.12), channel_id=1, source_target_pairs={{0,32},{4,12},{8,40},{12,20},{16,48},{20,28},{24,56},{28,4},{32,64... | collective-permute-start | bytes 688136 | tf_op jit(solution)/shard_map/ppermute | solution.py:69
  71.1 2.8 %collective-permute-start.4 = (bf16[32,3584]{1,0:T(8,128)(2,1)S(1)}, bf16[32,3584]{1,0:T(8,128)(2,1)S(1)}, u32[]{:S(2)}, u32[]{:S(2)}) collective-permute-start(bf16[32,3584]{1,0:T(8,128)(2,1)S(1)} %get-tuple-element.12), channel_id=1, source_target_pairs={{0,64},{4,20},{8,72},{12,28},{16,80},{20,4},{24,88},{28,12},{32,96... | collective-permute-start | bytes 688136 | tf_op jit(solution)/shard_map/ppermute | solution.py:69
  74.0 2.5 %collective-permute-done.3 = bf16[32,3584]{1,0:T(8,128)(2,1)S(1)} collective-permute-done((bf16[32,3584]{1,0:T(8,128)(2,1)S(1)}, bf16[32,3584]{1,0:T(8,128)(2,1)S(1)}, u32[]{:S(2)}, u32[]{:S(2)}) %collective-permute-start.3) | collective-permute-done | bytes 229408 | tf_op jit(solution)/shard_map/ppermute | solution.py:69
  76.5 2.0 %collective-permute-start.5 = (bf16[32,3584]{1,0:T(8,128)(2,1)S(1)}, bf16[32,3584]{1,0:T(8,128)(2,1)S(1)}, u32[]{:S(2)}, u32[]{:S(2)}) collective-permute-start(bf16[32,3584]{1,0:T(8,128)(2,1)S(1)} %get-tuple-element.12), channel_id=1, source_target_pairs={{0,96},{4,28},{8,104},{12,4},{16,112},{20,12},{24,120},{28,20},{32... | collective-permute-start | bytes 688136 | tf_op jit(solution)/shard_map/ppermute | solution.py:69
  78.5 1.9 %collective-permute-done.4 = bf16[32,3584]{1,0:T(8,128)(2,1)S(1)} collective-permute-done((bf16[32,3584]{1,0:T(8,128)(2,1)S(1)}, bf16[32,3584]{1,0:T(8,128)(2,1)S(1)}, u32[]{:S(2)}, u32[]{:S(2)}) %collective-permute-start.4) | collective-permute-done | bytes 229408 | tf_op jit(solution)/shard_map/ppermute | solution.py:69
  80.4 3.6 %collective-permute-done.5 = bf16[32,3584]{1,0:T(8,128)(2,1)S(1)} collective-permute-done((bf16[32,3584]{1,0:T(8,128)(2,1)S(1)}, bf16[32,3584]{1,0:T(8,128)(2,1)S(1)}, u32[]{:S(2)}, u32[]{:S(2)}) %collective-permute-start.5) | collective-permute-done | bytes 229408 | tf_op jit(solution)/shard_map/ppermute | solution.py:69
  84.0 7.2 %collective-permute-start.10 = (bf16[128,3584]{1,0:T(8,128)(2,1)S(1)}, bf16[128,3584]{1,0:T(8,128)(2,1)S(1)}, u32[]{:S(2)}, u32[]{:S(2)}) collective-permute-start(bf16[128,3584]{1,0:T(8,128)(2,1)S(1)} %constant_dynamic-update-slice_fusion.rows_ref), channel_id=1, source_target_pairs={{0,24},{4,100},{8,0},{12,108},{16,8},{20,116},{24,16},{28,124},{32... | collective-permute-start | bytes 2752520 | tf_op jit(solution)/shard_map/ppermute | solution.py:69
  91.3 1.9 %copy-done.2 = bf16[3584,448]{0,1:T(8,128)(2,1)S(1)} copy-done((bf16[3584,448]{0,1:T(8,128)(2,1)S(1)}, bf16[3584,448]{0,1:T(8,128)(2,1)}, u32[]{:S(2)}) %copy-start.2) | copy-done | bytes 3211288
  93.2 1.9 %copy-done.3 = bf16[448,3584]{1,0:T(8,128)(2,1)S(1)} copy-done((bf16[448,3584]{1,0:T(8,128)(2,1)S(1)}, bf16[448,3584]{1,0:T(8,128)(2,1)}, u32[]{:S(2)}) %copy-start.3) | copy-done | bytes 3211288
  95.1 8.8 %mlp.3 = f32[128,3584]{1,0:T(8,128)S(1)} custom-call(bf16[128,3584]{1,0:T(8,128)(2,1)S(1)} %constant_dynamic-update-slice_fusion.rows_ref, bf16[448,3584]{1,0:T(8,128)(2,1)S(1)} %bitcast.25, bf16[448,3584]{1,0:T(8,128)(2,1)S(1)} %bitcast.29, bf16[448,3584]{1,0:T(8,128)(2,1)S(1)} %copy-done.3, bf16[448,3584]{1,0:T(8,128)(2,1)} %collective-permute-done.6.gate2_ref, ...), custom_call_target="tpu_custom_call" | custom-call | flops 2466250752 | bytes 21102592 | tf_op jit(solution)/shard_map/mlp/pallas_call | solution.py:236
  103.9 1.6 %collective-permute-start.13 = (bf16[128,3584]{1,0:T(8,128)(2,1)S(1)}, bf16[128,3584]{1,0:T(8,128)(2,1)S(1)}, u32[]{:S(2)}, u32[]{:S(2)}) collective-permute-start(bf16[128,3584]{1,0:T(8,128)(2,1)S(1)} %constant_dynamic-update-slice_fusion.rows_ref), channel_id=1, source_target_pairs={{0,16},{4,68},{8,24},{12,76},{16,0},{20,84},{24,8},{28,92},{32,48}... | collective-permute-start | bytes 2752520 | tf_op jit(solution)/shard_map/ppermute | solution.py:69
  106.0 10.0 %mlp.4 = bf16[256,3584]{1,0:T(8,128)(2,1)S(1)} custom-call(bf16[256,3584]{1,0:T(8,128)(2,1)S(1)} %pad_maximum_fusion.rows_ref, bf16[448,3584]{1,0:T(8,128)(2,1)S(1)} %bitcast.26, bf16[448,3584]{1,0:T(8,128)(2,1)S(1)} %bitcast.30, bf16[448,3584]{1,0:T(8,128)(2,1)S(1)} %copy-done.3, bf16[448,3584]{1,0:T(8,128)(2,1)} %collective-permute-done.6.gate2_ref, ...), custom_call_target="tpu_custom_call" | custom-call | flops 4932501504 | bytes 22937600 | tf_op jit(solution)/shard_map/mlp/pallas_call | solution.py:236
  116.2 1.6 collective-permute-start.11
  118.9 8.8 %mlp.5 = bf16[128,3584]{1,0:T(8,128)(2,1)S(1)} custom-call(bf16[128,3584]{1,0:T(8,128)(2,1)S(1)} %collective-permute-done.13.rows_ref, bf16[448,3584]{1,0:T(8,128)(2,1)S(1)} %bitcast.27, bf16[448,3584]{1,0:T(8,128)(2,1)S(1)} %bitcast.31, bf16[448,3584]{1,0:T(8,128)(2,1)S(1)} %copy-done.3, bf16[448,3584]{1,0:T(8,128)(2,1)} %collective-permute-done.6.gate2_ref, ...), custom_call_target="tpu_custom_call" | custom-call | flops 2466250752 | bytes 21102592 | tf_op jit(solution)/shard_map/mlp/pallas_call | solution.py:236
  127.7 1.7 %collective-permute-start.14 = (bf16[128,3584]{1,0:T(8,128)(2,1)S(1)}, bf16[128,3584]{1,0:T(8,128)(2,1)S(1)}, u32[]{:S(2)}, u32[]{:S(2)}) collective-permute-start(bf16[128,3584]{1,0:T(8,128)(2,1)S(1)} %mlp.5), channel_id=1, source_target_pairs={{0,16},{4,68},{8,24},{12,76},{16,0},{20,84},{24,8},{28,92},{32,48}... | collective-permute-start | bytes 2752520 | tf_op jit(solution)/shard_map/ppermute | solution.py:69
  129.8 2.5 %collective-permute-done.12 = bf16[128,3584]{1,0:T(8,128)(2,1)S(1)} collective-permute-done((bf16[128,3584]{1,0:T(8,128)(2,1)S(1)}, bf16[128,3584]{1,0:T(8,128)(2,1)S(1)}, u32[]{:S(2)}, u32[]{:S(2)}) %collective-permute-start.12) | collective-permute-done | bytes 917536 | tf_op jit(solution)/shard_map/ppermute | solution.py:69
  132.3 15.3 %collective-permute-done.14 = bf16[128,3584]{1,0:T(8,128)(2,1)S(1)} collective-permute-done((bf16[128,3584]{1,0:T(8,128)(2,1)S(1)}, bf16[128,3584]{1,0:T(8,128)(2,1)S(1)}, u32[]{:S(2)}, u32[]{:S(2)}) %collective-permute-start.14) | collective-permute-done | bytes 917536 | tf_op jit(solution)/shard_map/ppermute | solution.py:69
  150.4 3.8 %collective-permute-done.15.b_ref = bf16[32,3584]{1,0:T(8,128)(2,1)S(1)} collective-permute-done((bf16[32,3584]{1,0:T(8,128)(2,1)S(1)}, bf16[32,3584]{1,0:T(8,128)(2,1)S(1)}, u32[]{:S(2)}, u32[]{:S(2)}) %collective-permute-start.15) | collective-permute-done | bytes 229408 | tf_op jit(solution)/shard_map/ppermute | solution.py:69
  154.2 2.8 %collective-permute-done.16.c_ref = bf16[32,3584]{1,0:T(8,128)(2,1)S(1)} collective-permute-done((bf16[32,3584]{1,0:T(8,128)(2,1)S(1)}, bf16[32,3584]{1,0:T(8,128)(2,1)S(1)}, u32[]{:S(2)}, u32[]{:S(2)}) %collective-permute-start.16) | collective-permute-done | bytes 229408 | tf_op jit(solution)/shard_map/ppermute | solution.py:69
  157.1 2.4 %collective-permute-done.17.d_ref = bf16[32,3584]{1,0:T(8,128)(2,1)S(1)} collective-permute-done((bf16[32,3584]{1,0:T(8,128)(2,1)S(1)}, bf16[32,3584]{1,0:T(8,128)(2,1)S(1)}, u32[]{:S(2)}, u32[]{:S(2)}) %collective-permute-start.17) | collective-permute-done | bytes 229408 | tf_op jit(solution)/shard_map/ppermute | solution.py:69
  (101 shorter events, 18.7 us)
Async XLA Ops:
  0.6 24.6 %copy-start = (bf16[3584,256]{1,0:T(8,128)(2,1)S(1)}, bf16[3584,256]{1,0:T(8,128)(2,1)}, u32[]{:S(2)}) copy-start(bf16[3584,256]{1,0:T(8,128)(2,1)} %param.27) | copy-start | bytes 5505028
  9.3 9.2 %copy-start.12 = (s32[1,128]{1,0:T(1,128)S(1)}, s32[1,128]{1,0:T(1,128)}, u32[]{:S(2)}) copy-start(s32[1,128]{1,0:T(1,128)} %seg_row_ref.1) | copy-start | bytes 1540
  9.3 10.8 %copy-start.15 = (f32[3584]{0:T(1024)S(1)}, f32[3584]{0:T(1024)}, u32[]{:S(2)}) copy-start(f32[3584]{0:T(1024)} %param.25) | copy-start | bytes 43012
  9.3 37.3 %all-to-all-start = ((bf16[32,2,64,256]{3,2,1,0:T(8,128)(2,1)}), bf16[32,2,64,256]{3,2,1,0:T(8,128)(2,1)}, u32[]{:S(2)}, u32[]{:S(2)}) async-start(bf16[32,2,64,256]{3,2,1,0:T(8,128)(2,1)} %copy-done.4), calls=%async_computation | async-start | bytes 4194304 | tf_op jit(solution)/shard_map/all_to_all | solution.py:277
  17.7 73.5 %collective-permute-start.6 = (bf16[448,3584]{1,0:T(8,128)(2,1)}, bf16[448,3584]{1,0:T(8,128)(2,1)}, u32[]{:S(2)}, u32[]{:S(2)}) collective-permute-start(bf16[448,3584]{1,0:T(8,128)(2,1)} %bitcast.24), channel_id=1, source_target_pairs={{0,4},{4,0},{1,5},{5,1},{2,6},{6,2},{3,7},{7,3},{8,12},{12,8},{9,1... | collective-permute-start | bytes 9633800 | tf_op jit(solution)/shard_map/ppermute | solution.py:281
  18.0 73.2 %collective-permute-start.7 = (bf16[448,3584]{1,0:T(8,128)(2,1)}, bf16[448,3584]{1,0:T(8,128)(2,1)}, u32[]{:S(2)}, u32[]{:S(2)}) collective-permute-start(bf16[448,3584]{1,0:T(8,128)(2,1)} %bitcast.28), channel_id=1, source_target_pairs={{0,4},{4,0},{1,5},{5,1},{2,6},{6,2},{3,7},{7,3},{8,12},{12,8},{9,1... | collective-permute-start | bytes 9633800 | tf_op jit(solution)/shard_map/ppermute | solution.py:281
  18.3 72.9 %collective-permute-start.8 = (bf16[448,3584]{1,0:T(8,128)(2,1)}, bf16[448,3584]{1,0:T(8,128)(2,1)}, u32[]{:S(2)}, u32[]{:S(2)}) collective-permute-start(bf16[448,3584]{1,0:T(8,128)(2,1)} %down_ref.5), channel_id=1, source_target_pairs={{0,4},{4,0},{1,5},{5,1},{2,6},{6,2},{3,7},{7,3},{8,12},{12,8},{9,1... | collective-permute-start | bytes 9633800 | tf_op jit(solution)/shard_map/ppermute | solution.py:281
  20.1 4.0 %copy-start.21 = (s32[1,64]{1,0:T(1,128)S(1)}, s32[1,64]{1,0:T(1,128)}, u32[]{:S(2)}) copy-start(s32[1,64]{1,0:T(1,128)} %param.21) | copy-start | bytes 772
  20.1 4.1 %copy-start.19 = (s32[1,4]{1,0:T(1,128)S(1)}, s32[1,4]{1,0:T(1,128)}, u32[]{:S(2)}) copy-start(s32[1,4]{1,0:T(1,128)} %param.20) | copy-start | bytes 52
  25.3 2.7 %copy-start.14 = (bf16[128,3584]{1,0:T(8,128)(2,1)S(1)}, bf16[128,3584]{1,0:T(8,128)(2,1)}, u32[]{:S(2)}) copy-start(bf16[128,3584]{1,0:T(8,128)(2,1)} %param.18) | copy-start | bytes 2752516
  25.3 2.7 %copy-start.20 = (bf16[3584,256]{1,0:T(8,128)(2,1)S(1)}, bf16[3584,256]{1,0:T(8,128)(2,1)}, u32[]{:S(2)}) copy-start(bf16[3584,256]{1,0:T(8,128)(2,1)} %param.28) | copy-start | bytes 5505028
  28.5 24.4 %copy-start.11 = (bf16[128,256]{1,0:T(8,128)(2,1)}, bf16[128,256]{1,0:T(8,128)(2,1)S(1)}, u32[]{:S(2)}) copy-start(bf16[128,256]{1,0:T(8,128)(2,1)S(1)} %convolution_convert_fusion.new_values_ref) | copy-start | bytes 196612
  46.7 2.0 %copy-start.9 = (bf16[512,3584]{1,0:T(8,128)(2,1)S(1)}, bf16[512,3584]{1,0:T(8,128)(2,1)}, u32[]{:S(2)}) copy-start(bf16[512,3584]{1,0:T(8,128)(2,1)} %w_ref.1) | copy-start | bytes 11010052
  53.0 8.6 %collective-permute-start = (bf16[32,3584]{1,0:T(8,128)(2,1)S(1)}, bf16[32,3584]{1,0:T(8,128)(2,1)S(1)}, u32[]{:S(2)}, u32[]{:S(2)}) collective-permute-start(bf16[32,3584]{1,0:T(8,128)(2,1)S(1)} %get-tuple-element.27), channel_id=1, source_target_pairs={{0,1},{1,2},{2,3},{3,0},{4,5},{5,6},{6,7},{7,4},{8,9},{9,10},{10,1... | collective-permute-start | bytes 688136 | tf_op jit(solution)/shard_map/ppermute | solution.py:335
  54.3 36.9 %copy-start.1 = (bf16[3584,448]{0,1:T(8,128)(2,1)S(1)}, bf16[3584,448]{0,1:T(8,128)(2,1)}, u32[]{:S(2)}) copy-start(bf16[3584,448]{0,1:T(8,128)(2,1)} %param.32) | copy-start | bytes 9633796
  54.4 10.7 %collective-permute-start.1 = (bf16[32,3584]{1,0:T(8,128)(2,1)S(1)}, bf16[32,3584]{1,0:T(8,128)(2,1)S(1)}, u32[]{:S(2)}, u32[]{:S(2)}) collective-permute-start(bf16[32,3584]{1,0:T(8,128)(2,1)S(1)} %get-tuple-element.26), channel_id=1, source_target_pairs={{0,2},{1,3},{2,0},{3,1},{4,6},{5,7},{6,4},{7,5},{8,10},{9,11},{10,... | collective-permute-start | bytes 688136 | tf_op jit(solution)/shard_map/ppermute | solution.py:335
  61.6 6.0 %collective-permute-start.2 = (bf16[32,3584]{1,0:T(8,128)(2,1)S(1)}, bf16[32,3584]{1,0:T(8,128)(2,1)S(1)}, u32[]{:S(2)}, u32[]{:S(2)}) collective-permute-start(bf16[32,3584]{1,0:T(8,128)(2,1)S(1)} %get-tuple-element.25), channel_id=1, source_target_pairs={{0,3},{1,0},{2,1},{3,2},{4,7},{5,4},{6,5},{7,6},{8,11},{9,8},{10,9... | collective-permute-start | bytes 688136 | tf_op jit(solution)/shard_map/ppermute | solution.py:335
  68.0 8.5 %collective-permute-start.3 = (bf16[32,3584]{1,0:T(8,128)(2,1)S(1)}, bf16[32,3584]{1,0:T(8,128)(2,1)S(1)}, u32[]{:S(2)}, u32[]{:S(2)}) collective-permute-start(bf16[32,3584]{1,0:T(8,128)(2,1)S(1)} %get-tuple-element.12), channel_id=1, source_target_pairs={{0,32},{4,12},{8,40},{12,20},{16,48},{20,28},{24,56},{28,4},{32,64... | collective-permute-start | bytes 688136 | tf_op jit(solution)/shard_map/ppermute | solution.py:69
  71.1 9.3 %collective-permute-start.4 = (bf16[32,3584]{1,0:T(8,128)(2,1)S(1)}, bf16[32,3584]{1,0:T(8,128)(2,1)S(1)}, u32[]{:S(2)}, u32[]{:S(2)}) collective-permute-start(bf16[32,3584]{1,0:T(8,128)(2,1)S(1)} %get-tuple-element.12), channel_id=1, source_target_pairs={{0,64},{4,20},{8,72},{12,28},{16,80},{20,4},{24,88},{28,12},{32,96... | collective-permute-start | bytes 688136 | tf_op jit(solution)/shard_map/ppermute | solution.py:69
  76.5 7.5 %collective-permute-start.5 = (bf16[32,3584]{1,0:T(8,128)(2,1)S(1)}, bf16[32,3584]{1,0:T(8,128)(2,1)S(1)}, u32[]{:S(2)}, u32[]{:S(2)}) collective-permute-start(bf16[32,3584]{1,0:T(8,128)(2,1)S(1)} %get-tuple-element.12), channel_id=1, source_target_pairs={{0,96},{4,28},{8,104},{12,4},{16,112},{20,12},{24,120},{28,20},{32... | collective-permute-start | bytes 688136 | tf_op jit(solution)/shard_map/ppermute | solution.py:69
  84.0 21.5 %collective-permute-start.10 = (bf16[128,3584]{1,0:T(8,128)(2,1)S(1)}, bf16[128,3584]{1,0:T(8,128)(2,1)S(1)}, u32[]{:S(2)}, u32[]{:S(2)}) collective-permute-start(bf16[128,3584]{1,0:T(8,128)(2,1)S(1)} %constant_dynamic-update-slice_fusion.rows_ref), channel_id=1, source_target_pairs={{0,24},{4,100},{8,0},{12,108},{16,8},{20,116},{24,16},{28,124},{32... | collective-permute-start | bytes 2752520 | tf_op jit(solution)/shard_map/ppermute | solution.py:69
  91.2 14.6 %collective-permute-start.9 = (bf16[128,3584]{1,0:T(8,128)(2,1)S(1)}, bf16[128,3584]{1,0:T(8,128)(2,1)S(1)}, u32[]{:S(2)}, u32[]{:S(2)}) collective-permute-start(bf16[128,3584]{1,0:T(8,128)(2,1)S(1)} %constant_dynamic-update-slice_fusion.rows_ref), channel_id=1, source_target_pairs={{0,8},{4,36},{8,16},{12,44},{16,24},{20,52},{24,0},{28,60},{32,40}... | collective-permute-start | bytes 2752520 | tf_op jit(solution)/shard_map/ppermute | solution.py:69
  91.3 1.9 %copy-start.2 = (bf16[3584,448]{0,1:T(8,128)(2,1)S(1)}, bf16[3584,448]{0,1:T(8,128)(2,1)}, u32[]{:S(2)}) copy-start(bf16[3584,448]{0,1:T(8,128)(2,1)} %param.33) | copy-start | bytes 9633796
  93.2 1.9 %copy-start.3 = (bf16[448,3584]{1,0:T(8,128)(2,1)S(1)}, bf16[448,3584]{1,0:T(8,128)(2,1)}, u32[]{:S(2)}) copy-start(bf16[448,3584]{1,0:T(8,128)(2,1)} %down_ref.5) | copy-start | bytes 9633796
  103.9 15.0 %collective-permute-start.13 = (bf16[128,3584]{1,0:T(8,128)(2,1)S(1)}, bf16[128,3584]{1,0:T(8,128)(2,1)S(1)}, u32[]{:S(2)}, u32[]{:S(2)}) collective-permute-start(bf16[128,3584]{1,0:T(8,128)(2,1)S(1)} %constant_dynamic-update-slice_fusion.rows_ref), channel_id=1, source_target_pairs={{0,16},{4,68},{8,24},{12,76},{16,0},{20,84},{24,8},{28,92},{32,48}... | collective-permute-start | bytes 2752520 | tf_op jit(solution)/shard_map/ppermute | solution.py:69
  116.2 13.7 %collective-permute-start.11 = (bf16[128,3584]{1,0:T(8,128)(2,1)S(1)}, bf16[128,3584]{1,0:T(8,128)(2,1)S(1)}, u32[]{:S(2)}, u32[]{:S(2)}) collective-permute-start(bf16[128,3584]{1,0:T(8,128)(2,1)S(1)} %get-tuple-element.19), channel_id=1, source_target_pairs={{0,24},{4,100},{8,0},{12,108},{16,8},{20,116},{24,16},{28,124},{32... | collective-permute-start | bytes 2752520 | tf_op jit(solution)/shard_map/ppermute | solution.py:69
  117.7 14.6 %collective-permute-start.12 = (bf16[128,3584]{1,0:T(8,128)(2,1)S(1)}, bf16[128,3584]{1,0:T(8,128)(2,1)S(1)}, u32[]{:S(2)}, u32[]{:S(2)}) collective-permute-start(bf16[128,3584]{1,0:T(8,128)(2,1)S(1)} %get-tuple-element.20), channel_id=1, source_target_pairs={{0,8},{4,36},{8,16},{12,44},{16,24},{20,52},{24,0},{28,60},{32,40}... | collective-permute-start | bytes 2752520 | tf_op jit(solution)/shard_map/ppermute | solution.py:69
  127.7 19.9 %collective-permute-start.14 = (bf16[128,3584]{1,0:T(8,128)(2,1)S(1)}, bf16[128,3584]{1,0:T(8,128)(2,1)S(1)}, u32[]{:S(2)}, u32[]{:S(2)}) collective-permute-start(bf16[128,3584]{1,0:T(8,128)(2,1)S(1)} %mlp.5), channel_id=1, source_target_pairs={{0,16},{4,68},{8,24},{12,76},{16,0},{20,84},{24,8},{28,92},{32,48}... | collective-permute-start | bytes 2752520 | tf_op jit(solution)/shard_map/ppermute | solution.py:69
  148.1 2.3 %copy-start.18 = (f32[3584]{0:T(1024)S(1)}, f32[3584]{0:T(1024)}, u32[]{:S(2)}) copy-start(f32[3584]{0:T(1024)} %param.35) | copy-start | bytes 43012
  148.2 6.1 %collective-permute-start.15 = (bf16[32,3584]{1,0:T(8,128)(2,1)S(1)}, bf16[32,3584]{1,0:T(8,128)(2,1)S(1)}, u32[]{:S(2)}, u32[]{:S(2)}) collective-permute-start(bf16[32,3584]{1,0:T(8,128)(2,1)S(1)} %get-tuple-element.23), channel_id=1, source_target_pairs={{0,96},{4,28},{8,104},{12,4},{16,112},{20,12},{24,120},{28,20},{32... | collective-permute-start | bytes 688136 | tf_op jit(solution)/shard_map/ppermute | solution.py:69
  149.4 7.6 %collective-permute-start.16 = (bf16[32,3584]{1,0:T(8,128)(2,1)S(1)}, bf16[32,3584]{1,0:T(8,128)(2,1)S(1)}, u32[]{:S(2)}, u32[]{:S(2)}) collective-permute-start(bf16[32,3584]{1,0:T(8,128)(2,1)S(1)} %get-tuple-element.22), channel_id=1, source_target_pairs={{0,64},{4,20},{8,72},{12,28},{16,80},{20,4},{24,88},{28,12},{32,96... | collective-permute-start | bytes 688136 | tf_op jit(solution)/shard_map/ppermute | solution.py:69
  149.8 9.6 %collective-permute-start.17 = (bf16[32,3584]{1,0:T(8,128)(2,1)S(1)}, bf16[32,3584]{1,0:T(8,128)(2,1)S(1)}, u32[]{:S(2)}, u32[]{:S(2)}) collective-permute-start(bf16[32,3584]{1,0:T(8,128)(2,1)S(1)} %get-tuple-element.21), channel_id=1, source_target_pairs={{0,32},{4,12},{8,40},{12,20},{16,48},{20,28},{24,56},{28,4},{32,64... | collective-permute-start | bytes 688136 | tf_op jit(solution)/shard_map/ppermute | solution.py:69
  (9 other events, 11.3 us)

commit v3 on v2

--- a/solution.py
+++ b/solution.py
@@ -17,6 +17,9 @@
 SOFT_CAP = 50.0
 NORM_EPS = 1e-06
 ROPE_BASE = 10000.0
+MLP_MIB = 8
+LOAD_MIB = 40
+FAR_MIB = 58
 
 BF16 = jnp.bfloat16
 F32 = jnp.float32
@@ -73,32 +76,76 @@
     return pltpu.CompilerParams(vmem_limit_bytes=megabytes * 1024 * 1024)
 
 
-def pick_pages_kernel(pages_ref, keys_ref, values_ref, out_ref, sems):
-    copies = []
+def pick_pages_kernel(pages_ref, keys_ref, values_ref, out_ref, held_ref, in_sems, out_sems):
+    loads = []
     for d in range(OWNERS):
         page = pages_ref[d]
-        copies.append(pltpu.make_async_copy(keys_ref.at[page], out_ref.at[d, 0], sems.at[d, 0]))
-        copies.append(pltpu.make_async_copy(values_ref.at[page], out_ref.at[d, 1], sems.at[d, 1]))
-    for copy in copies:
-        copy.start()
-    for copy in copies:
-        copy.wait()
+        loads.append((
+            pltpu.make_async_copy(keys_ref.at[page], held_ref.at[d, 0], in_sems.at[d, 0]),
+            pltpu.make_async_copy(values_ref.at[page], held_ref.at[d, 1], in_sems.at[d, 1]),
+        ))
+        for load in loads[d]:
+            load.start()
+    stores = []
+    for d in range(0, OWNERS, 4):
+        for e in range(d, d + 4):
+            for load in loads[e]:
+                load.wait()
+        stores.append(
+            pltpu.make_async_copy(held_ref.at[d:d + 4], out_ref.at[d:d + 4], out_sems.at[d // 4])
+        )
+        stores[-1].start()
+    for store in stores:
+        store.wait()
 
 
 def pick_pages(pages, keys, values):
+    hbm = pl.BlockSpec(memory_space=pltpu.HBM)
     return pl.pallas_call(
         pick_pages_kernel,
         out_shape=jax.ShapeDtypeStruct((OWNERS, 2, PAGE, HEAD_SIZE), BF16),
         grid_spec=pltpu.PrefetchScalarGridSpec(
             num_scalar_prefetch=1,
             grid=(),
-            in_specs=[pl.BlockSpec(memory_space=pl.ANY)] * 2,
-            out_specs=pl.BlockSpec(memory_space=pltpu.VMEM),
-            scratch_shapes=[pltpu.SemaphoreType.DMA((OWNERS, 2))],
-        ),
-        compiler_params=small(4),
+            in_specs=[hbm] * 2,
+            out_specs=hbm,
+            scratch_shapes=[
+                pltpu.VMEM((OWNERS, 2, PAGE, HEAD_SIZE), BF16),
+                pltpu.SemaphoreType.DMA((OWNERS, 2)),
+                pltpu.SemaphoreType.DMA((OWNERS // 4,)),
+            ],
+        ),
+        compiler_params=small(56),
         name="pick_pages",
     )(pages, keys, values)
+
+
+def load_kernel(*refs):
+    *weights, out_ref, sems = refs
+    copies = [
+        pltpu.make_async_copy(w, out_ref.at[i], sems.at[i]) for i, w in enumerate(weights)
+    ]
+    for copy in copies:
+        copy.start()
+    for copy in copies:
+        copy.wait()
+
+
+def load_weights(weights):
+    units, width = weights[0].shape
+    count = len(weights)
+    return pl.pallas_call(
+        load_kernel,
+        out_shape=pltpu.VMEM((count, units, width), BF16),
+        in_specs=[pl.BlockSpec(memory_space=pltpu.HBM)] * count,
+        out_specs=pl.BlockSpec(memory_space=pltpu.VMEM),
+        scratch_shapes=[pltpu.SemaphoreType.DMA((count,))],
+        cost_estimate=pl.CostEstimate(
+            flops=0, transcendentals=0, bytes_accessed=2 * count * units * width
+        ),
+        compiler_params=small(LOAD_MIB),
+        name="load_weights",
+    )(*weights)
 
 
 def weights_of(query, keys, visible):
@@ -156,43 +203,60 @@
     )(low, high, order, seg_row, query, new_keys, new_values, code, keys, values)
 
 
-def far_kernel(low_ref, high_ref, query_ref, code_ref, pages_ref, acc_in_ref, total_in_ref, w_ref,
-               out_ref, acc_ref, total_ref):
+def far_kernel(low_ref, high_ref, query_ref, code_ref, acc_in_ref, total_in_ref, pages_ref, w_ref,
+               out_ref, acc_ref, total_ref, held_ref, w_held_ref, page_sems, w_sem):
+    loads = [
+        pltpu.make_async_copy(
+            pages_ref.at[b * STEP_PAGES:(b + 1) * STEP_PAGES], held_ref.at[b], page_sems.at[b]
+        )
+        for b in range(OWNERS // STEP_PAGES)
+    ]
+    for load in loads:
+        load.start()
+    w_load = pltpu.make_async_copy(w_ref, w_held_ref, w_sem)
+    w_load.start()
     acc_ref[...] = acc_in_ref[...]
     total_ref[...] = total_in_ref[...]
     low, high = low_ref[...], high_ref[...]
     for b in range(OWNERS // STEP_PAGES):
-        keys = pages_ref[b * STEP_PAGES:(b + 1) * STEP_PAGES, 0].reshape(STEP, HEAD_SIZE)
-        values = pages_ref[b * STEP_PAGES:(b + 1) * STEP_PAGES, 1].reshape(STEP, HEAD_SIZE)
+        loads[b].wait()
+        keys = held_ref[b, :, 0].reshape(STEP, HEAD_SIZE)
+        values = held_ref[b, :, 1].reshape(STEP, HEAD_SIZE)
         code = code_ref[:, b * STEP:(b + 1) * STEP]
         attend(query_ref, keys, values, (code > low) & (code < high), acc_ref, total_ref)
     heads = [(acc_ref[h] / total_ref[h][:, :1]).astype(BF16) for h in range(HEADS)]
     attention = jnp.concatenate(heads, axis=1)
     width = out_ref.shape[1]
+    w_load.wait()
     for n in range(0, width, 512):
         out_ref[:, n:n + 512] = jnp.dot(
-            attention, w_ref[:, n:n + 512], preferred_element_type=F32
+            attention, w_held_ref[:, n:n + 512], preferred_element_type=F32
         ).astype(BF16)
 
 
-def far_attention(low, high, query, code, pages, acc, total, w_out):
+def far_attention(low, high, query, code, acc, total, pages, w_out):
     vmem = pl.BlockSpec(memory_space=pltpu.VMEM)
+    hbm = pl.BlockSpec(memory_space=pltpu.HBM)
     width = w_out.shape[1]
     return pl.pallas_call(
         far_kernel,
         out_shape=jax.ShapeDtypeStruct((128, width), BF16),
-        in_specs=[vmem] * 8,
+        in_specs=[vmem] * 6 + [hbm] * 2,
         out_specs=vmem,
         scratch_shapes=[
             pltpu.VMEM((HEADS, 128, HEAD_SIZE), F32),
             pltpu.VMEM((HEADS, 128, 128), F32),
+            pltpu.VMEM((OWNERS // STEP_PAGES, STEP_PAGES, 2, PAGE, HEAD_SIZE), BF16),
+            pltpu.VMEM(w_out.shape, BF16),
+            pltpu.SemaphoreType.DMA((OWNERS // STEP_PAGES,)),
+            pltpu.SemaphoreType.DMA,
         ],
         cost_estimate=pl.CostEstimate(
             flops=4 * 256 * 2048 * 256, transcendentals=2 * 256 * 2048, bytes_accessed=7_000_000
         ),
-        compiler_params=small(12),
+        compiler_params=small(FAR_MIB),
         name="far_attention",
-    )(low, high, query, code, pages, acc, total, w_out)
+    )(low, high, query, code, acc, total, pages, w_out)
 
 
 def enter_kernel(own_ref, a_ref, b_ref, c_ref, d_ref, post_ref, ffw_ref, residual_ref, out_ref):
@@ -211,42 +275,44 @@
     out_ref[...] = (residual_ref[...] + rms_scale(total, post_ref[...])).astype(BF16)
 
 
-def mlp_kernel(rows_ref, gate_ref, up_ref, down_ref, gate2_ref, up2_ref, down2_ref, out_ref, hidden_ref):
+def mlp_kernel(rows_ref, weights_ref, out_ref, hidden_ref):
     rows = rows_ref[...]
-    units = gate_ref.shape[0]
+    units = weights_ref.shape[1]
     last = (((1,), (1,)), ((), ()))
-    for i, (gate, up) in enumerate(((gate_ref, up_ref), (gate2_ref, up2_ref))):
-        gate_part = lax.dot_general(rows, gate[...], last, preferred_element_type=F32)
-        up_part = lax.dot_general(rows, up[...], last, preferred_element_type=F32)
+    for i in range(2):
+        gate_part = lax.dot_general(rows, weights_ref[3 * i], last, preferred_element_type=F32)
+        up_part = lax.dot_general(rows, weights_ref[3 * i + 1], last, preferred_element_type=F32)
         hidden_ref[:, i * units:(i + 1) * units] = (
             jax.nn.gelu(gate_part, approximate=True) * up_part
         ).astype(BF16)
     width = out_ref.shape[1]
     for n in range(0, width, 512):
-        out_ref[:, n:n + 512] = (
-            jnp.dot(hidden_ref[:, :units], down_ref[:, n:n + 512], preferred_element_type=F32)
-            + jnp.dot(hidden_ref[:, units:], down2_ref[:, n:n + 512], preferred_element_type=F32)
-        ).astype(out_ref.dtype)
+        total = jnp.dot(
+            hidden_ref[:, :units], weights_ref[2, :, n:n + 512], preferred_element_type=F32
+        ) + jnp.dot(
+            hidden_ref[:, units:], weights_ref[5, :, n:n + 512], preferred_element_type=F32
+        )
+        out_ref[:, n:n + 512] = total.astype(out_ref.dtype)
 
 
 def mlp(rows, weights, out_type):
     count, width = rows.shape
-    units = weights[0].shape[0]
+    units = weights.shape[1]
     vmem = pl.BlockSpec(memory_space=pltpu.VMEM)
     return pl.pallas_call(
         mlp_kernel,
         out_shape=jax.ShapeDtypeStruct((count, width), out_type),
-        in_specs=[vmem] * 7,
+        in_specs=[vmem] * 2,
         out_specs=vmem,
         scratch_shapes=[pltpu.VMEM((count, 2 * units), BF16)],
         cost_estimate=pl.CostEstimate(
             flops=12 * count * width * units,
             transcendentals=2 * count * units,
-            bytes_accessed=12 * units * width + 4 * count * width,
-        ),
-        compiler_params=small(20),
+            bytes_accessed=4 * count * width,
+        ),
+        compiler_params=small(MLP_MIB),
         name="mlp",
-    )(rows, *weights)
+    )(rows, weights)
 
 
 def local(
@@ -327,9 +393,11 @@
         code[:, : POOL * PAGE], pooled_key_cache, pooled_value_cache,
     )
     partial = far_attention(
-        low, high, query, code[:, POOL * PAGE:], received, acc, total, w_out
-    )
-
+        low, high, query, code[:, POOL * PAGE:], acc, total, received, w_out
+    )
+
+    weights, partial = lax.optimization_barrier((weights, partial))
+    weights = load_weights(weights)
     parts = [partial[k * ROWS:(k + 1) * ROWS] for k in range(4)]
     for k in range(1, 4):
         parts[k] = lax.ppermute(parts[k], "mlp", [(i, (i + k) % 4) for i in range(4)])
@@ -349,8 +417,7 @@
     line = jnp.concatenate([entering] + [shift(entering, True, k) for k in (1, 2, 3)], axis=0)
     near_out = mlp(line, weights, F32)
     sides = jnp.concatenate([shift(line, False, k) for k in (1, 3)], axis=0)
-    line_later, near_out = lax.optimization_barrier((line, near_out))
-    across = shift(line_later, False, 2)
+    across = shift(line, False, 2)
     side_out = mlp(sides, weights, BF16)
     across_out = mlp(across, weights, BF16)
     step = 4 * ROWS

time: 161 us -> 137 us (0.85)
  local copies, waits for them, and re-layouts: 13.4 us -> 4.79 us
  starting transfers between devices: 35.1 us -> 26.8 us
  Pallas kernels: 39.5 us -> 36.6 us
  waiting for transfers between devices: 61.8 us -> 59.7 us
    pallas_call x3, Pallas kernels: 27.7 us -> 16.2 us  [mlp(): pl.pallas_call(mlp_kernel, out_shape=jax.ShapeDtypeStruct((count, width),...]
    unnamed x49 -> x45, local copies, waits for them, and re-layouts: 11.7 us -> 2.1 us
    ppermute x12, starting transfers between devices: 23.4 us -> 14.6 us  [shift(): return lax.ppermute(value, REQ, chip_shift(first, k % 4))]
    pallas_call x0 -> x1, Pallas kernels: none -> 6.6 us  [load_weights(): pl.pallas_call(load_kernel, out_shape=pltpu.VMEM((count, units, width), B...]
    ppermute x12, waiting for transfers between devices: 35.7 us -> 31.7 us  [shift(): return lax.ppermute(value, REQ, chip_shift(first, k % 4))]
    pallas_call x1, Pallas kernels: 4.19 us -> 6.33 us  [far_attention(): pl.pallas_call(far_kernel, out_shape=jax.ShapeDtypeStruct((128, width), B...]
    all_to_all x1, waiting for transfers between devices: 15 us -> 17.1 us  [local(): lax.all_to_all(packed, REQ, split_axis=0, concat_axis=0, tiled=True)]
  transfers between devices with their start and end apart: 19 -> 19, of which waited for: 15 -> 13; matrix products, arithmetic and copies ran while one was open for 7% -> 6% of each run, Pallas kernels for 22% -> 26%
where the time goes in v3:
time: 137 us; the launch traced here: 136 us
  waiting for transfers between devices  59.7 us (44%)
  Pallas kernels  36.6 us (27%)
  starting transfers between devices  26.8 us (20%)
  local copies, waits for them, and re-layouts  4.79 us (3%)
  matrix products  4.53 us (3%)
  other arithmetic  2.19 us (2%)
    ppermute x12, waiting for transfers between devices, shift(): return lax.ppermute(value, REQ, chip_shift(first, k % 4))  31.7 us
    all_to_all x1, waiting for transfers between devices, local(): lax.all_to_all(packed, REQ, split_axis=0, concat_axis=0, tiled=True)  17.1 us
    pallas_call x3, Pallas kernels, mlp(): pl.pallas_call(mlp_kernel, out_shape=jax.ShapeDtypeStruct((count, width),...  16.2 us
    ppermute x12, starting transfers between devices, shift(): return lax.ppermute(value, REQ, chip_shift(first, k % 4))  14.6 us
    ppermute x3, waiting for transfers between devices, local(): lax.ppermute(parts[k], 'mlp', [(i, (i + k) % 4) for i in range(4)])  10.9 us
    all_to_all x1, starting transfers between devices, local(): lax.all_to_all(packed, REQ, split_axis=0, concat_axis=0, tiled=True)  8.48 us
    pallas_call x1, Pallas kernels, load_weights(): pl.pallas_call(load_kernel, out_shape=pltpu.VMEM((count, units, width), B...  6.6 us
    pallas_call x1, Pallas kernels, far_attention(): pl.pallas_call(far_kernel, out_shape=jax.ShapeDtypeStruct((128, width), B...  6.33 us
  transfers between devices with their start and end apart: 19, of which 13 were waited for; matrix products, arithmetic and copies ran while one was open for 6% of the time, Pallas kernels for 26%

profile of v3, /device:TPU:16, one launch (start us, length us, event | category | flops | bytes accessed | tf_op | source)
XLA Modules:
  0.0 135.8 jit_solution(17205754871175139960)
XLA Ops:
  1.3 3.9 %pick_pages.1 = bf16[32,2,64,256]{3,2,1,0:T(8,128)(2,1)} custom-call(s32[32]{0:T(128)} %bitcast.31, bf16[32,64,256]{2,1,0:T(8,128)(2,1)} %keys_ref.3, bf16[32,64,256]{2,1,0:T(8,128)(2,1)} %values_ref.3), custom_call_target="tpu_custom_call" | custom-call | tf_op jit(solution)/shard_map/pick_pages/pallas_call | solution.py:104
  5.3 8.5 %all-to-all-start = ((bf16[32,2,64,256]{3,2,1,0:T(8,128)(2,1)}), bf16[32,2,64,256]{3,2,1,0:T(8,128)(2,1)}, u32[]{:S(2)}, u32[]{:S(2)}) async-start(bf16[32,2,64,256]{3,2,1,0:T(8,128)(2,1)} %pick_pages.1), calls=%async_computation | async-start | bytes 4194304 | tf_op jit(solution)/shard_map/all_to_all | solution.py:343
  14.8 3.6 %fusion.26 = f32[128,512]{0,1:T(8,128)S(1)} fusion(bf16[3584,512]{1,0:T(8,128)(2,1)} %param.26, bf16[128,3584]{1,0:T(8,128)(2,1)S(1)} %copy-done.12, f32[3584]{0:T(1024)S(1)} %copy-done.13, f32[128]{0:T(128)S(1)} %add_rsqrt_fusion), kind=kOutput, calls=%fused_computation.76 | convolution fusion | flops 471597056 | bytes 4864512 | tf_op jit(solution)/shard_map/dot_general | solution.py:355
  22.0 2.2 %own_attention.1 = (f32[2,128,256]{2,1,0:T(8,128)S(1)}, f32[2,128,128]{2,1,0:T(8,128)S(1)}) custom-call(s32[128,1]{1,0:T(8,128)S(1)} %copy.37.low_ref, s32[128,1]{1,0:T(8,128)S(1)} %copy.38.high_ref, s32[128,1]{1,0:T(8,128)S(1)} %add_select_fusion.order_ref, s32[1,128]{1,0:T(1,128)S(1)} %copy-done.11, bf16[2,128,256]{2,1,0:T(8,128)(2,1)S(1)} %fusion.5.query_ref, ...), custom_call_target="tpu_custom_call" | custom-call | flops 570425344 | bytes 3000000 | tf_op jit(solution)/shard_map/own_attention/pallas_call | solution.py:190
  25.7 17.1 %all-to-all-done.pages_ref = bf16[32,2,64,256]{3,2,1,0:T(8,128)(2,1)} async-done(((bf16[32,2,64,256]{3,2,1,0:T(8,128)(2,1)}), bf16[32,2,64,256]{3,2,1,0:T(8,128)(2,1)}, u32[]{:S(2)}, u32[]{:S(2)}) %all-to-all-start) | async-done | bytes 2097184 | tf_op jit(solution)/shard_map/all_to_all | solution.py:343
  42.7 6.3 %far_attention.1 = bf16[128,3584]{1,0:T(8,128)(2,1)} custom-call(s32[128,1]{1,0:T(8,128)} %copy-done.5, s32[128,1]{1,0:T(8,128)} %copy-done.6, bf16[2,128,256]{2,1,0:T(8,128)(2,1)} %copy-done.4, s32[1,2048]{1,0:T(1,128)} %get-tuple-element.46.code_ref, f32[2,128,256]{2,1,0:T(8,128)} %copy-done.7, f32[2,128,128]{2,1,0:T(8,128)} %copy-done.9, ...), custom_call_target="tpu_custom_call" | custom-call | flops 536870912 | bytes 7000000 | tf_op jit(solution)/shard_map/far_attention/pallas_call | solution.py:241
  49.1 1.3 fusion.30
  50.5 1.4 collective-permute-start.3
  52.4 1.1 collective-permute-start.5
  53.5 9.1 %collective-permute-done.3.b_ref = bf16[32,3584]{1,0:T(8,128)(2,1)S(1)} collective-permute-done((bf16[32,3584]{1,0:T(8,128)(2,1)S(1)}, bf16[32,3584]{1,0:T(8,128)(2,1)S(1)}, u32[]{:S(2)}, u32[]{:S(2)}) %collective-permute-start.3) | collective-permute-done | bytes 229408 | tf_op jit(solution)/shard_map/ppermute | solution.py:403
  62.6 1.8 %collective-permute-done.5.d_ref = bf16[32,3584]{1,0:T(8,128)(2,1)S(1)} collective-permute-done((bf16[32,3584]{1,0:T(8,128)(2,1)S(1)}, bf16[32,3584]{1,0:T(8,128)(2,1)S(1)}, u32[]{:S(2)}, u32[]{:S(2)}) %collective-permute-start.5) | collective-permute-done | bytes 229408 | tf_op jit(solution)/shard_map/ppermute | solution.py:403
  64.9 2.3 %collective-permute-start.7 = (bf16[32,3584]{1,0:T(8,128)(2,1)S(1)}, bf16[32,3584]{1,0:T(8,128)(2,1)S(1)}, u32[]{:S(2)}, u32[]{:S(2)}) collective-permute-start(bf16[32,3584]{1,0:T(8,128)(2,1)S(1)} %get-tuple-element.18), channel_id=1, source_target_pairs={{0,64},{4,20},{8,72},{12,28},{16,80},{20,4},{24,88},{28,12},{32,96... | collective-permute-start | bytes 688136 | tf_op jit(solution)/shard_map/ppermute | solution.py:72
  67.2 1.4 %collective-permute-start.8 = (bf16[32,3584]{1,0:T(8,128)(2,1)S(1)}, bf16[32,3584]{1,0:T(8,128)(2,1)S(1)}, u32[]{:S(2)}, u32[]{:S(2)}) collective-permute-start(bf16[32,3584]{1,0:T(8,128)(2,1)S(1)} %get-tuple-element.18), channel_id=1, source_target_pairs={{0,96},{4,28},{8,104},{12,4},{16,112},{20,12},{24,120},{28,20},{32... | collective-permute-start | bytes 688136 | tf_op jit(solution)/shard_map/ppermute | solution.py:72
  68.7 5.9 %collective-permute-done.6 = bf16[32,3584]{1,0:T(8,128)(2,1)S(1)} collective-permute-done((bf16[32,3584]{1,0:T(8,128)(2,1)S(1)}, bf16[32,3584]{1,0:T(8,128)(2,1)S(1)}, u32[]{:S(2)}, u32[]{:S(2)}) %collective-permute-start.6) | collective-permute-done | bytes 229408 | tf_op jit(solution)/shard_map/ppermute | solution.py:72
  74.6 0.8 collective-permute-done.8
  75.5 1.2 collective-permute-start.13
  76.7 1.5 %collective-permute-start.10 = (bf16[128,3584]{1,0:T(8,128)(2,1)S(1)}, bf16[128,3584]{1,0:T(8,128)(2,1)S(1)}, u32[]{:S(2)}, u32[]{:S(2)}) collective-permute-start(bf16[128,3584]{1,0:T(8,128)(2,1)S(1)} %constant_dynamic-update-slice_fusion.rows_ref), channel_id=1, source_target_pairs={{0,24},{4,100},{8,0},{12,108},{16,8},{20,116},{24,16},{28,124},{32... | collective-permute-start | bytes 2752520 | tf_op jit(solution)/shard_map/ppermute | solution.py:72
  78.7 6.6 %load_weights.1.weights_ref = bf16[6,448,3584]{2,1,0:T(8,128)(2,1)S(1)} custom-call(bf16[448,3584]{1,0:T(8,128)(2,1)} %bitcast.27, bf16[448,3584]{1,0:T(8,128)(2,1)} %bitcast.29, bf16[448,3584]{1,0:T(8,128)(2,1)} %refs_2_, bf16[448,3584]{1,0:T(8,128)(2,1)} %collective-permute-done.refs_3_, bf16[448,3584]{1,0:T(8,128)(2,1)} %collective-permute-done.1.refs_4_, ...), custom_call_target="tpu_custom_call" | custom-call | bytes 19267584 | tf_op jit(solution)/shard_map/load_weights/pallas_call | solution.py:137
  85.3 5.5 %collective-permute-done.13.rows_ref = bf16[128,3584]{1,0:T(8,128)(2,1)S(1)} collective-permute-done((bf16[128,3584]{1,0:T(8,128)(2,1)S(1)}, bf16[128,3584]{1,0:T(8,128)(2,1)S(1)}, u32[]{:S(2)}, u32[]{:S(2)}) %collective-permute-start.13) | collective-permute-done | bytes 917536 | tf_op jit(solution)/shard_map/ppermute | solution.py:72
  90.8 5.0 %mlp.5 = bf16[128,3584]{1,0:T(8,128)(2,1)S(1)} custom-call(bf16[128,3584]{1,0:T(8,128)(2,1)S(1)} %collective-permute-done.13.rows_ref, bf16[6,448,3584]{2,1,0:T(8,128)(2,1)S(1)} %load_weights.1.weights_ref), custom_call_target="tpu_custom_call" | custom-call | flops 2466250752 | bytes 1835008 | tf_op jit(solution)/shard_map/mlp/pallas_call | solution.py:302
  95.8 1.0 collective-permute-start.14
  96.8 2.2 %collective-permute-done.10 = bf16[128,3584]{1,0:T(8,128)(2,1)S(1)} collective-permute-done((bf16[128,3584]{1,0:T(8,128)(2,1)S(1)}, bf16[128,3584]{1,0:T(8,128)(2,1)S(1)}, u32[]{:S(2)}, u32[]{:S(2)}) %collective-permute-start.10) | collective-permute-done | bytes 917536 | tf_op jit(solution)/shard_map/ppermute | solution.py:72
  99.0 1.5 %collective-permute-done.9 = bf16[128,3584]{1,0:T(8,128)(2,1)S(1)} collective-permute-done((bf16[128,3584]{1,0:T(8,128)(2,1)S(1)}, bf16[128,3584]{1,0:T(8,128)(2,1)S(1)}, u32[]{:S(2)}, u32[]{:S(2)}) %collective-permute-start.9) | collective-permute-done | bytes 917536 | tf_op jit(solution)/shard_map/ppermute | solution.py:72
  100.6 6.2 %mlp.4 = bf16[256,3584]{1,0:T(8,128)(2,1)S(1)} custom-call(bf16[256,3584]{1,0:T(8,128)(2,1)S(1)} %pad_maximum_fusion.rows_ref, bf16[6,448,3584]{2,1,0:T(8,128)(2,1)S(1)} %load_weights.1.weights_ref), custom_call_target="tpu_custom_call" | custom-call | flops 4932501504 | bytes 3670016 | tf_op jit(solution)/shard_map/mlp/pallas_call | solution.py:302
  107.1 3.2 %collective-permute-start.11 = (bf16[128,3584]{1,0:T(8,128)(2,1)S(1)}, bf16[128,3584]{1,0:T(8,128)(2,1)S(1)}, u32[]{:S(2)}, u32[]{:S(2)}) collective-permute-start(bf16[128,3584]{1,0:T(8,128)(2,1)S(1)} %get-tuple-element.29), channel_id=1, source_target_pairs={{0,24},{4,100},{8,0},{12,108},{16,8},{20,116},{24,16},{28,124},{32... | collective-permute-start | bytes 2752520 | tf_op jit(solution)/shard_map/ppermute | solution.py:72
  110.3 5.0 %mlp.3 = f32[128,3584]{1,0:T(8,128)S(1)} custom-call(bf16[128,3584]{1,0:T(8,128)(2,1)S(1)} %constant_dynamic-update-slice_fusion.rows_ref, bf16[6,448,3584]{2,1,0:T(8,128)(2,1)S(1)} %load_weights.1.weights_ref), custom_call_target="tpu_custom_call" | custom-call | flops 2466250752 | bytes 1835008 | tf_op jit(solution)/shard_map/mlp/pallas_call | solution.py:302
  115.3 6.4 %collective-permute-done.12 = bf16[128,3584]{1,0:T(8,128)(2,1)S(1)} collective-permute-done((bf16[128,3584]{1,0:T(8,128)(2,1)S(1)}, bf16[128,3584]{1,0:T(8,128)(2,1)S(1)}, u32[]{:S(2)}, u32[]{:S(2)}) %collective-permute-start.12) | collective-permute-done | bytes 917536 | tf_op jit(solution)/shard_map/ppermute | solution.py:72
  122.5 2.4 %collective-permute-start.15 = (bf16[32,3584]{1,0:T(8,128)(2,1)S(1)}, bf16[32,3584]{1,0:T(8,128)(2,1)S(1)}, u32[]{:S(2)}, u32[]{:S(2)}) collective-permute-start(bf16[32,3584]{1,0:T(8,128)(2,1)S(1)} %get-tuple-element.33), channel_id=1, source_target_pairs={{0,96},{4,28},{8,104},{12,4},{16,112},{20,12},{24,120},{28,20},{32... | collective-permute-start | bytes 688136 | tf_op jit(solution)/shard_map/ppermute | solution.py:72
  125.8 5.1 %collective-permute-done.15.b_ref = bf16[32,3584]{1,0:T(8,128)(2,1)S(1)} collective-permute-done((bf16[32,3584]{1,0:T(8,128)(2,1)S(1)}, bf16[32,3584]{1,0:T(8,128)(2,1)S(1)}, u32[]{:S(2)}, u32[]{:S(2)}) %collective-permute-start.15) | collective-permute-done | bytes 229408 | tf_op jit(solution)/shard_map/ppermute | solution.py:72
  130.9 1.6 %collective-permute-done.16.c_ref = bf16[32,3584]{1,0:T(8,128)(2,1)S(1)} collective-permute-done((bf16[32,3584]{1,0:T(8,128)(2,1)S(1)}, bf16[32,3584]{1,0:T(8,128)(2,1)S(1)}, u32[]{:S(2)}, u32[]{:S(2)}) %collective-permute-start.16) | collective-permute-done | bytes 229408 | tf_op jit(solution)/shard_map/ppermute | solution.py:72
  132.5 2.4 %collective-permute-done.17.d_ref = bf16[32,3584]{1,0:T(8,128)(2,1)S(1)} collective-permute-done((bf16[32,3584]{1,0:T(8,128)(2,1)S(1)}, bf16[32,3584]{1,0:T(8,128)(2,1)S(1)}, u32[]{:S(2)}, u32[]{:S(2)}) %collective-permute-start.17) | collective-permute-done | bytes 229408 | tf_op jit(solution)/shard_map/ppermute | solution.py:72
  134.9 0.9 leave.1
  (98 shorter events, 10.2 us)
Async XLA Ops:
  0.6 18.5 %copy-start = (bf16[3584,256]{1,0:T(8,128)(2,1)S(1)}, bf16[3584,256]{1,0:T(8,128)(2,1)}, u32[]{:S(2)}) copy-start(bf16[3584,256]{1,0:T(8,128)(2,1)} %param.27) | copy-start | bytes 5505028
  0.6 48.4 %collective-permute-start = (bf16[448,3584]{1,0:T(8,128)(2,1)}, bf16[448,3584]{1,0:T(8,128)(2,1)}, u32[]{:S(2)}, u32[]{:S(2)}) collective-permute-start(bf16[448,3584]{1,0:T(8,128)(2,1)} %bitcast.26), channel_id=1, source_target_pairs={{0,4},{4,0},{1,5},{5,1},{2,6},{6,2},{3,7},{7,3},{8,12},{12,8},{9,1... | collective-permute-start | bytes 9633800 | tf_op jit(solution)/shard_map/ppermute | solution.py:347
  0.7 48.3 %collective-permute-start.1 = (bf16[448,3584]{1,0:T(8,128)(2,1)}, bf16[448,3584]{1,0:T(8,128)(2,1)}, u32[]{:S(2)}, u32[]{:S(2)}) collective-permute-start(bf16[448,3584]{1,0:T(8,128)(2,1)} %bitcast.28), channel_id=1, source_target_pairs={{0,4},{4,0},{1,5},{5,1},{2,6},{6,2},{3,7},{7,3},{8,12},{12,8},{9,1... | collective-permute-start | bytes 9633800 | tf_op jit(solution)/shard_map/ppermute | solution.py:347
  1.2 47.9 %collective-permute-start.2 = (bf16[448,3584]{1,0:T(8,128)(2,1)}, bf16[448,3584]{1,0:T(8,128)(2,1)}, u32[]{:S(2)}, u32[]{:S(2)}) collective-permute-start(bf16[448,3584]{1,0:T(8,128)(2,1)} %refs_2_), channel_id=1, source_target_pairs={{0,4},{4,0},{1,5},{5,1},{2,6},{6,2},{3,7},{7,3},{8,12},{12,8},{9,1... | collective-permute-start | bytes 9633800 | tf_op jit(solution)/shard_map/ppermute | solution.py:347
  5.3 8.6 %copy-start.11 = (s32[1,128]{1,0:T(1,128)S(1)}, s32[1,128]{1,0:T(1,128)}, u32[]{:S(2)}) copy-start(s32[1,128]{1,0:T(1,128)} %seg_row_ref.1) | copy-start | bytes 1540
  5.3 8.7 %copy-start.12 = (bf16[128,3584]{1,0:T(8,128)(2,1)S(1)}, bf16[128,3584]{1,0:T(8,128)(2,1)}, u32[]{:S(2)}) copy-start(bf16[128,3584]{1,0:T(8,128)(2,1)} %param.18) | copy-start | bytes 2752516
  5.3 9.0 %copy-start.19 = (s32[1,64]{1,0:T(1,128)S(1)}, s32[1,64]{1,0:T(1,128)}, u32[]{:S(2)}) copy-start(s32[1,64]{1,0:T(1,128)} %param.21) | copy-start | bytes 772
  5.3 9.1 %copy-start.17 = (s32[1,4]{1,0:T(1,128)S(1)}, s32[1,4]{1,0:T(1,128)}, u32[]{:S(2)}) copy-start(s32[1,4]{1,0:T(1,128)} %param.20) | copy-start | bytes 52
  5.3 9.5 %copy-start.13 = (f32[3584]{0:T(1024)S(1)}, f32[3584]{0:T(1024)}, u32[]{:S(2)}) copy-start(f32[3584]{0:T(1024)} %param.25) | copy-start | bytes 43012
  5.3 37.4 %all-to-all-start = ((bf16[32,2,64,256]{3,2,1,0:T(8,128)(2,1)}), bf16[32,2,64,256]{3,2,1,0:T(8,128)(2,1)}, u32[]{:S(2)}, u32[]{:S(2)}) async-start(bf16[32,2,64,256]{3,2,1,0:T(8,128)(2,1)} %pick_pages.1), calls=%async_computation | async-start | bytes 4194304 | tf_op jit(solution)/shard_map/all_to_all | solution.py:343
  14.8 4.3 %copy-start.14 = (f32[3584]{0:T(1024)S(1)}, f32[3584]{0:T(1024)}, u32[]{:S(2)}) copy-start(f32[3584]{0:T(1024)} %param.30) | copy-start | bytes 43012
  14.8 4.3 %copy-start.15 = (f32[3584]{0:T(1024)S(1)}, f32[3584]{0:T(1024)}, u32[]{:S(2)}) copy-start(f32[3584]{0:T(1024)} %param.31) | copy-start | bytes 43012
  18.7 3.1 %copy-start.5 = (s32[128,1]{1,0:T(8,128)}, s32[128,1]{1,0:T(8,128)S(1)}, u32[]{:S(2)}) copy-start(s32[128,1]{1,0:T(8,128)S(1)} %copy.37.low_ref) | copy-start | bytes 1540
  20.7 3.6 %copy-start.4 = (bf16[2,128,256]{2,1,0:T(8,128)(2,1)}, bf16[2,128,256]{2,1,0:T(8,128)(2,1)S(1)}, u32[]{:S(2)}) copy-start(bf16[2,128,256]{2,1,0:T(8,128)(2,1)S(1)} %fusion.5.query_ref) | copy-start | bytes 393220
  21.1 27.9 %copy-start.10 = (bf16[128,256]{1,0:T(8,128)(2,1)}, bf16[128,256]{1,0:T(8,128)(2,1)S(1)}, u32[]{:S(2)}) copy-start(bf16[128,256]{1,0:T(8,128)(2,1)S(1)} %convolution_convert_fusion.new_values_ref) | copy-start | bytes 196612
  50.5 12.1 %collective-permute-start.3 = (bf16[32,3584]{1,0:T(8,128)(2,1)S(1)}, bf16[32,3584]{1,0:T(8,128)(2,1)S(1)}, u32[]{:S(2)}, u32[]{:S(2)}) collective-permute-start(bf16[32,3584]{1,0:T(8,128)(2,1)S(1)} %get-tuple-element.37), channel_id=1, source_target_pairs={{0,1},{1,2},{2,3},{3,0},{4,5},{5,6},{6,7},{7,4},{8,9},{9,10},{10,1... | collective-permute-start | bytes 688136 | tf_op jit(solution)/shard_map/ppermute | solution.py:403
  51.8 10.8 %collective-permute-start.4 = (bf16[32,3584]{1,0:T(8,128)(2,1)S(1)}, bf16[32,3584]{1,0:T(8,128)(2,1)S(1)}, u32[]{:S(2)}, u32[]{:S(2)}) collective-permute-start(bf16[32,3584]{1,0:T(8,128)(2,1)S(1)} %get-tuple-element.36), channel_id=1, source_target_pairs={{0,2},{1,3},{2,0},{3,1},{4,6},{5,7},{6,4},{7,5},{8,10},{9,11},{10,... | collective-permute-start | bytes 688136 | tf_op jit(solution)/shard_map/ppermute | solution.py:403
  52.4 12.0 %collective-permute-start.5 = (bf16[32,3584]{1,0:T(8,128)(2,1)S(1)}, bf16[32,3584]{1,0:T(8,128)(2,1)S(1)}, u32[]{:S(2)}, u32[]{:S(2)}) collective-permute-start(bf16[32,3584]{1,0:T(8,128)(2,1)S(1)} %get-tuple-element.35), channel_id=1, source_target_pairs={{0,3},{1,0},{2,1},{3,2},{4,7},{5,4},{6,5},{7,6},{8,11},{9,8},{10,9... | collective-permute-start | bytes 688136 | tf_op jit(solution)/shard_map/ppermute | solution.py:403
  64.8 9.8 %collective-permute-start.6 = (bf16[32,3584]{1,0:T(8,128)(2,1)S(1)}, bf16[32,3584]{1,0:T(8,128)(2,1)S(1)}, u32[]{:S(2)}, u32[]{:S(2)}) collective-permute-start(bf16[32,3584]{1,0:T(8,128)(2,1)S(1)} %get-tuple-element.18), channel_id=1, source_target_pairs={{0,32},{4,12},{8,40},{12,20},{16,48},{20,28},{24,56},{28,4},{32,64... | collective-permute-start | bytes 688136 | tf_op jit(solution)/shard_map/ppermute | solution.py:72
  64.9 9.7 %collective-permute-start.7 = (bf16[32,3584]{1,0:T(8,128)(2,1)S(1)}, bf16[32,3584]{1,0:T(8,128)(2,1)S(1)}, u32[]{:S(2)}, u32[]{:S(2)}) collective-permute-start(bf16[32,3584]{1,0:T(8,128)(2,1)S(1)} %get-tuple-element.18), channel_id=1, source_target_pairs={{0,64},{4,20},{8,72},{12,28},{16,80},{20,4},{24,88},{28,12},{32,96... | collective-permute-start | bytes 688136 | tf_op jit(solution)/shard_map/ppermute | solution.py:72
  67.2 8.3 %collective-permute-start.8 = (bf16[32,3584]{1,0:T(8,128)(2,1)S(1)}, bf16[32,3584]{1,0:T(8,128)(2,1)S(1)}, u32[]{:S(2)}, u32[]{:S(2)}) collective-permute-start(bf16[32,3584]{1,0:T(8,128)(2,1)S(1)} %get-tuple-element.18), channel_id=1, source_target_pairs={{0,96},{4,28},{8,104},{12,4},{16,112},{20,12},{24,120},{28,20},{32... | collective-permute-start | bytes 688136 | tf_op jit(solution)/shard_map/ppermute | solution.py:72
  75.5 15.3 %collective-permute-start.13 = (bf16[128,3584]{1,0:T(8,128)(2,1)S(1)}, bf16[128,3584]{1,0:T(8,128)(2,1)S(1)}, u32[]{:S(2)}, u32[]{:S(2)}) collective-permute-start(bf16[128,3584]{1,0:T(8,128)(2,1)S(1)} %constant_dynamic-update-slice_fusion.rows_ref), channel_id=1, source_target_pairs={{0,16},{4,68},{8,24},{12,76},{16,0},{20,84},{24,8},{28,92},{32,48}... | collective-permute-start | bytes 2752520 | tf_op jit(solution)/shard_map/ppermute | solution.py:72
  76.7 22.3 %collective-permute-start.10 = (bf16[128,3584]{1,0:T(8,128)(2,1)S(1)}, bf16[128,3584]{1,0:T(8,128)(2,1)S(1)}, u32[]{:S(2)}, u32[]{:S(2)}) collective-permute-start(bf16[128,3584]{1,0:T(8,128)(2,1)S(1)} %constant_dynamic-update-slice_fusion.rows_ref), channel_id=1, source_target_pairs={{0,24},{4,100},{8,0},{12,108},{16,8},{20,116},{24,16},{28,124},{32... | collective-permute-start | bytes 2752520 | tf_op jit(solution)/shard_map/ppermute | solution.py:72
  78.2 22.3 %collective-permute-start.9 = (bf16[128,3584]{1,0:T(8,128)(2,1)S(1)}, bf16[128,3584]{1,0:T(8,128)(2,1)S(1)}, u32[]{:S(2)}, u32[]{:S(2)}) collective-permute-start(bf16[128,3584]{1,0:T(8,128)(2,1)S(1)} %constant_dynamic-update-slice_fusion.rows_ref), channel_id=1, source_target_pairs={{0,8},{4,36},{8,16},{12,44},{16,24},{20,52},{24,0},{28,60},{32,40}... | collective-permute-start | bytes 2752520 | tf_op jit(solution)/shard_map/ppermute | solution.py:72
  95.8 19.5 %collective-permute-start.14 = (bf16[128,3584]{1,0:T(8,128)(2,1)S(1)}, bf16[128,3584]{1,0:T(8,128)(2,1)S(1)}, u32[]{:S(2)}, u32[]{:S(2)}) collective-permute-start(bf16[128,3584]{1,0:T(8,128)(2,1)S(1)} %mlp.5), channel_id=1, source_target_pairs={{0,16},{4,68},{8,24},{12,76},{16,0},{20,84},{24,8},{28,92},{32,48}... | collective-permute-start | bytes 2752520 | tf_op jit(solution)/shard_map/ppermute | solution.py:72
  107.0 14.7 %collective-permute-start.12 = (bf16[128,3584]{1,0:T(8,128)(2,1)S(1)}, bf16[128,3584]{1,0:T(8,128)(2,1)S(1)}, u32[]{:S(2)}, u32[]{:S(2)}) collective-permute-start(bf16[128,3584]{1,0:T(8,128)(2,1)S(1)} %get-tuple-element.30), channel_id=1, source_target_pairs={{0,8},{4,36},{8,16},{12,44},{16,24},{20,52},{24,0},{28,60},{32,40}... | collective-permute-start | bytes 2752520 | tf_op jit(solution)/shard_map/ppermute | solution.py:72
  107.1 14.9 %collective-permute-start.11 = (bf16[128,3584]{1,0:T(8,128)(2,1)S(1)}, bf16[128,3584]{1,0:T(8,128)(2,1)S(1)}, u32[]{:S(2)}, u32[]{:S(2)}) collective-permute-start(bf16[128,3584]{1,0:T(8,128)(2,1)S(1)} %get-tuple-element.29), channel_id=1, source_target_pairs={{0,24},{4,100},{8,0},{12,108},{16,8},{20,116},{24,16},{28,124},{32... | collective-permute-start | bytes 2752520 | tf_op jit(solution)/shard_map/ppermute | solution.py:72
  122.0 13.8 %copy-start.1 = (bf16[3584,256]{1,0:T(8,128)(2,1)S(1)}, bf16[3584,256]{1,0:T(8,128)(2,1)}, u32[]{:S(2)}) copy-start(bf16[3584,256]{1,0:T(8,128)(2,1)} %param.27) | copy-start | bytes 5505028
  122.4 3.4 %copy-start.16 = (f32[3584]{0:T(1024)S(1)}, f32[3584]{0:T(1024)}, u32[]{:S(2)}) copy-start(f32[3584]{0:T(1024)} %param.35) | copy-start | bytes 43012
  122.5 8.4 %collective-permute-start.15 = (bf16[32,3584]{1,0:T(8,128)(2,1)S(1)}, bf16[32,3584]{1,0:T(8,128)(2,1)S(1)}, u32[]{:S(2)}, u32[]{:S(2)}) collective-permute-start(bf16[32,3584]{1,0:T(8,128)(2,1)S(1)} %get-tuple-element.33), channel_id=1, source_target_pairs={{0,96},{4,28},{8,104},{12,4},{16,112},{20,12},{24,120},{28,20},{32... | collective-permute-start | bytes 688136 | tf_op jit(solution)/shard_map/ppermute | solution.py:72
  124.9 7.6 %collective-permute-start.16 = (bf16[32,3584]{1,0:T(8,128)(2,1)S(1)}, bf16[32,3584]{1,0:T(8,128)(2,1)S(1)}, u32[]{:S(2)}, u32[]{:S(2)}) collective-permute-start(bf16[32,3584]{1,0:T(8,128)(2,1)S(1)} %get-tuple-element.32), channel_id=1, source_target_pairs={{0,64},{4,20},{8,72},{12,28},{16,80},{20,4},{24,88},{28,12},{32,96... | collective-permute-start | bytes 688136 | tf_op jit(solution)/shard_map/ppermute | solution.py:72
  125.2 9.7 %collective-permute-start.17 = (bf16[32,3584]{1,0:T(8,128)(2,1)S(1)}, bf16[32,3584]{1,0:T(8,128)(2,1)S(1)}, u32[]{:S(2)}, u32[]{:S(2)}) collective-permute-start(bf16[32,3584]{1,0:T(8,128)(2,1)S(1)} %get-tuple-element.31), channel_id=1, source_target_pairs={{0,32},{4,12},{8,40},{12,20},{16,48},{20,28},{24,56},{28,4},{32,64... | collective-permute-start | bytes 688136 | tf_op jit(solution)/shard_map/ppermute | solution.py:72
  (7 other events, 10.6 us)

commit v4 on v3

--- a/solution.py
+++ b/solution.py
@@ -18,7 +18,7 @@
 NORM_EPS = 1e-06
 ROPE_BASE = 10000.0
 MLP_MIB = 8
-LOAD_MIB = 40
+LOAD_MIB = 4
 FAR_MIB = 58
 
 BF16 = jnp.bfloat16
@@ -76,24 +76,28 @@
     return pltpu.CompilerParams(vmem_limit_bytes=megabytes * 1024 * 1024)
 
 
-def pick_pages_kernel(pages_ref, keys_ref, values_ref, out_ref, held_ref, in_sems, out_sems):
+GROUP = 8
+
+
+def pick_pages_kernel(pages_ref, keys_ref, values_ref, out_ref, keys_held, values_held, held_ref,
+                      in_sems, out_sems):
     loads = []
-    for d in range(OWNERS):
-        page = pages_ref[d]
-        loads.append((
-            pltpu.make_async_copy(keys_ref.at[page], held_ref.at[d, 0], in_sems.at[d, 0]),
-            pltpu.make_async_copy(values_ref.at[page], held_ref.at[d, 1], in_sems.at[d, 1]),
-        ))
-        for load in loads[d]:
-            load.start()
+    for g in range(POOL // GROUP):
+        part = pl.ds(g * GROUP, GROUP)
+        loads.append(pltpu.make_async_copy(keys_ref.at[part], keys_held.at[part], in_sems.at[0, g]))
+        loads.append(pltpu.make_async_copy(values_ref.at[part], values_held.at[part], in_sems.at[1, g]))
+    for load in loads:
+        load.start()
+    for load in loads:
+        load.wait()
     stores = []
-    for d in range(0, OWNERS, 4):
-        for e in range(d, d + 4):
-            for load in loads[e]:
-                load.wait()
-        stores.append(
-            pltpu.make_async_copy(held_ref.at[d:d + 4], out_ref.at[d:d + 4], out_sems.at[d // 4])
-        )
+    for g in range(OWNERS // GROUP):
+        for d in range(g * GROUP, (g + 1) * GROUP):
+            page = pages_ref[d]
+            held_ref[d, 0] = keys_held[page]
+            held_ref[d, 1] = values_held[page]
+        part = pl.ds(g * GROUP, GROUP)
+        stores.append(pltpu.make_async_copy(held_ref.at[part], out_ref.at[part], out_sems.at[g]))
         stores[-1].start()
     for store in stores:
         store.wait()
@@ -110,9 +114,11 @@
             in_specs=[hbm] * 2,
             out_specs=hbm,
             scratch_shapes=[
+                pltpu.VMEM((POOL, PAGE, HEAD_SIZE), BF16),
+                pltpu.VMEM((POOL, PAGE, HEAD_SIZE), BF16),
                 pltpu.VMEM((OWNERS, 2, PAGE, HEAD_SIZE), BF16),
-                pltpu.SemaphoreType.DMA((OWNERS, 2)),
-                pltpu.SemaphoreType.DMA((OWNERS // 4,)),
+                pltpu.SemaphoreType.DMA((2, POOL // GROUP)),
+                pltpu.SemaphoreType.DMA((OWNERS // GROUP,)),
             ],
         ),
         compiler_params=small(56),
@@ -203,60 +209,91 @@
     )(low, high, order, seg_row, query, new_keys, new_values, code, keys, values)
 
 
-def far_kernel(low_ref, high_ref, query_ref, code_ref, acc_in_ref, total_in_ref, pages_ref, w_ref,
-               out_ref, acc_ref, total_ref, held_ref, w_held_ref, page_sems, w_sem):
+def far_kernel(low_hbm, high_hbm, code_hbm, query_hbm, acc_hbm, total_hbm, pages_ref, w_hbm, *refs):
+    (*out_refs, acc_ref, total_ref, query_ref, acc_in_ref, total_in_ref, held_ref, w_ref,
+     low_ref, high_ref, code_ref, page_sems, sems) = refs
+    blocks = OWNERS // STEP_PAGES
     loads = [
         pltpu.make_async_copy(
             pages_ref.at[b * STEP_PAGES:(b + 1) * STEP_PAGES], held_ref.at[b], page_sems.at[b]
         )
-        for b in range(OWNERS // STEP_PAGES)
+        for b in range(blocks)
     ]
+    query_load = pltpu.make_async_copy(query_hbm, query_ref, sems.at[0])
+    acc_load = pltpu.make_async_copy(acc_hbm, acc_in_ref, sems.at[1])
+    total_load = pltpu.make_async_copy(total_hbm, total_in_ref, sems.at[2])
+    w_load = pltpu.make_async_copy(w_hbm, w_ref, sems.at[3])
+    small_loads = [
+        pltpu.make_async_copy(low_hbm, low_ref, sems.at[4]),
+        pltpu.make_async_copy(high_hbm, high_ref, sems.at[5]),
+        pltpu.make_async_copy(code_hbm, code_ref, sems.at[6]),
+        query_load,
+    ]
+    for load in small_loads:
+        load.start()
     for load in loads:
         load.start()
-    w_load = pltpu.make_async_copy(w_ref, w_held_ref, w_sem)
-    w_load.start()
-    acc_ref[...] = acc_in_ref[...]
-    total_ref[...] = total_in_ref[...]
+    acc_ref[...] = jnp.zeros_like(acc_ref)
+    total_ref[...] = jnp.zeros_like(total_ref)
+    for load in small_loads:
+        load.wait()
     low, high = low_ref[...], high_ref[...]
-    for b in range(OWNERS // STEP_PAGES):
+    for b in range(blocks):
         loads[b].wait()
+        if b == 0:
+            w_load.start()
+            acc_load.start()
+            total_load.start()
         keys = held_ref[b, :, 0].reshape(STEP, HEAD_SIZE)
         values = held_ref[b, :, 1].reshape(STEP, HEAD_SIZE)
         code = code_ref[:, b * STEP:(b + 1) * STEP]
         attend(query_ref, keys, values, (code > low) & (code < high), acc_ref, total_ref)
-    heads = [(acc_ref[h] / total_ref[h][:, :1]).astype(BF16) for h in range(HEADS)]
+    acc_load.wait()
+    total_load.wait()
+    heads = [
+        ((acc_ref[h] + acc_in_ref[h]) / (total_ref[h] + total_in_ref[h])[:, :1]).astype(BF16)
+        for h in range(HEADS)
+    ]
     attention = jnp.concatenate(heads, axis=1)
-    width = out_ref.shape[1]
+    rows, width = out_refs[0].shape
     w_load.wait()
     for n in range(0, width, 512):
-        out_ref[:, n:n + 512] = jnp.dot(
-            attention, w_held_ref[:, n:n + 512], preferred_element_type=F32
+        block = jnp.dot(
+            attention, w_ref[:, n:n + 512], preferred_element_type=F32
         ).astype(BF16)
-
-
-def far_attention(low, high, query, code, acc, total, pages, w_out):
+        for i, out_ref in enumerate(out_refs):
+            out_ref[:, n:n + 512] = block[i * rows:(i + 1) * rows]
+
+
+def far_attention(low, high, query, code, acc, total, pages, w_out, blocks):
     vmem = pl.BlockSpec(memory_space=pltpu.VMEM)
     hbm = pl.BlockSpec(memory_space=pltpu.HBM)
     width = w_out.shape[1]
     return pl.pallas_call(
         far_kernel,
-        out_shape=jax.ShapeDtypeStruct((128, width), BF16),
-        in_specs=[vmem] * 6 + [hbm] * 2,
-        out_specs=vmem,
+        out_shape=[pltpu.VMEM((128 // blocks, width), BF16)] * blocks,
+        in_specs=[hbm] * 8,
+        out_specs=[vmem] * blocks,
         scratch_shapes=[
+            pltpu.VMEM((HEADS, 128, HEAD_SIZE), F32),
+            pltpu.VMEM((HEADS, 128, 128), F32),
+            pltpu.VMEM((HEADS, 128, HEAD_SIZE), BF16),
             pltpu.VMEM((HEADS, 128, HEAD_SIZE), F32),
             pltpu.VMEM((HEADS, 128, 128), F32),
             pltpu.VMEM((OWNERS // STEP_PAGES, STEP_PAGES, 2, PAGE, HEAD_SIZE), BF16),
             pltpu.VMEM(w_out.shape, BF16),
+            pltpu.VMEM(low.shape, jnp.int32),
+            pltpu.VMEM(high.shape, jnp.int32),
+            pltpu.VMEM(code.shape, jnp.int32),
             pltpu.SemaphoreType.DMA((OWNERS // STEP_PAGES,)),
-            pltpu.SemaphoreType.DMA,
+            pltpu.SemaphoreType.DMA((7,)),
         ],
         cost_estimate=pl.CostEstimate(
             flops=4 * 256 * 2048 * 256, transcendentals=2 * 256 * 2048, bytes_accessed=7_000_000
         ),
         compiler_params=small(FAR_MIB),
         name="far_attention",
-    )(low, high, query, code, acc, total, pages, w_out)
+    )(low, high, code, query, acc, total, pages, w_out)
 
 
 def enter_kernel(own_ref, a_ref, b_ref, c_ref, d_ref, post_ref, ffw_ref, residual_ref, out_ref):
@@ -392,13 +429,11 @@
         low, high, order[:, None], segment[None, :], query, incoming_keys, incoming_values,
         code[:, : POOL * PAGE], pooled_key_cache, pooled_value_cache,
     )
-    partial = far_attention(
-        low, high, query, code[:, POOL * PAGE:], acc, total, received, w_out
-    )
-
-    weights, partial = lax.optimization_barrier((weights, partial))
+    parts = far_attention(
+        low, high, query, code[:, POOL * PAGE:], acc, total, received, w_out, 4
+    )
+    weights, *parts = lax.optimization_barrier((weights, *parts))
     weights = load_weights(weights)
-    parts = [partial[k * ROWS:(k + 1) * ROWS] for k in range(4)]
     for k in range(1, 4):
         parts[k] = lax.ppermute(parts[k], "mlp", [(i, (i + k) % 4) for i in range(4)])
     vmem = pl.BlockSpec(memory_space=pltpu.VMEM)

time: 137 us -> 133 us (0.971)
  Pallas kernels: 36.6 us -> 33.2 us
  local copies, waits for them, and re-layouts: 4.79 us -> 6.91 us
  waiting for transfers between devices: 59.7 us -> 58.1 us
    unnamed x45 -> x51, local copies, waits for them, and re-layouts: 2.1 us -> 4.92 us
    pallas_call x1, Pallas kernels: 6.6 us -> 4.75 us  [load_weights(): pl.pallas_call(load_kernel, out_shape=pltpu.VMEM((count, units, width), B...]
    all_to_all x1, waiting for transfers between devices: 17.1 us -> 15.5 us  [local(): lax.all_to_all(packed, REQ, split_axis=0, concat_axis=0, tiled=True)]
  transfers between devices with their start and end apart: 19 -> 19, of which waited for: 13 -> 13; matrix products, arithmetic and copies ran while one was open for 6% -> 7% of each run, Pallas kernels for 26% -> 24%
where the time goes in v4:
time: 133 us
  waiting for transfers between devices  58.1 us (44%)
  Pallas kernels  33.2 us (25%)
  starting transfers between devices  26.6 us (20%)
  local copies, waits for them, and re-layouts  6.91 us (5%)
  matrix products  4.53 us (3%)
  other arithmetic  2.18 us (2%)
    ppermute x12, waiting for transfers between devices, shift(): return lax.ppermute(value, REQ, chip_shift(first, k % 4))  31.6 us
    pallas_call x3, Pallas kernels, mlp(): pl.pallas_call(mlp_kernel, out_shape=jax.ShapeDtypeStruct((count, width),...  16.2 us
    all_to_all x1, waiting for transfers between devices, local(): lax.all_to_all(packed, REQ, split_axis=0, concat_axis=0, tiled=True)  15.5 us
    ppermute x12, starting transfers between devices, shift(): return lax.ppermute(value, REQ, chip_shift(first, k % 4))  14.5 us
    ppermute x3, waiting for transfers between devices, local(): lax.ppermute(parts[k], 'mlp', [(i, (i + k) % 4) for i in range(4)])  10.9 us
    all_to_all x1, starting transfers between devices, local(): lax.all_to_all(packed, REQ, split_axis=0, concat_axis=0, tiled=True)  8.47 us
    pallas_call x1, Pallas kernels, far_attention(): pl.pallas_call(far_kernel, out_shape=[pltpu.VMEM((128 // blocks, width),...  5.02 us
    unnamed x51, local copies, waits for them, and re-layouts  4.92 us
  transfers between devices with their start and end apart: 19, of which 13 were waited for; matrix products, arithmetic and copies ran while one was open for 7% of the time, Pallas kernels for 24%

profile of v4, /device:TPU:16, one launch (start us, length us, event | category | flops | bytes accessed | tf_op | source)
XLA Modules:
  0.0 132.7 jit_solution(16730644599731322478)
XLA Ops:
  1.3 3.7 %pick_pages.1 = bf16[32,2,64,256]{3,2,1,0:T(8,128)(2,1)} custom-call(s32[32]{0:T(128)} %bitcast.31, bf16[32,64,256]{2,1,0:T(8,128)(2,1)} %keys_ref.3, bf16[32,64,256]{2,1,0:T(8,128)(2,1)} %values_ref.3), custom_call_target="tpu_custom_call" | custom-call | tf_op jit(solution)/shard_map/pick_pages/pallas_call | solution.py:108
  5.1 8.5 %all-to-all-start = ((bf16[32,2,64,256]{3,2,1,0:T(8,128)(2,1)}), bf16[32,2,64,256]{3,2,1,0:T(8,128)(2,1)}, u32[]{:S(2)}, u32[]{:S(2)}) async-start(bf16[32,2,64,256]{3,2,1,0:T(8,128)(2,1)} %pick_pages.1), calls=%async_computation | async-start | bytes 4194304 | tf_op jit(solution)/shard_map/all_to_all | solution.py:380
  14.6 3.6 %fusion.26 = f32[128,512]{0,1:T(8,128)S(1)} fusion(bf16[3584,512]{1,0:T(8,128)(2,1)} %param.26, bf16[128,3584]{1,0:T(8,128)(2,1)S(1)} %copy-done.15, f32[3584]{0:T(1024)S(1)} %copy-done.16, f32[128]{0:T(128)S(1)} %add_rsqrt_fusion), kind=kOutput, calls=%fused_computation.76 | convolution fusion | flops 471597056 | bytes 4864512 | tf_op jit(solution)/shard_map/dot_general | solution.py:392
  19.4 1.0 copy.41
  23.3 2.2 %own_attention.1 = (f32[2,128,256]{2,1,0:T(8,128)S(1)}, f32[2,128,128]{2,1,0:T(8,128)S(1)}) custom-call(s32[128,1]{1,0:T(8,128)S(1)} %copy.37.low_ref.low_hbm, s32[128,1]{1,0:T(8,128)S(1)} %copy.38.high_ref.high_hbm, s32[128,1]{1,0:T(8,128)S(1)} %add_select_fusion.order_ref, s32[1,128]{1,0:T(1,128)S(1)} %copy-done.14, ...), custom_call_target="tpu_custom_call" | custom-call | flops 570425344 | bytes 3000000 | tf_op jit(solution)/shard_map/own_attention/pallas_call | solution.py:196
  26.9 15.5 %all-to-all-done.pages_ref = bf16[32,2,64,256]{3,2,1,0:T(8,128)(2,1)} async-done(((bf16[32,2,64,256]{3,2,1,0:T(8,128)(2,1)}), bf16[32,2,64,256]{3,2,1,0:T(8,128)(2,1)}, u32[]{:S(2)}, u32[]{:S(2)}) %all-to-all-start) | async-done | bytes 2097184 | tf_op jit(solution)/shard_map/all_to_all | solution.py:380
  42.5 5.0 %far_attention.1 = (bf16[32,3584]{1,0:T(8,128)(2,1)S(1)}, bf16[32,3584]{1,0:T(8,128)(2,1)S(1)}, bf16[32,3584]{1,0:T(8,128)(2,1)S(1)}, bf16[32,3584]{1,0:T(8,128)(2,1)S(1)}) custom-call(s32[128,1]{1,0:T(8,128)} %copy-done.8, s32[128,1]{1,0:T(8,128)} %copy-done.9, s32[1,2048]{1,0:T(1,128)} %get-tuple-element.56.code_hbm, bf16[2,128,256]{2,1,0:T(8,128)(2,1)} %copy-done.7, ...), custom_call_target="tpu_custom_call" | custom-call | flops 536870912 | bytes 7000000 | tf_op jit(solution)/shard_map/far_attention/pallas_call | solution.py:272
  47.6 1.4 %collective-permute-start.3 = (bf16[32,3584]{1,0:T(8,128)(2,1)S(1)}, bf16[32,3584]{1,0:T(8,128)(2,1)S(1)}, u32[]{:S(2)}, u32[]{:S(2)}) collective-permute-start(bf16[32,3584]{1,0:T(8,128)(2,1)S(1)} %get-tuple-element.28), channel_id=1, source_target_pairs={{0,1},{1,2},{2,3},{3,0},{4,5},{5,6},{6,7},{7,4},{8,9},{9,10},{10,1... | collective-permute-start | bytes 688136 | tf_op jit(solution)/shard_map/ppermute | solution.py:438
  49.5 1.1 collective-permute-start.5
  50.6 9.1 %collective-permute-done.3.b_ref = bf16[32,3584]{1,0:T(8,128)(2,1)S(1)} collective-permute-done((bf16[32,3584]{1,0:T(8,128)(2,1)S(1)}, bf16[32,3584]{1,0:T(8,128)(2,1)S(1)}, u32[]{:S(2)}, u32[]{:S(2)}) %collective-permute-start.3) | collective-permute-done | bytes 229408 | tf_op jit(solution)/shard_map/ppermute | solution.py:438
  59.7 1.8 %collective-permute-done.5.d_ref = bf16[32,3584]{1,0:T(8,128)(2,1)S(1)} collective-permute-done((bf16[32,3584]{1,0:T(8,128)(2,1)S(1)}, bf16[32,3584]{1,0:T(8,128)(2,1)S(1)}, u32[]{:S(2)}, u32[]{:S(2)}) %collective-permute-start.5) | collective-permute-done | bytes 229408 | tf_op jit(solution)/shard_map/ppermute | solution.py:438
  62.0 2.3 %collective-permute-start.7 = (bf16[32,3584]{1,0:T(8,128)(2,1)S(1)}, bf16[32,3584]{1,0:T(8,128)(2,1)S(1)}, u32[]{:S(2)}, u32[]{:S(2)}) collective-permute-start(bf16[32,3584]{1,0:T(8,128)(2,1)S(1)} %get-tuple-element.32), channel_id=1, source_target_pairs={{0,64},{4,20},{8,72},{12,28},{16,80},{20,4},{24,88},{28,12},{32,96... | collective-permute-start | bytes 688136 | tf_op jit(solution)/shard_map/ppermute | solution.py:72
  64.3 1.4 %collective-permute-start.8 = (bf16[32,3584]{1,0:T(8,128)(2,1)S(1)}, bf16[32,3584]{1,0:T(8,128)(2,1)S(1)}, u32[]{:S(2)}, u32[]{:S(2)}) collective-permute-start(bf16[32,3584]{1,0:T(8,128)(2,1)S(1)} %get-tuple-element.32), channel_id=1, source_target_pairs={{0,96},{4,28},{8,104},{12,4},{16,112},{20,12},{24,120},{28,20},{32... | collective-permute-start | bytes 688136 | tf_op jit(solution)/shard_map/ppermute | solution.py:72
  65.8 5.9 %collective-permute-done.6 = bf16[32,3584]{1,0:T(8,128)(2,1)S(1)} collective-permute-done((bf16[32,3584]{1,0:T(8,128)(2,1)S(1)}, bf16[32,3584]{1,0:T(8,128)(2,1)S(1)}, u32[]{:S(2)}, u32[]{:S(2)}) %collective-permute-start.6) | collective-permute-done | bytes 229408 | tf_op jit(solution)/shard_map/ppermute | solution.py:72
  72.6 1.0 collective-permute-start.13
  73.6 1.5 %collective-permute-start.10 = (bf16[128,3584]{1,0:T(8,128)(2,1)S(1)}, bf16[128,3584]{1,0:T(8,128)(2,1)S(1)}, u32[]{:S(2)}, u32[]{:S(2)}) collective-permute-start(bf16[128,3584]{1,0:T(8,128)(2,1)S(1)} %constant_dynamic-update-slice_fusion.rows_ref), channel_id=1, source_target_pairs={{0,24},{4,100},{8,0},{12,108},{16,8},{20,116},{24,16},{28,124},{32... | collective-permute-start | bytes 2752520 | tf_op jit(solution)/shard_map/ppermute | solution.py:72
  75.6 1.9 %copy-done.6 = bf16[448,3584]{1,0:T(8,128)(2,1)S(1)} copy-done((bf16[448,3584]{1,0:T(8,128)(2,1)S(1)}, bf16[448,3584]{1,0:T(8,128)(2,1)}, u32[]{:S(2)}) %copy-start.6) | copy-done | bytes 3211288
  77.5 4.8 %load_weights.1.weights_ref = bf16[6,448,3584]{2,1,0:T(8,128)(2,1)S(1)} custom-call(bf16[448,3584]{1,0:T(8,128)(2,1)S(1)} %bitcast.25, bf16[448,3584]{1,0:T(8,128)(2,1)S(1)} %bitcast.27, bf16[448,3584]{1,0:T(8,128)(2,1)S(1)} %copy-done.6, bf16[448,3584]{1,0:T(8,128)(2,1)} %collective-permute-done.refs_3_, bf16[448,3584]{1,0:T(8,128)(2,1)} %collective-permute-done.1.refs_4_, ...), custom_call_target="tpu_custom_call" | custom-call | bytes 19267584 | tf_op jit(solution)/shard_map/load_weights/pallas_call | solution.py:143
  82.3 5.4 %collective-permute-done.13.rows_ref = bf16[128,3584]{1,0:T(8,128)(2,1)S(1)} collective-permute-done((bf16[128,3584]{1,0:T(8,128)(2,1)S(1)}, bf16[128,3584]{1,0:T(8,128)(2,1)S(1)}, u32[]{:S(2)}, u32[]{:S(2)}) %collective-permute-start.13) | collective-permute-done | bytes 917536 | tf_op jit(solution)/shard_map/ppermute | solution.py:72
  87.7 5.0 %mlp.5 = bf16[128,3584]{1,0:T(8,128)(2,1)S(1)} custom-call(bf16[128,3584]{1,0:T(8,128)(2,1)S(1)} %collective-permute-done.13.rows_ref, bf16[6,448,3584]{2,1,0:T(8,128)(2,1)S(1)} %load_weights.1.weights_ref), custom_call_target="tpu_custom_call" | custom-call | flops 2466250752 | bytes 1835008 | tf_op jit(solution)/shard_map/mlp/pallas_call | solution.py:339
  92.7 1.0 collective-permute-start.14
  93.7 2.2 %collective-permute-done.10 = bf16[128,3584]{1,0:T(8,128)(2,1)S(1)} collective-permute-done((bf16[128,3584]{1,0:T(8,128)(2,1)S(1)}, bf16[128,3584]{1,0:T(8,128)(2,1)S(1)}, u32[]{:S(2)}, u32[]{:S(2)}) %collective-permute-start.10) | collective-permute-done | bytes 917536 | tf_op jit(solution)/shard_map/ppermute | solution.py:72
  95.9 1.5 %collective-permute-done.9 = bf16[128,3584]{1,0:T(8,128)(2,1)S(1)} collective-permute-done((bf16[128,3584]{1,0:T(8,128)(2,1)S(1)}, bf16[128,3584]{1,0:T(8,128)(2,1)S(1)}, u32[]{:S(2)}, u32[]{:S(2)}) %collective-permute-start.9) | collective-permute-done | bytes 917536 | tf_op jit(solution)/shard_map/ppermute | solution.py:72
  97.5 6.2 %mlp.4 = bf16[256,3584]{1,0:T(8,128)(2,1)S(1)} custom-call(bf16[256,3584]{1,0:T(8,128)(2,1)S(1)} %pad_maximum_fusion.rows_ref, bf16[6,448,3584]{2,1,0:T(8,128)(2,1)S(1)} %load_weights.1.weights_ref), custom_call_target="tpu_custom_call" | custom-call | flops 4932501504 | bytes 3670016 | tf_op jit(solution)/shard_map/mlp/pallas_call | solution.py:339
  104.0 3.2 %collective-permute-start.11 = (bf16[128,3584]{1,0:T(8,128)(2,1)S(1)}, bf16[128,3584]{1,0:T(8,128)(2,1)S(1)}, u32[]{:S(2)}, u32[]{:S(2)}) collective-permute-start(bf16[128,3584]{1,0:T(8,128)(2,1)S(1)} %get-tuple-element.43), channel_id=1, source_target_pairs={{0,24},{4,100},{8,0},{12,108},{16,8},{20,116},{24,16},{28,124},{32... | collective-permute-start | bytes 2752520 | tf_op jit(solution)/shard_map/ppermute | solution.py:72
  107.2 5.0 %mlp.3 = f32[128,3584]{1,0:T(8,128)S(1)} custom-call(bf16[128,3584]{1,0:T(8,128)(2,1)S(1)} %constant_dynamic-update-slice_fusion.rows_ref, bf16[6,448,3584]{2,1,0:T(8,128)(2,1)S(1)} %load_weights.1.weights_ref), custom_call_target="tpu_custom_call" | custom-call | flops 2466250752 | bytes 1835008 | tf_op jit(solution)/shard_map/mlp/pallas_call | solution.py:339
  112.2 6.4 %collective-permute-done.12 = bf16[128,3584]{1,0:T(8,128)(2,1)S(1)} collective-permute-done((bf16[128,3584]{1,0:T(8,128)(2,1)S(1)}, bf16[128,3584]{1,0:T(8,128)(2,1)S(1)}, u32[]{:S(2)}, u32[]{:S(2)}) %collective-permute-start.12) | collective-permute-done | bytes 917536 | tf_op jit(solution)/shard_map/ppermute | solution.py:72
  119.4 2.4 %collective-permute-start.15 = (bf16[32,3584]{1,0:T(8,128)(2,1)S(1)}, bf16[32,3584]{1,0:T(8,128)(2,1)S(1)}, u32[]{:S(2)}, u32[]{:S(2)}) collective-permute-start(bf16[32,3584]{1,0:T(8,128)(2,1)S(1)} %get-tuple-element.47), channel_id=1, source_target_pairs={{0,96},{4,28},{8,104},{12,4},{16,112},{20,12},{24,120},{28,20},{32... | collective-permute-start | bytes 688136 | tf_op jit(solution)/shard_map/ppermute | solution.py:72
  122.8 5.1 %collective-permute-done.15.b_ref = bf16[32,3584]{1,0:T(8,128)(2,1)S(1)} collective-permute-done((bf16[32,3584]{1,0:T(8,128)(2,1)S(1)}, bf16[32,3584]{1,0:T(8,128)(2,1)S(1)}, u32[]{:S(2)}, u32[]{:S(2)}) %collective-permute-start.15) | collective-permute-done | bytes 229408 | tf_op jit(solution)/shard_map/ppermute | solution.py:72
  127.8 1.6 %collective-permute-done.16.c_ref = bf16[32,3584]{1,0:T(8,128)(2,1)S(1)} collective-permute-done((bf16[32,3584]{1,0:T(8,128)(2,1)S(1)}, bf16[32,3584]{1,0:T(8,128)(2,1)S(1)}, u32[]{:S(2)}, u32[]{:S(2)}) %collective-permute-start.16) | collective-permute-done | bytes 229408 | tf_op jit(solution)/shard_map/ppermute | solution.py:72
  129.4 2.3 %collective-permute-done.17.d_ref = bf16[32,3584]{1,0:T(8,128)(2,1)S(1)} collective-permute-done((bf16[32,3584]{1,0:T(8,128)(2,1)S(1)}, bf16[32,3584]{1,0:T(8,128)(2,1)S(1)}, u32[]{:S(2)}, u32[]{:S(2)}) %collective-permute-start.17) | collective-permute-done | bytes 229408 | tf_op jit(solution)/shard_map/ppermute | solution.py:72
  131.8 0.9 leave.1
  (103 shorter events, 11.7 us)
Async XLA Ops:
  0.6 19.8 %copy-start = (bf16[3584,256]{1,0:T(8,128)(2,1)S(1)}, bf16[3584,256]{1,0:T(8,128)(2,1)}, u32[]{:S(2)}) copy-start(bf16[3584,256]{1,0:T(8,128)(2,1)} %param.27) | copy-start | bytes 5505028
  0.6 46.9 %collective-permute-start = (bf16[448,3584]{1,0:T(8,128)(2,1)}, bf16[448,3584]{1,0:T(8,128)(2,1)}, u32[]{:S(2)}, u32[]{:S(2)}) collective-permute-start(bf16[448,3584]{1,0:T(8,128)(2,1)} %bitcast.24), channel_id=1, source_target_pairs={{0,4},{4,0},{1,5},{5,1},{2,6},{6,2},{3,7},{7,3},{8,12},{12,8},{9,1... | collective-permute-start | bytes 9633800 | tf_op jit(solution)/shard_map/ppermute | solution.py:384
  0.7 46.8 %collective-permute-start.1 = (bf16[448,3584]{1,0:T(8,128)(2,1)}, bf16[448,3584]{1,0:T(8,128)(2,1)}, u32[]{:S(2)}, u32[]{:S(2)}) collective-permute-start(bf16[448,3584]{1,0:T(8,128)(2,1)} %bitcast.26), channel_id=1, source_target_pairs={{0,4},{4,0},{1,5},{5,1},{2,6},{6,2},{3,7},{7,3},{8,12},{12,8},{9,1... | collective-permute-start | bytes 9633800 | tf_op jit(solution)/shard_map/ppermute | solution.py:384
  1.2 46.3 %collective-permute-start.2 = (bf16[448,3584]{1,0:T(8,128)(2,1)}, bf16[448,3584]{1,0:T(8,128)(2,1)}, u32[]{:S(2)}, u32[]{:S(2)}) collective-permute-start(bf16[448,3584]{1,0:T(8,128)(2,1)} %refs_2_), channel_id=1, source_target_pairs={{0,4},{4,0},{1,5},{5,1},{2,6},{6,2},{3,7},{7,3},{8,12},{12,8},{9,1... | collective-permute-start | bytes 9633800 | tf_op jit(solution)/shard_map/ppermute | solution.py:384
  5.0 8.6 %copy-start.14 = (s32[1,128]{1,0:T(1,128)S(1)}, s32[1,128]{1,0:T(1,128)}, u32[]{:S(2)}) copy-start(s32[1,128]{1,0:T(1,128)} %seg_row_ref.1) | copy-start | bytes 1540
  5.0 8.7 %copy-start.22 = (s32[1,64]{1,0:T(1,128)S(1)}, s32[1,64]{1,0:T(1,128)}, u32[]{:S(2)}) copy-start(s32[1,64]{1,0:T(1,128)} %param.21) | copy-start | bytes 772
  5.1 8.8 %copy-start.20 = (s32[1,4]{1,0:T(1,128)S(1)}, s32[1,4]{1,0:T(1,128)}, u32[]{:S(2)}) copy-start(s32[1,4]{1,0:T(1,128)} %param.20) | copy-start | bytes 52
  5.1 9.0 %copy-start.15 = (bf16[128,3584]{1,0:T(8,128)(2,1)S(1)}, bf16[128,3584]{1,0:T(8,128)(2,1)}, u32[]{:S(2)}) copy-start(bf16[128,3584]{1,0:T(8,128)(2,1)} %param.18) | copy-start | bytes 2752516
  5.1 9.5 %copy-start.16 = (f32[3584]{0:T(1024)S(1)}, f32[3584]{0:T(1024)}, u32[]{:S(2)}) copy-start(f32[3584]{0:T(1024)} %param.25) | copy-start | bytes 43012
  5.1 37.4 %all-to-all-start = ((bf16[32,2,64,256]{3,2,1,0:T(8,128)(2,1)}), bf16[32,2,64,256]{3,2,1,0:T(8,128)(2,1)}, u32[]{:S(2)}, u32[]{:S(2)}) async-start(bf16[32,2,64,256]{3,2,1,0:T(8,128)(2,1)} %pick_pages.1), calls=%async_computation | async-start | bytes 4194304 | tf_op jit(solution)/shard_map/all_to_all | solution.py:380
  14.6 5.8 %copy-start.17 = (f32[3584]{0:T(1024)S(1)}, f32[3584]{0:T(1024)}, u32[]{:S(2)}) copy-start(f32[3584]{0:T(1024)} %param.30) | copy-start | bytes 43012
  14.6 5.9 %copy-start.18 = (f32[3584]{0:T(1024)S(1)}, f32[3584]{0:T(1024)}, u32[]{:S(2)}) copy-start(f32[3584]{0:T(1024)} %param.31) | copy-start | bytes 43012
  19.1 4.0 %copy-start.8 = (s32[128,1]{1,0:T(8,128)}, s32[128,1]{1,0:T(8,128)S(1)}, u32[]{:S(2)}) copy-start(s32[128,1]{1,0:T(8,128)S(1)} %copy.37.low_ref.low_hbm) | copy-start | bytes 1540
  22.4 25.1 %copy-start.13 = (bf16[128,256]{1,0:T(8,128)(2,1)}, bf16[128,256]{1,0:T(8,128)(2,1)S(1)}, u32[]{:S(2)}) copy-start(bf16[128,256]{1,0:T(8,128)(2,1)S(1)} %convolution_convert_fusion.new_values_ref) | copy-start | bytes 196612
  42.5 33.2 %copy-start.5 = (bf16[3584,448]{0,1:T(8,128)(2,1)S(1)}, bf16[3584,448]{0,1:T(8,128)(2,1)}, u32[]{:S(2)}) copy-start(bf16[3584,448]{0,1:T(8,128)(2,1)} %param.33) | copy-start | bytes 9633796
  47.5 28.1 %copy-start.4 = (bf16[3584,448]{0,1:T(8,128)(2,1)S(1)}, bf16[3584,448]{0,1:T(8,128)(2,1)}, u32[]{:S(2)}) copy-start(bf16[3584,448]{0,1:T(8,128)(2,1)} %param.32) | copy-start | bytes 9633796
  47.6 12.1 %collective-permute-start.3 = (bf16[32,3584]{1,0:T(8,128)(2,1)S(1)}, bf16[32,3584]{1,0:T(8,128)(2,1)S(1)}, u32[]{:S(2)}, u32[]{:S(2)}) collective-permute-start(bf16[32,3584]{1,0:T(8,128)(2,1)S(1)} %get-tuple-element.28), channel_id=1, source_target_pairs={{0,1},{1,2},{2,3},{3,0},{4,5},{5,6},{6,7},{7,4},{8,9},{9,10},{10,1... | collective-permute-start | bytes 688136 | tf_op jit(solution)/shard_map/ppermute | solution.py:438
  48.9 10.8 %collective-permute-start.4 = (bf16[32,3584]{1,0:T(8,128)(2,1)S(1)}, bf16[32,3584]{1,0:T(8,128)(2,1)S(1)}, u32[]{:S(2)}, u32[]{:S(2)}) collective-permute-start(bf16[32,3584]{1,0:T(8,128)(2,1)S(1)} %get-tuple-element.29), channel_id=1, source_target_pairs={{0,2},{1,3},{2,0},{3,1},{4,6},{5,7},{6,4},{7,5},{8,10},{9,11},{10,... | collective-permute-start | bytes 688136 | tf_op jit(solution)/shard_map/ppermute | solution.py:438
  49.5 12.0 %collective-permute-start.5 = (bf16[32,3584]{1,0:T(8,128)(2,1)S(1)}, bf16[32,3584]{1,0:T(8,128)(2,1)S(1)}, u32[]{:S(2)}, u32[]{:S(2)}) collective-permute-start(bf16[32,3584]{1,0:T(8,128)(2,1)S(1)} %get-tuple-element.30), channel_id=1, source_target_pairs={{0,3},{1,0},{2,1},{3,2},{4,7},{5,4},{6,5},{7,6},{8,11},{9,8},{10,9... | collective-permute-start | bytes 688136 | tf_op jit(solution)/shard_map/ppermute | solution.py:438
  61.9 9.8 %collective-permute-start.6 = (bf16[32,3584]{1,0:T(8,128)(2,1)S(1)}, bf16[32,3584]{1,0:T(8,128)(2,1)S(1)}, u32[]{:S(2)}, u32[]{:S(2)}) collective-permute-start(bf16[32,3584]{1,0:T(8,128)(2,1)S(1)} %get-tuple-element.32), channel_id=1, source_target_pairs={{0,32},{4,12},{8,40},{12,20},{16,48},{20,28},{24,56},{28,4},{32,64... | collective-permute-start | bytes 688136 | tf_op jit(solution)/shard_map/ppermute | solution.py:72
  62.0 9.7 %collective-permute-start.7 = (bf16[32,3584]{1,0:T(8,128)(2,1)S(1)}, bf16[32,3584]{1,0:T(8,128)(2,1)S(1)}, u32[]{:S(2)}, u32[]{:S(2)}) collective-permute-start(bf16[32,3584]{1,0:T(8,128)(2,1)S(1)} %get-tuple-element.32), channel_id=1, source_target_pairs={{0,64},{4,20},{8,72},{12,28},{16,80},{20,4},{24,88},{28,12},{32,96... | collective-permute-start | bytes 688136 | tf_op jit(solution)/shard_map/ppermute | solution.py:72
  64.3 8.3 %collective-permute-start.8 = (bf16[32,3584]{1,0:T(8,128)(2,1)S(1)}, bf16[32,3584]{1,0:T(8,128)(2,1)S(1)}, u32[]{:S(2)}, u32[]{:S(2)}) collective-permute-start(bf16[32,3584]{1,0:T(8,128)(2,1)S(1)} %get-tuple-element.32), channel_id=1, source_target_pairs={{0,96},{4,28},{8,104},{12,4},{16,112},{20,12},{24,120},{28,20},{32... | collective-permute-start | bytes 688136 | tf_op jit(solution)/shard_map/ppermute | solution.py:72
  72.6 15.1 %collective-permute-start.13 = (bf16[128,3584]{1,0:T(8,128)(2,1)S(1)}, bf16[128,3584]{1,0:T(8,128)(2,1)S(1)}, u32[]{:S(2)}, u32[]{:S(2)}) collective-permute-start(bf16[128,3584]{1,0:T(8,128)(2,1)S(1)} %constant_dynamic-update-slice_fusion.rows_ref), channel_id=1, source_target_pairs={{0,16},{4,68},{8,24},{12,76},{16,0},{20,84},{24,8},{28,92},{32,48}... | collective-permute-start | bytes 2752520 | tf_op jit(solution)/shard_map/ppermute | solution.py:72
  73.6 22.3 %collective-permute-start.10 = (bf16[128,3584]{1,0:T(8,128)(2,1)S(1)}, bf16[128,3584]{1,0:T(8,128)(2,1)S(1)}, u32[]{:S(2)}, u32[]{:S(2)}) collective-permute-start(bf16[128,3584]{1,0:T(8,128)(2,1)S(1)} %constant_dynamic-update-slice_fusion.rows_ref), channel_id=1, source_target_pairs={{0,24},{4,100},{8,0},{12,108},{16,8},{20,116},{24,16},{28,124},{32... | collective-permute-start | bytes 2752520 | tf_op jit(solution)/shard_map/ppermute | solution.py:72
  75.1 22.3 %collective-permute-start.9 = (bf16[128,3584]{1,0:T(8,128)(2,1)S(1)}, bf16[128,3584]{1,0:T(8,128)(2,1)S(1)}, u32[]{:S(2)}, u32[]{:S(2)}) collective-permute-start(bf16[128,3584]{1,0:T(8,128)(2,1)S(1)} %constant_dynamic-update-slice_fusion.rows_ref), channel_id=1, source_target_pairs={{0,8},{4,36},{8,16},{12,44},{16,24},{20,52},{24,0},{28,60},{32,40}... | collective-permute-start | bytes 2752520 | tf_op jit(solution)/shard_map/ppermute | solution.py:72
  92.7 19.5 %collective-permute-start.14 = (bf16[128,3584]{1,0:T(8,128)(2,1)S(1)}, bf16[128,3584]{1,0:T(8,128)(2,1)S(1)}, u32[]{:S(2)}, u32[]{:S(2)}) collective-permute-start(bf16[128,3584]{1,0:T(8,128)(2,1)S(1)} %mlp.5), channel_id=1, source_target_pairs={{0,16},{4,68},{8,24},{12,76},{16,0},{20,84},{24,8},{28,92},{32,48}... | collective-permute-start | bytes 2752520 | tf_op jit(solution)/shard_map/ppermute | solution.py:72
  103.9 14.7 %collective-permute-start.12 = (bf16[128,3584]{1,0:T(8,128)(2,1)S(1)}, bf16[128,3584]{1,0:T(8,128)(2,1)S(1)}, u32[]{:S(2)}, u32[]{:S(2)}) collective-permute-start(bf16[128,3584]{1,0:T(8,128)(2,1)S(1)} %get-tuple-element.44), channel_id=1, source_target_pairs={{0,8},{4,36},{8,16},{12,44},{16,24},{20,52},{24,0},{28,60},{32,40}... | collective-permute-start | bytes 2752520 | tf_op jit(solution)/shard_map/ppermute | solution.py:72
  104.0 14.9 %collective-permute-start.11 = (bf16[128,3584]{1,0:T(8,128)(2,1)S(1)}, bf16[128,3584]{1,0:T(8,128)(2,1)S(1)}, u32[]{:S(2)}, u32[]{:S(2)}) collective-permute-start(bf16[128,3584]{1,0:T(8,128)(2,1)S(1)} %get-tuple-element.43), channel_id=1, source_target_pairs={{0,24},{4,100},{8,0},{12,108},{16,8},{20,116},{24,16},{28,124},{32... | collective-permute-start | bytes 2752520 | tf_op jit(solution)/shard_map/ppermute | solution.py:72
  118.9 13.8 %copy-start.1 = (bf16[3584,256]{1,0:T(8,128)(2,1)S(1)}, bf16[3584,256]{1,0:T(8,128)(2,1)}, u32[]{:S(2)}) copy-start(bf16[3584,256]{1,0:T(8,128)(2,1)} %param.27) | copy-start | bytes 5505028
  119.4 8.4 %collective-permute-start.15 = (bf16[32,3584]{1,0:T(8,128)(2,1)S(1)}, bf16[32,3584]{1,0:T(8,128)(2,1)S(1)}, u32[]{:S(2)}, u32[]{:S(2)}) collective-permute-start(bf16[32,3584]{1,0:T(8,128)(2,1)S(1)} %get-tuple-element.47), channel_id=1, source_target_pairs={{0,96},{4,28},{8,104},{12,4},{16,112},{20,12},{24,120},{28,20},{32... | collective-permute-start | bytes 688136 | tf_op jit(solution)/shard_map/ppermute | solution.py:72
  121.8 7.6 %collective-permute-start.16 = (bf16[32,3584]{1,0:T(8,128)(2,1)S(1)}, bf16[32,3584]{1,0:T(8,128)(2,1)S(1)}, u32[]{:S(2)}, u32[]{:S(2)}) collective-permute-start(bf16[32,3584]{1,0:T(8,128)(2,1)S(1)} %get-tuple-element.46), channel_id=1, source_target_pairs={{0,64},{4,20},{8,72},{12,28},{16,80},{20,4},{24,88},{28,12},{32,96... | collective-permute-start | bytes 688136 | tf_op jit(solution)/shard_map/ppermute | solution.py:72
  122.1 9.7 %collective-permute-start.17 = (bf16[32,3584]{1,0:T(8,128)(2,1)S(1)}, bf16[32,3584]{1,0:T(8,128)(2,1)S(1)}, u32[]{:S(2)}, u32[]{:S(2)}) collective-permute-start(bf16[32,3584]{1,0:T(8,128)(2,1)S(1)} %get-tuple-element.45), channel_id=1, source_target_pairs={{0,32},{4,12},{8,40},{12,20},{16,48},{20,28},{24,56},{28,4},{32,64... | collective-permute-start | bytes 688136 | tf_op jit(solution)/shard_map/ppermute | solution.py:72
  (10 other events, 20.5 us)

commit v5 on v4

--- a/solution.py
+++ b/solution.py
@@ -154,21 +154,14 @@
     )(*weights)
 
 
-def weights_of(query, keys, visible):
+def attend(query, keys, values, visible, acc_ref, total_ref):
     scores = lax.dot_general(
         query, keys, (((1,), (1,)), ((), ())), preferred_element_type=F32
     )
     raw = jnp.exp(SOFT_CAP * jnp.tanh(scores * (1.0 / (16.0 * SOFT_CAP))))
-    return jnp.where(visible, raw, 0.0)
-
-
-def attend(query_ref, keys, values, visible, acc_ref, total_ref):
-    for h in range(HEADS):
-        weight = weights_of(query_ref[h], keys, visible)
-        total_ref[h] += jnp.broadcast_to(
-            jnp.sum(weight, axis=-1, keepdims=True), total_ref.shape[1:]
-        )
-        acc_ref[h] += jnp.dot(weight.astype(BF16), values, preferred_element_type=F32)
+    weight = jnp.where(jnp.concatenate([visible] * HEADS, axis=0), raw, 0.0)
+    total_ref[...] += jnp.broadcast_to(jnp.sum(weight, axis=-1, keepdims=True), total_ref.shape)
+    acc_ref[...] += jnp.dot(weight.astype(BF16), values, preferred_element_type=F32)
 
 
 STEP_PAGES = 8
@@ -183,12 +176,12 @@
     count = order.shape[0]
     column = lax.broadcasted_iota(jnp.int32, (count, count), 1)
     same = lax.div(high, 4096) == seg_row_ref[...]
-    attend(query_ref, new_keys_ref[...], new_values_ref[...], same & (column <= order), acc_ref, total_ref)
+    attend(query_ref[...], new_keys_ref[...], new_values_ref[...], same & (column <= order), acc_ref, total_ref)
     for b in range(POOL // STEP_PAGES):
         keys = keys_ref[b * STEP_PAGES:(b + 1) * STEP_PAGES].reshape(STEP, HEAD_SIZE)
         values = values_ref[b * STEP_PAGES:(b + 1) * STEP_PAGES].reshape(STEP, HEAD_SIZE)
         code = code_ref[:, b * STEP:(b + 1) * STEP]
-        attend(query_ref, keys, values, (code > low) & (code < high), acc_ref, total_ref)
+        attend(query_ref[...], keys, values, (code > low) & (code < high), acc_ref, total_ref)
 
 
 def own_attention(low, high, order, seg_row, query, new_keys, new_values, code, keys, values):
@@ -196,8 +189,8 @@
     return pl.pallas_call(
         own_kernel,
         out_shape=(
-            jax.ShapeDtypeStruct((HEADS, 128, HEAD_SIZE), F32),
-            jax.ShapeDtypeStruct((HEADS, 128, 128), F32),
+            jax.ShapeDtypeStruct((HEADS * 128, HEAD_SIZE), F32),
+            jax.ShapeDtypeStruct((HEADS * 128, 128), F32),
         ),
         in_specs=[vmem] * 10,
         out_specs=(vmem, vmem),
@@ -247,14 +240,13 @@
         keys = held_ref[b, :, 0].reshape(STEP, HEAD_SIZE)
         values = held_ref[b, :, 1].reshape(STEP, HEAD_SIZE)
         code = code_ref[:, b * STEP:(b + 1) * STEP]
-        attend(query_ref, keys, values, (code > low) & (code < high), acc_ref, total_ref)
+        attend(query_ref[...], keys, values, (code > low) & (code < high), acc_ref, total_ref)
     acc_load.wait()
     total_load.wait()
-    heads = [
-        ((acc_ref[h] + acc_in_ref[h]) / (total_ref[h] + total_in_ref[h])[:, :1]).astype(BF16)
-        for h in range(HEADS)
-    ]
-    attention = jnp.concatenate(heads, axis=1)
+    heads = (
+        (acc_ref[...] + acc_in_ref[...]) / (total_ref[...] + total_in_ref[...])[:, :1]
+    ).astype(BF16)
+    attention = jnp.concatenate([heads[h * 128:(h + 1) * 128] for h in range(HEADS)], axis=1)
     rows, width = out_refs[0].shape
     w_load.wait()
     for n in range(0, width, 512):
@@ -275,11 +267,11 @@
         in_specs=[hbm] * 8,
         out_specs=[vmem] * blocks,
         scratch_shapes=[
-            pltpu.VMEM((HEADS, 128, HEAD_SIZE), F32),
-            pltpu.VMEM((HEADS, 128, 128), F32),
-            pltpu.VMEM((HEADS, 128, HEAD_SIZE), BF16),
-            pltpu.VMEM((HEADS, 128, HEAD_SIZE), F32),
-            pltpu.VMEM((HEADS, 128, 128), F32),
+            pltpu.VMEM((HEADS * 128, HEAD_SIZE), F32),
+            pltpu.VMEM((HEADS * 128, 128), F32),
+            pltpu.VMEM((HEADS * 128, HEAD_SIZE), BF16),
+            pltpu.VMEM((HEADS * 128, HEAD_SIZE), F32),
+            pltpu.VMEM((HEADS * 128, 128), F32),
             pltpu.VMEM((OWNERS // STEP_PAGES, STEP_PAGES, 2, PAGE, HEAD_SIZE), BF16),
             pltpu.VMEM(w_out.shape, BF16),
             pltpu.VMEM(low.shape, jnp.int32),
@@ -377,12 +369,11 @@
     other = [(0, 1), (1, 0)]
 
     packed = pick_pages(migrate_pages.reshape(-1), pooled_key_cache, pooled_value_cache)
+
+    gate, up = w_gate.T, w_up.T
+    packed, *sent = lax.optimization_barrier((packed, gate, up, w_down))
     received = lax.all_to_all(packed, REQ, split_axis=0, concat_axis=0, tiled=True)
-
-    gate, up = w_gate.T, w_up.T
-    weights = (gate, up, w_down) + tuple(
-        lax.ppermute(w, "core", other) for w in (gate, up, w_down)
-    )
+    weights = (gate, up, w_down) + tuple(lax.ppermute(w, "core", other) for w in sent)
 
     segment = segment_ids[0]
     past = past_len[0]
@@ -422,7 +413,7 @@
     turn = lambda v: lax.dynamic_slice_in_dim(jnp.concatenate([v, v], 0), here * ROWS, tok_count, 0)
     low = turn(segment * 4096 + offsets)[:, None]
     high = turn(segment * 4096 + WINDOW_LENGTH)[:, None]
-    query = turn(query_rows).transpose(1, 0, 2)
+    query = turn(query_rows).transpose(1, 0, 2).reshape(HEADS * tok_count, HEAD_SIZE)
     own_rows = lax.dynamic_slice_in_dim(tokens, here * ROWS, ROWS, 0)
 
     acc, total = own_attention(

time: 133 us -> 133 us (level)
  local copies, waits for them, and re-layouts: 6.91 us -> 3.47 us
  waiting for transfers between devices: 58.1 us -> 61.4 us
    all_to_all x1, waiting for transfers between devices: 15.5 us -> 18.9 us  [local(): lax.all_to_all(packed, REQ, split_axis=0, concat_axis=0, tiled=True)]
    unnamed x51 -> x43, local copies, waits for them, and re-layouts: 4.92 us -> 1.88 us
    pallas_call x1, Pallas kernels: 4.75 us -> 6.6 us  [load_weights(): pl.pallas_call(load_kernel, out_shape=pltpu.VMEM((count, units, width), B...]
  transfers between devices with their start and end apart: 19 -> 19, of which waited for: 13 -> 13; matrix products, arithmetic and copies ran while one was open for 7% -> 5% of each run, Pallas kernels for 24% -> 22%
where the time goes in v5:
time: 133 us; the launch traced here: 132 us
  waiting for transfers between devices  61.4 us (46%)
  Pallas kernels  33.8 us (25%)
  starting transfers between devices  26.5 us (20%)
  matrix products  3.64 us (3%)
  local copies, waits for them, and re-layouts  3.47 us (3%)
  other arithmetic  2.18 us (2%)
    ppermute x12, waiting for transfers between devices, shift(): return lax.ppermute(value, REQ, chip_shift(first, k % 4))  31.6 us
    all_to_all x1, waiting for transfers between devices, local(): lax.all_to_all(packed, REQ, split_axis=0, concat_axis=0, tiled=True)  18.9 us
    pallas_call x3, Pallas kernels, mlp(): pl.pallas_call(mlp_kernel, out_shape=jax.ShapeDtypeStruct((count, width),...  16.4 us
    ppermute x12, starting transfers between devices, shift(): return lax.ppermute(value, REQ, chip_shift(first, k % 4))  14.4 us
    ppermute x3, waiting for transfers between devices, local(): lax.ppermute(parts[k], 'mlp', [(i, (i + k) % 4) for i in range(4)])  10.9 us
    all_to_all x1, starting transfers between devices, local(): lax.all_to_all(packed, REQ, split_axis=0, concat_axis=0, tiled=True)  8.33 us
    pallas_call x1, Pallas kernels, load_weights(): pl.pallas_call(load_kernel, out_shape=pltpu.VMEM((count, units, width), B...  6.6 us
    pallas_call x1, Pallas kernels, far_attention(): pl.pallas_call(far_kernel, out_shape=[pltpu.VMEM((128 // blocks, width),...  4.5 us
  transfers between devices with their start and end apart: 19, of which 13 were waited for; matrix products, arithmetic and copies ran while one was open for 5% of the time, Pallas kernels for 22%

profile of v5, /device:TPU:16, one launch (start us, length us, event | category | flops | bytes accessed | tf_op | source)
XLA Modules:
  0.0 132.1 jit_solution(8514416676822903172)
XLA Ops:
  0.6 3.7 %pick_pages.1 = bf16[32,2,64,256]{3,2,1,0:T(8,128)(2,1)} custom-call(s32[32]{0:T(128)} %bitcast.28, bf16[32,64,256]{2,1,0:T(8,128)(2,1)} %keys_ref.3, bf16[32,64,256]{2,1,0:T(8,128)(2,1)} %values_ref.3), custom_call_target="tpu_custom_call" | custom-call | tf_op jit(solution)/shard_map/pick_pages/pallas_call | solution.py:108
  5.1 8.3 %all-to-all-start = ((bf16[32,2,64,256]{3,2,1,0:T(8,128)(2,1)}), bf16[32,2,64,256]{3,2,1,0:T(8,128)(2,1)}, u32[]{:S(2)}, u32[]{:S(2)}) async-start(bf16[32,2,64,256]{3,2,1,0:T(8,128)(2,1)} %pick_pages.1), calls=%async_computation | async-start | bytes 4194304 | tf_op jit(solution)/shard_map/all_to_all | solution.py:375
  14.9 2.7 %fusion.25 = f32[128,512]{1,0:T(8,128)S(1)} fusion(bf16[3584,512]{1,0:T(8,128)(2,1)} %param.26, bf16[128,3584]{1,0:T(8,128)(2,1)S(1)} %copy-done.12, f32[3584]{0:T(1024)S(1)} %copy-done.18, f32[128]{0:T(128)S(1)} %add_rsqrt_fusion), kind=kOutput, calls=%fused_computation.75 | convolution fusion | flops 471597056 | bytes 4864512 | tf_op jit(solution)/shard_map/dot_general | solution.py:383
  20.8 1.3 own_attention.1
  22.1 0.7 copy-done.7
  23.5 18.9 %all-to-all-done.pages_ref = bf16[32,2,64,256]{3,2,1,0:T(8,128)(2,1)} async-done(((bf16[32,2,64,256]{3,2,1,0:T(8,128)(2,1)}), bf16[32,2,64,256]{3,2,1,0:T(8,128)(2,1)}, u32[]{:S(2)}, u32[]{:S(2)}) %all-to-all-start) | async-done | bytes 2097184 | tf_op jit(solution)/shard_map/all_to_all | solution.py:375
  42.4 4.5 %far_attention.1 = (bf16[32,3584]{1,0:T(8,128)(2,1)S(1)}, bf16[32,3584]{1,0:T(8,128)(2,1)S(1)}, bf16[32,3584]{1,0:T(8,128)(2,1)S(1)}, bf16[32,3584]{1,0:T(8,128)(2,1)S(1)}) custom-call(s32[128,1]{1,0:T(8,128)} %copy-done.5, s32[128,1]{1,0:T(8,128)} %copy-done.6, s32[1,2048]{1,0:T(1,128)} %get-tuple-element.64.code_hbm, bf16[256,256]{1,0:T(8,128)(2,1)} %bitcast.25, ...), custom_call_target="tpu_custom_call" | custom-call | flops 536870912 | bytes 7000000 | tf_op jit(solution)/shard_map/far_attention/pallas_call | solution.py:264
  46.9 1.4 %collective-permute-start.3 = (bf16[32,3584]{1,0:T(8,128)(2,1)S(1)}, bf16[32,3584]{1,0:T(8,128)(2,1)S(1)}, u32[]{:S(2)}, u32[]{:S(2)}) collective-permute-start(bf16[32,3584]{1,0:T(8,128)(2,1)S(1)} %get-tuple-element.36), channel_id=1, source_target_pairs={{0,1},{1,2},{2,3},{3,0},{4,5},{5,6},{6,7},{7,4},{8,9},{9,10},{10,1... | collective-permute-start | bytes 688136 | tf_op jit(solution)/shard_map/ppermute | solution.py:429
  48.9 1.1 collective-permute-start.5
  50.0 9.1 %collective-permute-done.3.b_ref = bf16[32,3584]{1,0:T(8,128)(2,1)S(1)} collective-permute-done((bf16[32,3584]{1,0:T(8,128)(2,1)S(1)}, bf16[32,3584]{1,0:T(8,128)(2,1)S(1)}, u32[]{:S(2)}, u32[]{:S(2)}) %collective-permute-start.3) | collective-permute-done | bytes 229408 | tf_op jit(solution)/shard_map/ppermute | solution.py:429
  59.1 1.8 %collective-permute-done.5.d_ref = bf16[32,3584]{1,0:T(8,128)(2,1)S(1)} collective-permute-done((bf16[32,3584]{1,0:T(8,128)(2,1)S(1)}, bf16[32,3584]{1,0:T(8,128)(2,1)S(1)}, u32[]{:S(2)}, u32[]{:S(2)}) %collective-permute-start.5) | collective-permute-done | bytes 229408 | tf_op jit(solution)/shard_map/ppermute | solution.py:429
  61.4 2.3 %collective-permute-start.7 = (bf16[32,3584]{1,0:T(8,128)(2,1)S(1)}, bf16[32,3584]{1,0:T(8,128)(2,1)S(1)}, u32[]{:S(2)}, u32[]{:S(2)}) collective-permute-start(bf16[32,3584]{1,0:T(8,128)(2,1)S(1)} %get-tuple-element.40), channel_id=1, source_target_pairs={{0,64},{4,20},{8,72},{12,28},{16,80},{20,4},{24,88},{28,12},{32,96... | collective-permute-start | bytes 688136 | tf_op jit(solution)/shard_map/ppermute | solution.py:72
  63.7 1.4 %collective-permute-start.8 = (bf16[32,3584]{1,0:T(8,128)(2,1)S(1)}, bf16[32,3584]{1,0:T(8,128)(2,1)S(1)}, u32[]{:S(2)}, u32[]{:S(2)}) collective-permute-start(bf16[32,3584]{1,0:T(8,128)(2,1)S(1)} %get-tuple-element.40), channel_id=1, source_target_pairs={{0,96},{4,28},{8,104},{12,4},{16,112},{20,12},{24,120},{28,20},{32... | collective-permute-start | bytes 688136 | tf_op jit(solution)/shard_map/ppermute | solution.py:72
  65.1 5.9 %collective-permute-done.6 = bf16[32,3584]{1,0:T(8,128)(2,1)S(1)} collective-permute-done((bf16[32,3584]{1,0:T(8,128)(2,1)S(1)}, bf16[32,3584]{1,0:T(8,128)(2,1)S(1)}, u32[]{:S(2)}, u32[]{:S(2)}) %collective-permute-start.6) | collective-permute-done | bytes 229408 | tf_op jit(solution)/shard_map/ppermute | solution.py:72
  71.1 0.8 collective-permute-done.8
  72.0 1.0 collective-permute-start.13
  73.0 1.5 %collective-permute-start.10 = (bf16[128,3584]{1,0:T(8,128)(2,1)S(1)}, bf16[128,3584]{1,0:T(8,128)(2,1)S(1)}, u32[]{:S(2)}, u32[]{:S(2)}) collective-permute-start(bf16[128,3584]{1,0:T(8,128)(2,1)S(1)} %constant_dynamic-update-slice_fusion.rows_ref), channel_id=1, source_target_pairs={{0,24},{4,100},{8,0},{12,108},{16,8},{20,116},{24,16},{28,124},{32... | collective-permute-start | bytes 2752520 | tf_op jit(solution)/shard_map/ppermute | solution.py:72
  75.0 6.6 %load_weights.1.weights_ref = bf16[6,448,3584]{2,1,0:T(8,128)(2,1)S(1)} custom-call(bf16[448,3584]{1,0:T(8,128)(2,1)} %bitcast.refs_0_, bf16[448,3584]{1,0:T(8,128)(2,1)} %bitcast.1.refs_1_, bf16[448,3584]{1,0:T(8,128)(2,1)} %refs_2_, bf16[448,3584]{1,0:T(8,128)(2,1)} %collective-permute-done.refs_3_, bf16[448,3584]{1,0:T(8,128)(2,1)} %collective-permute-done.1.refs_4_, ...), custom_call_target="tpu_custom_call" | custom-call | bytes 19267584 | tf_op jit(solution)/shard_map/load_weights/pallas_call | solution.py:143
  81.6 5.5 %collective-permute-done.13.rows_ref = bf16[128,3584]{1,0:T(8,128)(2,1)S(1)} collective-permute-done((bf16[128,3584]{1,0:T(8,128)(2,1)S(1)}, bf16[128,3584]{1,0:T(8,128)(2,1)S(1)}, u32[]{:S(2)}, u32[]{:S(2)}) %collective-permute-start.13) | collective-permute-done | bytes 917536 | tf_op jit(solution)/shard_map/ppermute | solution.py:72
  87.1 5.1 %mlp.5 = bf16[128,3584]{1,0:T(8,128)(2,1)S(1)} custom-call(bf16[128,3584]{1,0:T(8,128)(2,1)S(1)} %collective-permute-done.13.rows_ref, bf16[6,448,3584]{2,1,0:T(8,128)(2,1)S(1)} %load_weights.1.weights_ref), custom_call_target="tpu_custom_call" | custom-call | flops 2466250752 | bytes 1835008 | tf_op jit(solution)/shard_map/mlp/pallas_call | solution.py:331
  92.1 1.0 collective-permute-start.14
  93.1 2.2 %collective-permute-done.10 = bf16[128,3584]{1,0:T(8,128)(2,1)S(1)} collective-permute-done((bf16[128,3584]{1,0:T(8,128)(2,1)S(1)}, bf16[128,3584]{1,0:T(8,128)(2,1)S(1)}, u32[]{:S(2)}, u32[]{:S(2)}) %collective-permute-start.10) | collective-permute-done | bytes 917536 | tf_op jit(solution)/shard_map/ppermute | solution.py:72
  95.3 1.5 %collective-permute-done.9 = bf16[128,3584]{1,0:T(8,128)(2,1)S(1)} collective-permute-done((bf16[128,3584]{1,0:T(8,128)(2,1)S(1)}, bf16[128,3584]{1,0:T(8,128)(2,1)S(1)}, u32[]{:S(2)}, u32[]{:S(2)}) %collective-permute-start.9) | collective-permute-done | bytes 917536 | tf_op jit(solution)/shard_map/ppermute | solution.py:72
  96.9 6.3 %mlp.4 = bf16[256,3584]{1,0:T(8,128)(2,1)S(1)} custom-call(bf16[256,3584]{1,0:T(8,128)(2,1)S(1)} %pad_maximum_fusion.rows_ref, bf16[6,448,3584]{2,1,0:T(8,128)(2,1)S(1)} %load_weights.1.weights_ref), custom_call_target="tpu_custom_call" | custom-call | flops 4932501504 | bytes 3670016 | tf_op jit(solution)/shard_map/mlp/pallas_call | solution.py:331
  103.4 3.2 %collective-permute-start.11 = (bf16[128,3584]{1,0:T(8,128)(2,1)S(1)}, bf16[128,3584]{1,0:T(8,128)(2,1)S(1)}, u32[]{:S(2)}, u32[]{:S(2)}) collective-permute-start(bf16[128,3584]{1,0:T(8,128)(2,1)S(1)} %get-tuple-element.51), channel_id=1, source_target_pairs={{0,24},{4,100},{8,0},{12,108},{16,8},{20,116},{24,16},{28,124},{32... | collective-permute-start | bytes 2752520 | tf_op jit(solution)/shard_map/ppermute | solution.py:72
  106.6 5.0 %mlp.3 = f32[128,3584]{1,0:T(8,128)S(1)} custom-call(bf16[128,3584]{1,0:T(8,128)(2,1)S(1)} %constant_dynamic-update-slice_fusion.rows_ref, bf16[6,448,3584]{2,1,0:T(8,128)(2,1)S(1)} %load_weights.1.weights_ref), custom_call_target="tpu_custom_call" | custom-call | flops 2466250752 | bytes 1835008 | tf_op jit(solution)/shard_map/mlp/pallas_call | solution.py:331
  111.7 6.3 %collective-permute-done.12 = bf16[128,3584]{1,0:T(8,128)(2,1)S(1)} collective-permute-done((bf16[128,3584]{1,0:T(8,128)(2,1)S(1)}, bf16[128,3584]{1,0:T(8,128)(2,1)S(1)}, u32[]{:S(2)}, u32[]{:S(2)}) %collective-permute-start.12) | collective-permute-done | bytes 917536 | tf_op jit(solution)/shard_map/ppermute | solution.py:72
  118.8 2.4 %collective-permute-start.15 = (bf16[32,3584]{1,0:T(8,128)(2,1)S(1)}, bf16[32,3584]{1,0:T(8,128)(2,1)S(1)}, u32[]{:S(2)}, u32[]{:S(2)}) collective-permute-start(bf16[32,3584]{1,0:T(8,128)(2,1)S(1)} %get-tuple-element.55), channel_id=1, source_target_pairs={{0,96},{4,28},{8,104},{12,4},{16,112},{20,12},{24,120},{28,20},{32... | collective-permute-start | bytes 688136 | tf_op jit(solution)/shard_map/ppermute | solution.py:72
  122.2 5.1 %collective-permute-done.15.b_ref = bf16[32,3584]{1,0:T(8,128)(2,1)S(1)} collective-permute-done((bf16[32,3584]{1,0:T(8,128)(2,1)S(1)}, bf16[32,3584]{1,0:T(8,128)(2,1)S(1)}, u32[]{:S(2)}, u32[]{:S(2)}) %collective-permute-start.15) | collective-permute-done | bytes 229408 | tf_op jit(solution)/shard_map/ppermute | solution.py:72
  127.2 1.6 %collective-permute-done.16.c_ref = bf16[32,3584]{1,0:T(8,128)(2,1)S(1)} collective-permute-done((bf16[32,3584]{1,0:T(8,128)(2,1)S(1)}, bf16[32,3584]{1,0:T(8,128)(2,1)S(1)}, u32[]{:S(2)}, u32[]{:S(2)}) %collective-permute-start.16) | collective-permute-done | bytes 229408 | tf_op jit(solution)/shard_map/ppermute | solution.py:72
  128.8 2.4 %collective-permute-done.17.d_ref = bf16[32,3584]{1,0:T(8,128)(2,1)S(1)} collective-permute-done((bf16[32,3584]{1,0:T(8,128)(2,1)S(1)}, bf16[32,3584]{1,0:T(8,128)(2,1)S(1)}, u32[]{:S(2)}, u32[]{:S(2)}) %collective-permute-start.17) | collective-permute-done | bytes 229408 | tf_op jit(solution)/shard_map/ppermute | solution.py:72
  131.2 0.9 leave.1
  (96 shorter events, 9.6 us)
Async XLA Ops:
  0.6 17.3 %copy-start = (bf16[3584,256]{1,0:T(8,128)(2,1)S(1)}, bf16[3584,256]{1,0:T(8,128)(2,1)}, u32[]{:S(2)}) copy-start(bf16[3584,256]{1,0:T(8,128)(2,1)} %param.27) | copy-start | bytes 5505028
  4.4 9.1 %copy-start.11 = (s32[1,128]{1,0:T(1,128)S(1)}, s32[1,128]{1,0:T(1,128)}, u32[]{:S(2)}) copy-start(s32[1,128]{1,0:T(1,128)} %seg_row_ref.1) | copy-start | bytes 1540
  4.4 9.2 %copy-start.16 = (s32[1,4]{1,0:T(1,128)S(1)}, s32[1,4]{1,0:T(1,128)}, u32[]{:S(2)}) copy-start(s32[1,4]{1,0:T(1,128)} %param.20) | copy-start | bytes 52
  4.4 9.7 %copy-start.19 = (s32[1,64]{1,0:T(1,128)S(1)}, s32[1,64]{1,0:T(1,128)}, u32[]{:S(2)}) copy-start(s32[1,64]{1,0:T(1,128)} %param.21) | copy-start | bytes 772
  4.4 10.1 %copy-start.12 = (bf16[128,3584]{1,0:T(8,128)(2,1)S(1)}, bf16[128,3584]{1,0:T(8,128)(2,1)}, u32[]{:S(2)}) copy-start(bf16[128,3584]{1,0:T(8,128)(2,1)} %param.18) | copy-start | bytes 2752516
  4.4 10.4 %copy-start.18 = (f32[3584]{0:T(1024)S(1)}, f32[3584]{0:T(1024)}, u32[]{:S(2)}) copy-start(f32[3584]{0:T(1024)} %param.25) | copy-start | bytes 43012
  4.4 42.4 %collective-permute-start = (bf16[448,3584]{1,0:T(8,128)(2,1)}, bf16[448,3584]{1,0:T(8,128)(2,1)}, u32[]{:S(2)}, u32[]{:S(2)}) collective-permute-start(bf16[448,3584]{1,0:T(8,128)(2,1)} %bitcast.refs_0_), channel_id=1, source_target_pairs={{0,4},{4,0},{1,5},{5,1},{2,6},{6,2},{3,7},{7,3},{8,12},{12,8},{9,1... | collective-permute-start | bytes 9633800 | tf_op jit(solution)/shard_map/ppermute | solution.py:376
  4.5 42.4 %collective-permute-start.1 = (bf16[448,3584]{1,0:T(8,128)(2,1)}, bf16[448,3584]{1,0:T(8,128)(2,1)}, u32[]{:S(2)}, u32[]{:S(2)}) collective-permute-start(bf16[448,3584]{1,0:T(8,128)(2,1)} %bitcast.1.refs_1_), channel_id=1, source_target_pairs={{0,4},{4,0},{1,5},{5,1},{2,6},{6,2},{3,7},{7,3},{8,12},{12,8},{9,1... | collective-permute-start | bytes 9633800 | tf_op jit(solution)/shard_map/ppermute | solution.py:376
  5.0 41.9 %collective-permute-start.2 = (bf16[448,3584]{1,0:T(8,128)(2,1)}, bf16[448,3584]{1,0:T(8,128)(2,1)}, u32[]{:S(2)}, u32[]{:S(2)}) collective-permute-start(bf16[448,3584]{1,0:T(8,128)(2,1)} %refs_2_), channel_id=1, source_target_pairs={{0,4},{4,0},{1,5},{5,1},{2,6},{6,2},{3,7},{7,3},{8,12},{12,8},{9,1... | collective-permute-start | bytes 9633800 | tf_op jit(solution)/shard_map/ppermute | solution.py:376
  5.1 37.2 %all-to-all-start = ((bf16[32,2,64,256]{3,2,1,0:T(8,128)(2,1)}), bf16[32,2,64,256]{3,2,1,0:T(8,128)(2,1)}, u32[]{:S(2)}, u32[]{:S(2)}) async-start(bf16[32,2,64,256]{3,2,1,0:T(8,128)(2,1)} %pick_pages.1), calls=%async_computation | async-start | bytes 4194304 | tf_op jit(solution)/shard_map/all_to_all | solution.py:375
  13.9 6.6 %copy-start.5 = (s32[128,1]{1,0:T(8,128)}, s32[128,1]{1,0:T(8,128)S(1)}, u32[]{:S(2)}) copy-start(s32[128,1]{1,0:T(8,128)S(1)} %copy.31.low_ref.low_hbm) | copy-start | bytes 1540
  14.1 6.4 %copy-start.6 = (s32[128,1]{1,0:T(8,128)}, s32[128,1]{1,0:T(8,128)S(1)}, u32[]{:S(2)}) copy-start(s32[128,1]{1,0:T(8,128)S(1)} %copy.32.high_ref.high_hbm) | copy-start | bytes 1540
  14.8 2.9 %copy-start.13 = (f32[3584]{0:T(1024)S(1)}, f32[3584]{0:T(1024)}, u32[]{:S(2)}) copy-start(f32[3584]{0:T(1024)} %param.30) | copy-start | bytes 43012
  14.8 3.0 %copy-start.14 = (f32[3584]{0:T(1024)S(1)}, f32[3584]{0:T(1024)}, u32[]{:S(2)}) copy-start(f32[3584]{0:T(1024)} %param.31) | copy-start | bytes 43012
  19.9 27.0 %copy-start.10 = (bf16[128,256]{1,0:T(8,128)(2,1)}, bf16[128,256]{1,0:T(8,128)(2,1)S(1)}, u32[]{:S(2)}) copy-start(bf16[128,256]{1,0:T(8,128)(2,1)S(1)} %convolution_convert_fusion.new_values_ref) | copy-start | bytes 196612
  46.9 12.1 %collective-permute-start.3 = (bf16[32,3584]{1,0:T(8,128)(2,1)S(1)}, bf16[32,3584]{1,0:T(8,128)(2,1)S(1)}, u32[]{:S(2)}, u32[]{:S(2)}) collective-permute-start(bf16[32,3584]{1,0:T(8,128)(2,1)S(1)} %get-tuple-element.36), channel_id=1, source_target_pairs={{0,1},{1,2},{2,3},{3,0},{4,5},{5,6},{6,7},{7,4},{8,9},{9,10},{10,1... | collective-permute-start | bytes 688136 | tf_op jit(solution)/shard_map/ppermute | solution.py:429
  48.3 10.8 %collective-permute-start.4 = (bf16[32,3584]{1,0:T(8,128)(2,1)S(1)}, bf16[32,3584]{1,0:T(8,128)(2,1)S(1)}, u32[]{:S(2)}, u32[]{:S(2)}) collective-permute-start(bf16[32,3584]{1,0:T(8,128)(2,1)S(1)} %get-tuple-element.37), channel_id=1, source_target_pairs={{0,2},{1,3},{2,0},{3,1},{4,6},{5,7},{6,4},{7,5},{8,10},{9,11},{10,... | collective-permute-start | bytes 688136 | tf_op jit(solution)/shard_map/ppermute | solution.py:429
  48.9 12.0 %collective-permute-start.5 = (bf16[32,3584]{1,0:T(8,128)(2,1)S(1)}, bf16[32,3584]{1,0:T(8,128)(2,1)S(1)}, u32[]{:S(2)}, u32[]{:S(2)}) collective-permute-start(bf16[32,3584]{1,0:T(8,128)(2,1)S(1)} %get-tuple-element.38), channel_id=1, source_target_pairs={{0,3},{1,0},{2,1},{3,2},{4,7},{5,4},{6,5},{7,6},{8,11},{9,8},{10,9... | collective-permute-start | bytes 688136 | tf_op jit(solution)/shard_map/ppermute | solution.py:429
  61.3 9.8 %collective-permute-start.6 = (bf16[32,3584]{1,0:T(8,128)(2,1)S(1)}, bf16[32,3584]{1,0:T(8,128)(2,1)S(1)}, u32[]{:S(2)}, u32[]{:S(2)}) collective-permute-start(bf16[32,3584]{1,0:T(8,128)(2,1)S(1)} %get-tuple-element.40), channel_id=1, source_target_pairs={{0,32},{4,12},{8,40},{12,20},{16,48},{20,28},{24,56},{28,4},{32,64... | collective-permute-start | bytes 688136 | tf_op jit(solution)/shard_map/ppermute | solution.py:72
  61.4 9.7 %collective-permute-start.7 = (bf16[32,3584]{1,0:T(8,128)(2,1)S(1)}, bf16[32,3584]{1,0:T(8,128)(2,1)S(1)}, u32[]{:S(2)}, u32[]{:S(2)}) collective-permute-start(bf16[32,3584]{1,0:T(8,128)(2,1)S(1)} %get-tuple-element.40), channel_id=1, source_target_pairs={{0,64},{4,20},{8,72},{12,28},{16,80},{20,4},{24,88},{28,12},{32,96... | collective-permute-start | bytes 688136 | tf_op jit(solution)/shard_map/ppermute | solution.py:72
  63.7 8.3 %collective-permute-start.8 = (bf16[32,3584]{1,0:T(8,128)(2,1)S(1)}, bf16[32,3584]{1,0:T(8,128)(2,1)S(1)}, u32[]{:S(2)}, u32[]{:S(2)}) collective-permute-start(bf16[32,3584]{1,0:T(8,128)(2,1)S(1)} %get-tuple-element.40), channel_id=1, source_target_pairs={{0,96},{4,28},{8,104},{12,4},{16,112},{20,12},{24,120},{28,20},{32... | collective-permute-start | bytes 688136 | tf_op jit(solution)/shard_map/ppermute | solution.py:72
  72.0 15.1 %collective-permute-start.13 = (bf16[128,3584]{1,0:T(8,128)(2,1)S(1)}, bf16[128,3584]{1,0:T(8,128)(2,1)S(1)}, u32[]{:S(2)}, u32[]{:S(2)}) collective-permute-start(bf16[128,3584]{1,0:T(8,128)(2,1)S(1)} %constant_dynamic-update-slice_fusion.rows_ref), channel_id=1, source_target_pairs={{0,16},{4,68},{8,24},{12,76},{16,0},{20,84},{24,8},{28,92},{32,48}... | collective-permute-start | bytes 2752520 | tf_op jit(solution)/shard_map/ppermute | solution.py:72
  73.0 22.3 %collective-permute-start.10 = (bf16[128,3584]{1,0:T(8,128)(2,1)S(1)}, bf16[128,3584]{1,0:T(8,128)(2,1)S(1)}, u32[]{:S(2)}, u32[]{:S(2)}) collective-permute-start(bf16[128,3584]{1,0:T(8,128)(2,1)S(1)} %constant_dynamic-update-slice_fusion.rows_ref), channel_id=1, source_target_pairs={{0,24},{4,100},{8,0},{12,108},{16,8},{20,116},{24,16},{28,124},{32... | collective-permute-start | bytes 2752520 | tf_op jit(solution)/shard_map/ppermute | solution.py:72
  74.4 22.3 %collective-permute-start.9 = (bf16[128,3584]{1,0:T(8,128)(2,1)S(1)}, bf16[128,3584]{1,0:T(8,128)(2,1)S(1)}, u32[]{:S(2)}, u32[]{:S(2)}) collective-permute-start(bf16[128,3584]{1,0:T(8,128)(2,1)S(1)} %constant_dynamic-update-slice_fusion.rows_ref), channel_id=1, source_target_pairs={{0,8},{4,36},{8,16},{12,44},{16,24},{20,52},{24,0},{28,60},{32,40}... | collective-permute-start | bytes 2752520 | tf_op jit(solution)/shard_map/ppermute | solution.py:72
  92.1 19.5 %collective-permute-start.14 = (bf16[128,3584]{1,0:T(8,128)(2,1)S(1)}, bf16[128,3584]{1,0:T(8,128)(2,1)S(1)}, u32[]{:S(2)}, u32[]{:S(2)}) collective-permute-start(bf16[128,3584]{1,0:T(8,128)(2,1)S(1)} %mlp.5), channel_id=1, source_target_pairs={{0,16},{4,68},{8,24},{12,76},{16,0},{20,84},{24,8},{28,92},{32,48}... | collective-permute-start | bytes 2752520 | tf_op jit(solution)/shard_map/ppermute | solution.py:72
  103.3 14.7 %collective-permute-start.12 = (bf16[128,3584]{1,0:T(8,128)(2,1)S(1)}, bf16[128,3584]{1,0:T(8,128)(2,1)S(1)}, u32[]{:S(2)}, u32[]{:S(2)}) collective-permute-start(bf16[128,3584]{1,0:T(8,128)(2,1)S(1)} %get-tuple-element.52), channel_id=1, source_target_pairs={{0,8},{4,36},{8,16},{12,44},{16,24},{20,52},{24,0},{28,60},{32,40}... | collective-permute-start | bytes 2752520 | tf_op jit(solution)/shard_map/ppermute | solution.py:72
  103.4 14.9 %collective-permute-start.11 = (bf16[128,3584]{1,0:T(8,128)(2,1)S(1)}, bf16[128,3584]{1,0:T(8,128)(2,1)S(1)}, u32[]{:S(2)}, u32[]{:S(2)}) collective-permute-start(bf16[128,3584]{1,0:T(8,128)(2,1)S(1)} %get-tuple-element.51), channel_id=1, source_target_pairs={{0,24},{4,100},{8,0},{12,108},{16,8},{20,116},{24,16},{28,124},{32... | collective-permute-start | bytes 2752520 | tf_op jit(solution)/shard_map/ppermute | solution.py:72
  118.3 13.8 %copy-start.1 = (bf16[3584,256]{1,0:T(8,128)(2,1)S(1)}, bf16[3584,256]{1,0:T(8,128)(2,1)}, u32[]{:S(2)}) copy-start(bf16[3584,256]{1,0:T(8,128)(2,1)} %param.27) | copy-start | bytes 5505028
  118.7 3.4 %copy-start.15 = (f32[3584]{0:T(1024)S(1)}, f32[3584]{0:T(1024)}, u32[]{:S(2)}) copy-start(f32[3584]{0:T(1024)} %param.35) | copy-start | bytes 43012
  118.8 8.4 %collective-permute-start.15 = (bf16[32,3584]{1,0:T(8,128)(2,1)S(1)}, bf16[32,3584]{1,0:T(8,128)(2,1)S(1)}, u32[]{:S(2)}, u32[]{:S(2)}) collective-permute-start(bf16[32,3584]{1,0:T(8,128)(2,1)S(1)} %get-tuple-element.55), channel_id=1, source_target_pairs={{0,96},{4,28},{8,104},{12,4},{16,112},{20,12},{24,120},{28,20},{32... | collective-permute-start | bytes 688136 | tf_op jit(solution)/shard_map/ppermute | solution.py:72
  121.2 7.6 %collective-permute-start.16 = (bf16[32,3584]{1,0:T(8,128)(2,1)S(1)}, bf16[32,3584]{1,0:T(8,128)(2,1)S(1)}, u32[]{:S(2)}, u32[]{:S(2)}) collective-permute-start(bf16[32,3584]{1,0:T(8,128)(2,1)S(1)} %get-tuple-element.54), channel_id=1, source_target_pairs={{0,64},{4,20},{8,72},{12,28},{16,80},{20,4},{24,88},{28,12},{32,96... | collective-permute-start | bytes 688136 | tf_op jit(solution)/shard_map/ppermute | solution.py:72
  121.5 9.7 %collective-permute-start.17 = (bf16[32,3584]{1,0:T(8,128)(2,1)S(1)}, bf16[32,3584]{1,0:T(8,128)(2,1)S(1)}, u32[]{:S(2)}, u32[]{:S(2)}) collective-permute-start(bf16[32,3584]{1,0:T(8,128)(2,1)S(1)} %get-tuple-element.53), channel_id=1, source_target_pairs={{0,32},{4,12},{8,40},{12,20},{16,48},{20,28},{24,56},{28,4},{32,64... | collective-permute-start | bytes 688136 | tf_op jit(solution)/shard_map/ppermute | solution.py:72
  (7 other events, 10.3 us)

commit v6 on v5

--- a/solution.py
+++ b/solution.py
@@ -76,7 +76,7 @@
     return pltpu.CompilerParams(vmem_limit_bytes=megabytes * 1024 * 1024)
 
 
-GROUP = 8
+GROUP = 4
 
 
 def pick_pages_kernel(pages_ref, keys_ref, values_ref, out_ref, keys_held, values_held, held_ref,
@@ -226,6 +226,8 @@
         load.start()
     for load in loads:
         load.start()
+    for load in (w_load, acc_load, total_load):
+        load.start()
     acc_ref[...] = jnp.zeros_like(acc_ref)
     total_ref[...] = jnp.zeros_like(total_ref)
     for load in small_loads:
@@ -233,10 +235,6 @@
     low, high = low_ref[...], high_ref[...]
     for b in range(blocks):
         loads[b].wait()
-        if b == 0:
-            w_load.start()
-            acc_load.start()
-            total_load.start()
         keys = held_ref[b, :, 0].reshape(STEP, HEAD_SIZE)
         values = held_ref[b, :, 1].reshape(STEP, HEAD_SIZE)
         code = code_ref[:, b * STEP:(b + 1) * STEP]

time: 133 us -> 133 us (level)
  no operation moved by 1% of the time
where the time goes in v6:
time: 133 us; the launch traced here: 132 us
  waiting for transfers between devices  61.4 us (46%)
  Pallas kernels  34 us (26%)
  starting transfers between devices  26.5 us (20%)
  matrix products  3.63 us (3%)
  local copies, waits for them, and re-layouts  3.48 us (3%)
  other arithmetic  2.18 us (2%)
    ppermute x12, waiting for transfers between devices, shift(): return lax.ppermute(value, REQ, chip_shift(first, k % 4))  31.6 us
    all_to_all x1, waiting for transfers between devices, local(): lax.all_to_all(packed, REQ, split_axis=0, concat_axis=0, tiled=True)  18.9 us
    pallas_call x3, Pallas kernels, mlp(): pl.pallas_call(mlp_kernel, out_shape=jax.ShapeDtypeStruct((count, width),...  16.4 us
    ppermute x12, starting transfers between devices, shift(): return lax.ppermute(value, REQ, chip_shift(first, k % 4))  14.4 us
    ppermute x3, waiting for transfers between devices, local(): lax.ppermute(parts[k], 'mlp', [(i, (i + k) % 4) for i in range(4)])  10.9 us
    all_to_all x1, starting transfers between devices, local(): lax.all_to_all(packed, REQ, split_axis=0, concat_axis=0, tiled=True)  8.33 us
    pallas_call x1, Pallas kernels, load_weights(): pl.pallas_call(load_kernel, out_shape=pltpu.VMEM((count, units, width), B...  6.6 us
    pallas_call x1, Pallas kernels, far_attention(): pl.pallas_call(far_kernel, out_shape=[pltpu.VMEM((128 // blocks, width),...  4.45 us
  transfers between devices with their start and end apart: 19, of which 13 were waited for; matrix products, arithmetic and copies ran while one was open for 5% of the time, Pallas kernels for 22%

profile of v6, /device:TPU:16, one launch (start us, length us, event | category | flops | bytes accessed | tf_op | source)
XLA Modules:
  0.0 132.3 jit_solution(740172066382420948)
XLA Ops:
  0.6 3.9 %pick_pages.1 = bf16[32,2,64,256]{3,2,1,0:T(8,128)(2,1)} custom-call(s32[32]{0:T(128)} %bitcast.28, bf16[32,64,256]{2,1,0:T(8,128)(2,1)} %keys_ref.3, bf16[32,64,256]{2,1,0:T(8,128)(2,1)} %values_ref.3), custom_call_target="tpu_custom_call" | custom-call | tf_op jit(solution)/shard_map/pick_pages/pallas_call | solution.py:108
  5.3 8.3 %all-to-all-start = ((bf16[32,2,64,256]{3,2,1,0:T(8,128)(2,1)}), bf16[32,2,64,256]{3,2,1,0:T(8,128)(2,1)}, u32[]{:S(2)}, u32[]{:S(2)}) async-start(bf16[32,2,64,256]{3,2,1,0:T(8,128)(2,1)} %pick_pages.1), calls=%async_computation | async-start | bytes 4194304 | tf_op jit(solution)/shard_map/all_to_all | solution.py:373
  15.0 2.7 %fusion.25 = f32[128,512]{1,0:T(8,128)S(1)} fusion(bf16[3584,512]{1,0:T(8,128)(2,1)} %param.26, bf16[128,3584]{1,0:T(8,128)(2,1)S(1)} %copy-done.12, f32[3584]{0:T(1024)S(1)} %copy-done.18, f32[128]{0:T(128)S(1)} %add_rsqrt_fusion), kind=kOutput, calls=%fused_computation.75 | convolution fusion | flops 471597056 | bytes 4864512 | tf_op jit(solution)/shard_map/dot_general | solution.py:381
  21.0 1.3 own_attention.1
  22.3 0.7 copy-done.7
  23.6 18.9 %all-to-all-done.pages_ref = bf16[32,2,64,256]{3,2,1,0:T(8,128)(2,1)} async-done(((bf16[32,2,64,256]{3,2,1,0:T(8,128)(2,1)}), bf16[32,2,64,256]{3,2,1,0:T(8,128)(2,1)}, u32[]{:S(2)}, u32[]{:S(2)}) %all-to-all-start) | async-done | bytes 2097184 | tf_op jit(solution)/shard_map/all_to_all | solution.py:373
  42.6 4.5 %far_attention.1 = (bf16[32,3584]{1,0:T(8,128)(2,1)S(1)}, bf16[32,3584]{1,0:T(8,128)(2,1)S(1)}, bf16[32,3584]{1,0:T(8,128)(2,1)S(1)}, bf16[32,3584]{1,0:T(8,128)(2,1)S(1)}) custom-call(s32[128,1]{1,0:T(8,128)} %copy-done.5, s32[128,1]{1,0:T(8,128)} %copy-done.6, s32[1,2048]{1,0:T(1,128)} %get-tuple-element.64.code_hbm, bf16[256,256]{1,0:T(8,128)(2,1)} %bitcast.25, ...), custom_call_target="tpu_custom_call" | custom-call | flops 536870912 | bytes 7000000 | tf_op jit(solution)/shard_map/far_attention/pallas_call | solution.py:262
  47.1 1.4 %collective-permute-start.3 = (bf16[32,3584]{1,0:T(8,128)(2,1)S(1)}, bf16[32,3584]{1,0:T(8,128)(2,1)S(1)}, u32[]{:S(2)}, u32[]{:S(2)}) collective-permute-start(bf16[32,3584]{1,0:T(8,128)(2,1)S(1)} %get-tuple-element.36), channel_id=1, source_target_pairs={{0,1},{1,2},{2,3},{3,0},{4,5},{5,6},{6,7},{7,4},{8,9},{9,10},{10,1... | collective-permute-start | bytes 688136 | tf_op jit(solution)/shard_map/ppermute | solution.py:427
  49.0 1.1 collective-permute-start.5
  50.1 9.1 %collective-permute-done.3.b_ref = bf16[32,3584]{1,0:T(8,128)(2,1)S(1)} collective-permute-done((bf16[32,3584]{1,0:T(8,128)(2,1)S(1)}, bf16[32,3584]{1,0:T(8,128)(2,1)S(1)}, u32[]{:S(2)}, u32[]{:S(2)}) %collective-permute-start.3) | collective-permute-done | bytes 229408 | tf_op jit(solution)/shard_map/ppermute | solution.py:427
  59.2 1.8 %collective-permute-done.5.d_ref = bf16[32,3584]{1,0:T(8,128)(2,1)S(1)} collective-permute-done((bf16[32,3584]{1,0:T(8,128)(2,1)S(1)}, bf16[32,3584]{1,0:T(8,128)(2,1)S(1)}, u32[]{:S(2)}, u32[]{:S(2)}) %collective-permute-start.5) | collective-permute-done | bytes 229408 | tf_op jit(solution)/shard_map/ppermute | solution.py:427
  61.5 2.3 %collective-permute-start.7 = (bf16[32,3584]{1,0:T(8,128)(2,1)S(1)}, bf16[32,3584]{1,0:T(8,128)(2,1)S(1)}, u32[]{:S(2)}, u32[]{:S(2)}) collective-permute-start(bf16[32,3584]{1,0:T(8,128)(2,1)S(1)} %get-tuple-element.40), channel_id=1, source_target_pairs={{0,64},{4,20},{8,72},{12,28},{16,80},{20,4},{24,88},{28,12},{32,96... | collective-permute-start | bytes 688136 | tf_op jit(solution)/shard_map/ppermute | solution.py:72
  63.8 1.4 %collective-permute-start.8 = (bf16[32,3584]{1,0:T(8,128)(2,1)S(1)}, bf16[32,3584]{1,0:T(8,128)(2,1)S(1)}, u32[]{:S(2)}, u32[]{:S(2)}) collective-permute-start(bf16[32,3584]{1,0:T(8,128)(2,1)S(1)} %get-tuple-element.40), channel_id=1, source_target_pairs={{0,96},{4,28},{8,104},{12,4},{16,112},{20,12},{24,120},{28,20},{32... | collective-permute-start | bytes 688136 | tf_op jit(solution)/shard_map/ppermute | solution.py:72
  65.3 5.9 %collective-permute-done.6 = bf16[32,3584]{1,0:T(8,128)(2,1)S(1)} collective-permute-done((bf16[32,3584]{1,0:T(8,128)(2,1)S(1)}, bf16[32,3584]{1,0:T(8,128)(2,1)S(1)}, u32[]{:S(2)}, u32[]{:S(2)}) %collective-permute-start.6) | collective-permute-done | bytes 229408 | tf_op jit(solution)/shard_map/ppermute | solution.py:72
  71.3 0.8 collective-permute-done.8
  72.1 1.0 collective-permute-start.13
  73.1 1.5 %collective-permute-start.10 = (bf16[128,3584]{1,0:T(8,128)(2,1)S(1)}, bf16[128,3584]{1,0:T(8,128)(2,1)S(1)}, u32[]{:S(2)}, u32[]{:S(2)}) collective-permute-start(bf16[128,3584]{1,0:T(8,128)(2,1)S(1)} %constant_dynamic-update-slice_fusion.rows_ref), channel_id=1, source_target_pairs={{0,24},{4,100},{8,0},{12,108},{16,8},{20,116},{24,16},{28,124},{32... | collective-permute-start | bytes 2752520 | tf_op jit(solution)/shard_map/ppermute | solution.py:72
  75.1 6.6 %load_weights.1.weights_ref = bf16[6,448,3584]{2,1,0:T(8,128)(2,1)S(1)} custom-call(bf16[448,3584]{1,0:T(8,128)(2,1)} %bitcast.refs_0_, bf16[448,3584]{1,0:T(8,128)(2,1)} %bitcast.1.refs_1_, bf16[448,3584]{1,0:T(8,128)(2,1)} %refs_2_, bf16[448,3584]{1,0:T(8,128)(2,1)} %collective-permute-done.refs_3_, bf16[448,3584]{1,0:T(8,128)(2,1)} %collective-permute-done.1.refs_4_, ...), custom_call_target="tpu_custom_call" | custom-call | bytes 19267584 | tf_op jit(solution)/shard_map/load_weights/pallas_call | solution.py:143
  81.7 5.5 %collective-permute-done.13.rows_ref = bf16[128,3584]{1,0:T(8,128)(2,1)S(1)} collective-permute-done((bf16[128,3584]{1,0:T(8,128)(2,1)S(1)}, bf16[128,3584]{1,0:T(8,128)(2,1)S(1)}, u32[]{:S(2)}, u32[]{:S(2)}) %collective-permute-start.13) | collective-permute-done | bytes 917536 | tf_op jit(solution)/shard_map/ppermute | solution.py:72
  87.2 5.1 %mlp.5 = bf16[128,3584]{1,0:T(8,128)(2,1)S(1)} custom-call(bf16[128,3584]{1,0:T(8,128)(2,1)S(1)} %collective-permute-done.13.rows_ref, bf16[6,448,3584]{2,1,0:T(8,128)(2,1)S(1)} %load_weights.1.weights_ref), custom_call_target="tpu_custom_call" | custom-call | flops 2466250752 | bytes 1835008 | tf_op jit(solution)/shard_map/mlp/pallas_call | solution.py:329
  92.3 1.0 collective-permute-start.14
  93.3 2.1 %collective-permute-done.10 = bf16[128,3584]{1,0:T(8,128)(2,1)S(1)} collective-permute-done((bf16[128,3584]{1,0:T(8,128)(2,1)S(1)}, bf16[128,3584]{1,0:T(8,128)(2,1)S(1)}, u32[]{:S(2)}, u32[]{:S(2)}) %collective-permute-start.10) | collective-permute-done | bytes 917536 | tf_op jit(solution)/shard_map/ppermute | solution.py:72
  95.4 1.5 %collective-permute-done.9 = bf16[128,3584]{1,0:T(8,128)(2,1)S(1)} collective-permute-done((bf16[128,3584]{1,0:T(8,128)(2,1)S(1)}, bf16[128,3584]{1,0:T(8,128)(2,1)S(1)}, u32[]{:S(2)}, u32[]{:S(2)}) %collective-permute-start.9) | collective-permute-done | bytes 917536 | tf_op jit(solution)/shard_map/ppermute | solution.py:72
  97.1 6.3 %mlp.4 = bf16[256,3584]{1,0:T(8,128)(2,1)S(1)} custom-call(bf16[256,3584]{1,0:T(8,128)(2,1)S(1)} %pad_maximum_fusion.rows_ref, bf16[6,448,3584]{2,1,0:T(8,128)(2,1)S(1)} %load_weights.1.weights_ref), custom_call_target="tpu_custom_call" | custom-call | flops 4932501504 | bytes 3670016 | tf_op jit(solution)/shard_map/mlp/pallas_call | solution.py:329
  103.5 3.2 %collective-permute-start.11 = (bf16[128,3584]{1,0:T(8,128)(2,1)S(1)}, bf16[128,3584]{1,0:T(8,128)(2,1)S(1)}, u32[]{:S(2)}, u32[]{:S(2)}) collective-permute-start(bf16[128,3584]{1,0:T(8,128)(2,1)S(1)} %get-tuple-element.51), channel_id=1, source_target_pairs={{0,24},{4,100},{8,0},{12,108},{16,8},{20,116},{24,16},{28,124},{32... | collective-permute-start | bytes 2752520 | tf_op jit(solution)/shard_map/ppermute | solution.py:72
  106.8 5.0 %mlp.3 = f32[128,3584]{1,0:T(8,128)S(1)} custom-call(bf16[128,3584]{1,0:T(8,128)(2,1)S(1)} %constant_dynamic-update-slice_fusion.rows_ref, bf16[6,448,3584]{2,1,0:T(8,128)(2,1)S(1)} %load_weights.1.weights_ref), custom_call_target="tpu_custom_call" | custom-call | flops 2466250752 | bytes 1835008 | tf_op jit(solution)/shard_map/mlp/pallas_call | solution.py:329
  111.8 6.3 %collective-permute-done.12 = bf16[128,3584]{1,0:T(8,128)(2,1)S(1)} collective-permute-done((bf16[128,3584]{1,0:T(8,128)(2,1)S(1)}, bf16[128,3584]{1,0:T(8,128)(2,1)S(1)}, u32[]{:S(2)}, u32[]{:S(2)}) %collective-permute-start.12) | collective-permute-done | bytes 917536 | tf_op jit(solution)/shard_map/ppermute | solution.py:72
  119.0 2.4 %collective-permute-start.15 = (bf16[32,3584]{1,0:T(8,128)(2,1)S(1)}, bf16[32,3584]{1,0:T(8,128)(2,1)S(1)}, u32[]{:S(2)}, u32[]{:S(2)}) collective-permute-start(bf16[32,3584]{1,0:T(8,128)(2,1)S(1)} %get-tuple-element.55), channel_id=1, source_target_pairs={{0,96},{4,28},{8,104},{12,4},{16,112},{20,12},{24,120},{28,20},{32... | collective-permute-start | bytes 688136 | tf_op jit(solution)/shard_map/ppermute | solution.py:72
  122.3 5.1 %collective-permute-done.15.b_ref = bf16[32,3584]{1,0:T(8,128)(2,1)S(1)} collective-permute-done((bf16[32,3584]{1,0:T(8,128)(2,1)S(1)}, bf16[32,3584]{1,0:T(8,128)(2,1)S(1)}, u32[]{:S(2)}, u32[]{:S(2)}) %collective-permute-start.15) | collective-permute-done | bytes 229408 | tf_op jit(solution)/shard_map/ppermute | solution.py:72
  127.4 1.6 %collective-permute-done.16.c_ref = bf16[32,3584]{1,0:T(8,128)(2,1)S(1)} collective-permute-done((bf16[32,3584]{1,0:T(8,128)(2,1)S(1)}, bf16[32,3584]{1,0:T(8,128)(2,1)S(1)}, u32[]{:S(2)}, u32[]{:S(2)}) %collective-permute-start.16) | collective-permute-done | bytes 229408 | tf_op jit(solution)/shard_map/ppermute | solution.py:72
  129.0 2.4 %collective-permute-done.17.d_ref = bf16[32,3584]{1,0:T(8,128)(2,1)S(1)} collective-permute-done((bf16[32,3584]{1,0:T(8,128)(2,1)S(1)}, bf16[32,3584]{1,0:T(8,128)(2,1)S(1)}, u32[]{:S(2)}, u32[]{:S(2)}) %collective-permute-start.17) | collective-permute-done | bytes 229408 | tf_op jit(solution)/shard_map/ppermute | solution.py:72
  131.3 0.9 leave.1
  (96 shorter events, 9.6 us)
Async XLA Ops:
  0.6 17.4 %copy-start = (bf16[3584,256]{1,0:T(8,128)(2,1)S(1)}, bf16[3584,256]{1,0:T(8,128)(2,1)}, u32[]{:S(2)}) copy-start(bf16[3584,256]{1,0:T(8,128)(2,1)} %param.27) | copy-start | bytes 5505028
  4.6 9.1 %copy-start.11 = (s32[1,128]{1,0:T(1,128)S(1)}, s32[1,128]{1,0:T(1,128)}, u32[]{:S(2)}) copy-start(s32[1,128]{1,0:T(1,128)} %seg_row_ref.1) | copy-start | bytes 1540
  4.6 9.2 %copy-start.16 = (s32[1,4]{1,0:T(1,128)S(1)}, s32[1,4]{1,0:T(1,128)}, u32[]{:S(2)}) copy-start(s32[1,4]{1,0:T(1,128)} %param.20) | copy-start | bytes 52
  4.6 9.7 %copy-start.19 = (s32[1,64]{1,0:T(1,128)S(1)}, s32[1,64]{1,0:T(1,128)}, u32[]{:S(2)}) copy-start(s32[1,64]{1,0:T(1,128)} %param.21) | copy-start | bytes 772
  4.6 10.1 %copy-start.12 = (bf16[128,3584]{1,0:T(8,128)(2,1)S(1)}, bf16[128,3584]{1,0:T(8,128)(2,1)}, u32[]{:S(2)}) copy-start(bf16[128,3584]{1,0:T(8,128)(2,1)} %param.18) | copy-start | bytes 2752516
  4.6 10.4 %copy-start.18 = (f32[3584]{0:T(1024)S(1)}, f32[3584]{0:T(1024)}, u32[]{:S(2)}) copy-start(f32[3584]{0:T(1024)} %param.25) | copy-start | bytes 43012
  4.6 42.4 %collective-permute-start = (bf16[448,3584]{1,0:T(8,128)(2,1)}, bf16[448,3584]{1,0:T(8,128)(2,1)}, u32[]{:S(2)}, u32[]{:S(2)}) collective-permute-start(bf16[448,3584]{1,0:T(8,128)(2,1)} %bitcast.refs_0_), channel_id=1, source_target_pairs={{0,4},{4,0},{1,5},{5,1},{2,6},{6,2},{3,7},{7,3},{8,12},{12,8},{9,1... | collective-permute-start | bytes 9633800 | tf_op jit(solution)/shard_map/ppermute | solution.py:374
  4.7 42.3 %collective-permute-start.1 = (bf16[448,3584]{1,0:T(8,128)(2,1)}, bf16[448,3584]{1,0:T(8,128)(2,1)}, u32[]{:S(2)}, u32[]{:S(2)}) collective-permute-start(bf16[448,3584]{1,0:T(8,128)(2,1)} %bitcast.1.refs_1_), channel_id=1, source_target_pairs={{0,4},{4,0},{1,5},{5,1},{2,6},{6,2},{3,7},{7,3},{8,12},{12,8},{9,1... | collective-permute-start | bytes 9633800 | tf_op jit(solution)/shard_map/ppermute | solution.py:374
  5.2 41.8 %collective-permute-start.2 = (bf16[448,3584]{1,0:T(8,128)(2,1)}, bf16[448,3584]{1,0:T(8,128)(2,1)}, u32[]{:S(2)}, u32[]{:S(2)}) collective-permute-start(bf16[448,3584]{1,0:T(8,128)(2,1)} %refs_2_), channel_id=1, source_target_pairs={{0,4},{4,0},{1,5},{5,1},{2,6},{6,2},{3,7},{7,3},{8,12},{12,8},{9,1... | collective-permute-start | bytes 9633800 | tf_op jit(solution)/shard_map/ppermute | solution.py:374
  5.3 37.2 %all-to-all-start = ((bf16[32,2,64,256]{3,2,1,0:T(8,128)(2,1)}), bf16[32,2,64,256]{3,2,1,0:T(8,128)(2,1)}, u32[]{:S(2)}, u32[]{:S(2)}) async-start(bf16[32,2,64,256]{3,2,1,0:T(8,128)(2,1)} %pick_pages.1), calls=%async_computation | async-start | bytes 4194304 | tf_op jit(solution)/shard_map/all_to_all | solution.py:373
  14.1 6.5 %copy-start.5 = (s32[128,1]{1,0:T(8,128)}, s32[128,1]{1,0:T(8,128)S(1)}, u32[]{:S(2)}) copy-start(s32[128,1]{1,0:T(8,128)S(1)} %copy.31.low_ref.low_hbm) | copy-start | bytes 1540
  14.3 6.4 %copy-start.6 = (s32[128,1]{1,0:T(8,128)}, s32[128,1]{1,0:T(8,128)S(1)}, u32[]{:S(2)}) copy-start(s32[128,1]{1,0:T(8,128)S(1)} %copy.32.high_ref.high_hbm) | copy-start | bytes 1540
  15.0 2.9 %copy-start.13 = (f32[3584]{0:T(1024)S(1)}, f32[3584]{0:T(1024)}, u32[]{:S(2)}) copy-start(f32[3584]{0:T(1024)} %param.30) | copy-start | bytes 43012
  15.0 3.0 %copy-start.14 = (f32[3584]{0:T(1024)S(1)}, f32[3584]{0:T(1024)}, u32[]{:S(2)}) copy-start(f32[3584]{0:T(1024)} %param.31) | copy-start | bytes 43012
  20.0 27.0 %copy-start.10 = (bf16[128,256]{1,0:T(8,128)(2,1)}, bf16[128,256]{1,0:T(8,128)(2,1)S(1)}, u32[]{:S(2)}) copy-start(bf16[128,256]{1,0:T(8,128)(2,1)S(1)} %convolution_convert_fusion.new_values_ref) | copy-start | bytes 196612
  47.1 12.1 %collective-permute-start.3 = (bf16[32,3584]{1,0:T(8,128)(2,1)S(1)}, bf16[32,3584]{1,0:T(8,128)(2,1)S(1)}, u32[]{:S(2)}, u32[]{:S(2)}) collective-permute-start(bf16[32,3584]{1,0:T(8,128)(2,1)S(1)} %get-tuple-element.36), channel_id=1, source_target_pairs={{0,1},{1,2},{2,3},{3,0},{4,5},{5,6},{6,7},{7,4},{8,9},{9,10},{10,1... | collective-permute-start | bytes 688136 | tf_op jit(solution)/shard_map/ppermute | solution.py:427
  48.4 10.8 %collective-permute-start.4 = (bf16[32,3584]{1,0:T(8,128)(2,1)S(1)}, bf16[32,3584]{1,0:T(8,128)(2,1)S(1)}, u32[]{:S(2)}, u32[]{:S(2)}) collective-permute-start(bf16[32,3584]{1,0:T(8,128)(2,1)S(1)} %get-tuple-element.37), channel_id=1, source_target_pairs={{0,2},{1,3},{2,0},{3,1},{4,6},{5,7},{6,4},{7,5},{8,10},{9,11},{10,... | collective-permute-start | bytes 688136 | tf_op jit(solution)/shard_map/ppermute | solution.py:427
  49.0 12.0 %collective-permute-start.5 = (bf16[32,3584]{1,0:T(8,128)(2,1)S(1)}, bf16[32,3584]{1,0:T(8,128)(2,1)S(1)}, u32[]{:S(2)}, u32[]{:S(2)}) collective-permute-start(bf16[32,3584]{1,0:T(8,128)(2,1)S(1)} %get-tuple-element.38), channel_id=1, source_target_pairs={{0,3},{1,0},{2,1},{3,2},{4,7},{5,4},{6,5},{7,6},{8,11},{9,8},{10,9... | collective-permute-start | bytes 688136 | tf_op jit(solution)/shard_map/ppermute | solution.py:427
  61.4 9.8 %collective-permute-start.6 = (bf16[32,3584]{1,0:T(8,128)(2,1)S(1)}, bf16[32,3584]{1,0:T(8,128)(2,1)S(1)}, u32[]{:S(2)}, u32[]{:S(2)}) collective-permute-start(bf16[32,3584]{1,0:T(8,128)(2,1)S(1)} %get-tuple-element.40), channel_id=1, source_target_pairs={{0,32},{4,12},{8,40},{12,20},{16,48},{20,28},{24,56},{28,4},{32,64... | collective-permute-start | bytes 688136 | tf_op jit(solution)/shard_map/ppermute | solution.py:72
  61.5 9.7 %collective-permute-start.7 = (bf16[32,3584]{1,0:T(8,128)(2,1)S(1)}, bf16[32,3584]{1,0:T(8,128)(2,1)S(1)}, u32[]{:S(2)}, u32[]{:S(2)}) collective-permute-start(bf16[32,3584]{1,0:T(8,128)(2,1)S(1)} %get-tuple-element.40), channel_id=1, source_target_pairs={{0,64},{4,20},{8,72},{12,28},{16,80},{20,4},{24,88},{28,12},{32,96... | collective-permute-start | bytes 688136 | tf_op jit(solution)/shard_map/ppermute | solution.py:72
  63.8 8.3 %collective-permute-start.8 = (bf16[32,3584]{1,0:T(8,128)(2,1)S(1)}, bf16[32,3584]{1,0:T(8,128)(2,1)S(1)}, u32[]{:S(2)}, u32[]{:S(2)}) collective-permute-start(bf16[32,3584]{1,0:T(8,128)(2,1)S(1)} %get-tuple-element.40), channel_id=1, source_target_pairs={{0,96},{4,28},{8,104},{12,4},{16,112},{20,12},{24,120},{28,20},{32... | collective-permute-start | bytes 688136 | tf_op jit(solution)/shard_map/ppermute | solution.py:72
  72.1 15.1 %collective-permute-start.13 = (bf16[128,3584]{1,0:T(8,128)(2,1)S(1)}, bf16[128,3584]{1,0:T(8,128)(2,1)S(1)}, u32[]{:S(2)}, u32[]{:S(2)}) collective-permute-start(bf16[128,3584]{1,0:T(8,128)(2,1)S(1)} %constant_dynamic-update-slice_fusion.rows_ref), channel_id=1, source_target_pairs={{0,16},{4,68},{8,24},{12,76},{16,0},{20,84},{24,8},{28,92},{32,48}... | collective-permute-start | bytes 2752520 | tf_op jit(solution)/shard_map/ppermute | solution.py:72
  73.1 22.3 %collective-permute-start.10 = (bf16[128,3584]{1,0:T(8,128)(2,1)S(1)}, bf16[128,3584]{1,0:T(8,128)(2,1)S(1)}, u32[]{:S(2)}, u32[]{:S(2)}) collective-permute-start(bf16[128,3584]{1,0:T(8,128)(2,1)S(1)} %constant_dynamic-update-slice_fusion.rows_ref), channel_id=1, source_target_pairs={{0,24},{4,100},{8,0},{12,108},{16,8},{20,116},{24,16},{28,124},{32... | collective-permute-start | bytes 2752520 | tf_op jit(solution)/shard_map/ppermute | solution.py:72
  74.6 22.3 %collective-permute-start.9 = (bf16[128,3584]{1,0:T(8,128)(2,1)S(1)}, bf16[128,3584]{1,0:T(8,128)(2,1)S(1)}, u32[]{:S(2)}, u32[]{:S(2)}) collective-permute-start(bf16[128,3584]{1,0:T(8,128)(2,1)S(1)} %constant_dynamic-update-slice_fusion.rows_ref), channel_id=1, source_target_pairs={{0,8},{4,36},{8,16},{12,44},{16,24},{20,52},{24,0},{28,60},{32,40}... | collective-permute-start | bytes 2752520 | tf_op jit(solution)/shard_map/ppermute | solution.py:72
  92.3 19.6 %collective-permute-start.14 = (bf16[128,3584]{1,0:T(8,128)(2,1)S(1)}, bf16[128,3584]{1,0:T(8,128)(2,1)S(1)}, u32[]{:S(2)}, u32[]{:S(2)}) collective-permute-start(bf16[128,3584]{1,0:T(8,128)(2,1)S(1)} %mlp.5), channel_id=1, source_target_pairs={{0,16},{4,68},{8,24},{12,76},{16,0},{20,84},{24,8},{28,92},{32,48}... | collective-permute-start | bytes 2752520 | tf_op jit(solution)/shard_map/ppermute | solution.py:72
  103.5 14.7 %collective-permute-start.12 = (bf16[128,3584]{1,0:T(8,128)(2,1)S(1)}, bf16[128,3584]{1,0:T(8,128)(2,1)S(1)}, u32[]{:S(2)}, u32[]{:S(2)}) collective-permute-start(bf16[128,3584]{1,0:T(8,128)(2,1)S(1)} %get-tuple-element.52), channel_id=1, source_target_pairs={{0,8},{4,36},{8,16},{12,44},{16,24},{20,52},{24,0},{28,60},{32,40}... | collective-permute-start | bytes 2752520 | tf_op jit(solution)/shard_map/ppermute | solution.py:72
  103.5 14.9 %collective-permute-start.11 = (bf16[128,3584]{1,0:T(8,128)(2,1)S(1)}, bf16[128,3584]{1,0:T(8,128)(2,1)S(1)}, u32[]{:S(2)}, u32[]{:S(2)}) collective-permute-start(bf16[128,3584]{1,0:T(8,128)(2,1)S(1)} %get-tuple-element.51), channel_id=1, source_target_pairs={{0,24},{4,100},{8,0},{12,108},{16,8},{20,116},{24,16},{28,124},{32... | collective-permute-start | bytes 2752520 | tf_op jit(solution)/shard_map/ppermute | solution.py:72
  118.5 13.8 %copy-start.1 = (bf16[3584,256]{1,0:T(8,128)(2,1)S(1)}, bf16[3584,256]{1,0:T(8,128)(2,1)}, u32[]{:S(2)}) copy-start(bf16[3584,256]{1,0:T(8,128)(2,1)} %param.27) | copy-start | bytes 5505028
  118.9 3.4 %copy-start.15 = (f32[3584]{0:T(1024)S(1)}, f32[3584]{0:T(1024)}, u32[]{:S(2)}) copy-start(f32[3584]{0:T(1024)} %param.35) | copy-start | bytes 43012
  119.0 8.4 %collective-permute-start.15 = (bf16[32,3584]{1,0:T(8,128)(2,1)S(1)}, bf16[32,3584]{1,0:T(8,128)(2,1)S(1)}, u32[]{:S(2)}, u32[]{:S(2)}) collective-permute-start(bf16[32,3584]{1,0:T(8,128)(2,1)S(1)} %get-tuple-element.55), channel_id=1, source_target_pairs={{0,96},{4,28},{8,104},{12,4},{16,112},{20,12},{24,120},{28,20},{32... | collective-permute-start | bytes 688136 | tf_op jit(solution)/shard_map/ppermute | solution.py:72
  121.3 7.6 %collective-permute-start.16 = (bf16[32,3584]{1,0:T(8,128)(2,1)S(1)}, bf16[32,3584]{1,0:T(8,128)(2,1)S(1)}, u32[]{:S(2)}, u32[]{:S(2)}) collective-permute-start(bf16[32,3584]{1,0:T(8,128)(2,1)S(1)} %get-tuple-element.54), channel_id=1, source_target_pairs={{0,64},{4,20},{8,72},{12,28},{16,80},{20,4},{24,88},{28,12},{32,96... | collective-permute-start | bytes 688136 | tf_op jit(solution)/shard_map/ppermute | solution.py:72
  121.6 9.7 %collective-permute-start.17 = (bf16[32,3584]{1,0:T(8,128)(2,1)S(1)}, bf16[32,3584]{1,0:T(8,128)(2,1)S(1)}, u32[]{:S(2)}, u32[]{:S(2)}) collective-permute-start(bf16[32,3584]{1,0:T(8,128)(2,1)S(1)} %get-tuple-element.53), channel_id=1, source_target_pairs={{0,32},{4,12},{8,40},{12,20},{16,48},{20,28},{24,56},{28,4},{32,64... | collective-permute-start | bytes 688136 | tf_op jit(solution)/shard_map/ppermute | solution.py:72
  (7 other events, 10.3 us)
